TPU v7x, 32 devices: a whole 2x2x4 slice. The times are simulated.
32 devices in a mesh: dp: 4 (over z), freq: 2 (over core), tm: 4 (over y, x).
Axes of the slice: x: 2, y: 2, z: 4, core: 2. Of those that a mesh axis runs over, the one named last changes fastest.
Arguments:
- patches: bfloat16 [1312, 32, 768], P(('freq', 'tm'), 'dp'), may hold values from -6 to 6
- col_counts: int32 [4], replicated, may hold values from 26 to 27, as said below
- norm_gain: bfloat16 [2, 768], replicated, may hold values from 0.099609375 to 1.8984375
- norm_shift: bfloat16 [2, 768], replicated, may hold values from -3 to 3
- joint_proj: bfloat16 [768, 2304], replicated, may hold values from -0.3125 to 0.3125
- proj_bias: bfloat16 [2, 768], replicated, may hold values from -3 to 3
- out_proj: bfloat16 [768, 768], replicated, may hold values from -0.875 to 0.875
- up_proj: bfloat16 [768, 3072], replicated, may hold values from -0.21875 to 0.21875
- up_bias: bfloat16 [3072], replicated, may hold values from -3 to 3
- down_proj: bfloat16 [3072, 768], replicated, may hold values from -0.109375 to 0.109375
- out_bias: bfloat16 [2, 768], replicated, may hold values from -3 to 3
- cotangent: bfloat16 [1312, 32, 768], P(('freq', 'tm'), 'dp'), may hold values from -6 to 6
Outputs:
- output: bfloat16 [1312, 32, 768], P(('freq', 'tm'), 'dp')
- grad_patches: bfloat16 [1312, 32, 768], P(('freq', 'tm'), 'dp')
- grad_norm_gain: float32 [2, 768], P(None, ('freq', 'tm'))
- grad_norm_shift: float32 [2, 768], P(None, ('freq', 'tm'))
- grad_joint_proj: float32 [768, 2304], P(('freq', 'tm'))
- grad_proj_bias: float32 [2, 768], P(None, ('freq', 'tm'))
- grad_out_proj: float32 [768, 768], P(('freq', 'tm'))
- grad_up_proj: float32 [768, 3072], P(('freq', 'tm'))
- grad_up_bias: float32 [3072], P(('freq', 'tm'))
- grad_down_proj: float32 [3072, 768], P(('freq', 'tm'))
- grad_out_bias: float32 [2, 768], P(None, ('freq', 'tm'))
Inputs may be any that keep to these rules, and one draw needn't show every extreme that they name: `col_counts`: each entry is 26 or 27, and both occur in every draw.
All inputs are finite; a program needn't handle non-finite values.
Results may differ from a plain program's by a relative error of at most 0.019.
Values may be sent and summed in bfloat16 or wider, within the bound.
No kernel may reach another device: no remote copies, remote signals or barrier semaphores. Data moves between devices by JAX's collectives and lax.ppermute only.
A program may use at most 448 MiB of HBM per device.

v0:
```python
import math

import jax
import jax.numpy as jnp
from jax import lax
from jax.sharding import PartitionSpec as P

HEADS = 12
DH = 64
FREQ_ROWS = 12


EPS = 1e-06
NEG = -1000000000.0


def live_slots(col_counts, slot_ids, freq_ids, time_ids, freq_rows, cap_cols):
    table = jnp.arange(col_counts.shape[0], dtype=jnp.int32)
    live_cols = jnp.sum(
        jnp.where(time_ids[:, None] == table[None, :], col_counts[None, :], 0), axis=1
    )
    in_grid = slot_ids < freq_rows * cap_cols
    column_live = slot_ids // freq_rows < live_cols
    extra_live = (time_ids == 0) & (freq_ids == 0)
    return jnp.where(in_grid, column_live, extra_live)


def norm_rows(values, gain, shift):
    centered = values - jnp.mean(values, axis=-1, keepdims=True)
    inverse = lax.rsqrt(jnp.mean(centered * centered, axis=-1, keepdims=True) + EPS)
    return centered * inverse * gain + shift


def gelu_exact(values):
    return jax.nn.gelu(values, approximate=False)


def matmul(left, right):
    return jnp.dot(left, right, preferred_element_type=jnp.float32)


def matmul_tn(left, right):
    return lax.dot_general(
        left, right, (((0,), (0,)), ((), ())), preferred_element_type=jnp.float32
    )


def matmul_nt(left, right):
    return lax.dot_general(
        left, right, (((1,), (1,)), ((), ())), preferred_element_type=jnp.float32
    )


def head_pair(array, offset, lane_width, head_size):
    section = lax.dynamic_slice_in_dim(array, offset, lane_width, 2)
    return section.reshape(section.shape[0], section.shape[1], 2, head_size)


def add_lanes(target, addend, offset):
    current = lax.dynamic_slice_in_dim(target, offset, addend.shape[2], 2)
    return lax.dynamic_update_slice_in_dim(target, current + addend, offset, 2)


def pair_probs(query_pair, key_pair, log_pair, mask, scale):
    scores = (
        jnp.einsum("qchd,kchd->chqk", query_pair, key_pair, preferred_element_type=jnp.float32)
        * scale
        + mask
    )
    return jnp.exp(scores - jnp.transpose(log_pair, (1, 2, 0))[..., None])


def per_device(
    patches,
    col_counts,
    norm_gain,
    norm_shift,
    joint_proj,
    proj_bias,
    out_proj,
    up_proj,
    up_bias,
    down_proj,
    out_bias,
    cotangent,
):
    slots, clips, width = patches.shape
    row_count = slots * clips
    lane_width = 2 * DH
    pair_count = HEADS // 2
    scale = 1.0 / math.sqrt(DH)
    freq_size = lax.axis_size("freq")
    time_size = lax.axis_size("tm")
    freq_rows = FREQ_ROWS // freq_size
    cap_cols = (slots - 2) // freq_rows
    key_count = slots * freq_size * time_size
    slot_ids = jnp.arange(slots, dtype=jnp.int32)
    own_live = live_slots(
        col_counts,
        slot_ids,
        jnp.full((slots,), lax.axis_index("freq"), jnp.int32),
        jnp.full((slots,), lax.axis_index("tm"), jnp.int32),
        freq_rows,
        cap_cols,
    )
    key_ids = jnp.arange(key_count, dtype=jnp.int32)
    key_group = key_ids // slots
    key_live = live_slots(
        col_counts,
        key_ids % slots,
        key_group // time_size,
        key_group % time_size,
        freq_rows,
        cap_cols,
    )
    key_mask = jnp.where(key_live, 0.0, NEG).astype(jnp.float32)
    row_live = (
        jnp.broadcast_to(own_live[:, None], (slots, clips))
        .reshape(row_count, 1)
        .astype(jnp.float32)
    )
    gain_full = norm_gain.astype(jnp.float32)
    shift_full = norm_shift.astype(jnp.float32)
    bias_full = proj_bias.astype(jnp.float32)
    outb_full = out_bias.astype(jnp.float32)
    upb_full = up_bias.astype(jnp.float32)
    inputs = patches.reshape(row_count, width).astype(jnp.float32)
    normed1, ln1_back = jax.vjp(norm_rows, inputs, gain_full[0], shift_full[0])
    normed1_low = normed1.astype(jnp.bfloat16)
    joint = matmul(normed1_low, joint_proj)
    query_low = (joint[:, :width] + bias_full[0]).astype(jnp.bfloat16)
    keys_low = joint[:, width : 2 * width].astype(jnp.bfloat16)
    memory_low = (joint[:, 2 * width :] + bias_full[1]).astype(jnp.bfloat16)
    query3 = query_low.reshape(slots, clips, width)
    key_value = jnp.concatenate([keys_low, memory_low], axis=1).reshape(slots, clips, 2 * width)
    all_memory = lax.all_gather(key_value, ("freq", "tm"), axis=0, tiled=True)

    def forward_pair(number, state):
        mixed_acc, log_acc = state
        offset = number * lane_width
        query_pair = head_pair(query3, offset, lane_width, DH)
        key_pair = head_pair(all_memory, offset, lane_width, DH)
        value_pair = head_pair(all_memory, width + offset, lane_width, DH)
        scores = (
            jnp.einsum("qchd,kchd->chqk", query_pair, key_pair, preferred_element_type=jnp.float32)
            * scale
            + key_mask
        )
        highest = jnp.max(scores, axis=-1, keepdims=True)
        exponent = jnp.exp(scores - highest)
        summed = jnp.sum(exponent, axis=-1, keepdims=True)
        attention = (exponent / summed).astype(jnp.bfloat16)
        mixed = jnp.einsum(
            "chqk,kchd->qchd", attention, value_pair, preferred_element_type=jnp.float32
        )
        log_pair = jnp.transpose((highest + jnp.log(summed))[..., 0], (2, 0, 1))
        mixed_acc = lax.dynamic_update_slice_in_dim(
            mixed_acc, mixed.reshape(slots, clips, lane_width), offset, 2
        )
        log_acc = lax.dynamic_update_slice_in_dim(log_acc, log_pair, 2 * number, 2)
        return (mixed_acc, log_acc)

    mixed_full, log_rows = lax.fori_loop(
        0,
        pair_count,
        forward_pair,
        (
            jnp.zeros((slots, clips, width), jnp.float32),
            jnp.zeros((slots, clips, HEADS), jnp.float32),
        ),
    )
    mixed_low = mixed_full.reshape(row_count, width).astype(jnp.bfloat16)
    middle = inputs + matmul(mixed_low, out_proj) + outb_full[0]
    normed2, ln2_back = jax.vjp(norm_rows, middle, gain_full[1], shift_full[1])
    normed2_low = normed2.astype(jnp.bfloat16)
    pre_act = matmul(normed2_low, up_proj) + upb_full
    activated, gelu_back = jax.vjp(gelu_exact, pre_act)
    hidden_low = activated.astype(jnp.bfloat16)
    final = middle + matmul(hidden_low, down_proj) + outb_full[1]
    output = (final * row_live).astype(jnp.bfloat16).reshape(slots, clips, width)
    grad_out_rows = cotangent.reshape(row_count, width).astype(jnp.float32) * row_live
    grad_out_low = grad_out_rows.astype(jnp.bfloat16)
    grad_down_part = matmul_tn(hidden_low, grad_out_low)
    grad_outb_mlp = jnp.sum(grad_out_rows, axis=0)
    grad_hidden = matmul_nt(grad_out_low, down_proj)
    grad_pre_low = gelu_back(grad_hidden)[0].astype(jnp.bfloat16)
    grad_up_part = matmul_tn(normed2_low, grad_pre_low)
    grad_upb_part = jnp.sum(grad_pre_low.astype(jnp.float32), axis=0)
    grad_normed2 = matmul_nt(grad_pre_low, up_proj)
    grad_mid_part, grad_gain_mlp, grad_shift_mlp = ln2_back(grad_normed2)
    grad_middle = grad_out_rows + grad_mid_part
    grad_branch = grad_middle.astype(jnp.bfloat16)
    grad_outp_part = matmul_tn(mixed_low, grad_branch)
    grad_outb_attn = jnp.sum(grad_branch.astype(jnp.float32), axis=0)
    grad_mixed_low = matmul_nt(grad_branch, out_proj).astype(jnp.bfloat16)
    grad_mixed3 = grad_mixed_low.reshape(slots, clips, width)

    def query_side(number):
        offset = number * lane_width
        query_pair = head_pair(query3, offset, lane_width, DH)
        grad_pair = head_pair(grad_mixed3, offset, lane_width, DH)
        key_pair = head_pair(all_memory, offset, lane_width, DH)
        value_pair = head_pair(all_memory, width + offset, lane_width, DH)
        log_pair = lax.dynamic_slice_in_dim(log_rows, 2 * number, 2, 2)
        probability = pair_probs(query_pair, key_pair, log_pair, key_mask, scale)
        grad_probs = jnp.einsum(
            "qchd,kchd->chqk", grad_pair, value_pair, preferred_element_type=jnp.float32
        )
        delta = jnp.sum(probability * grad_probs, axis=-1, keepdims=True)
        grad_scores = (probability * (grad_probs - delta)).astype(jnp.bfloat16)
        grad_query = (
            jnp.einsum("chqk,kchd->qchd", grad_scores, key_pair, preferred_element_type=jnp.float32)
            * scale
        )
        return (
            offset,
            query_pair,
            grad_pair,
            probability,
            grad_scores,
            delta,
            grad_query.reshape(slots, clips, lane_width),
        )

    zero_query = jnp.zeros((slots, clips, width), jnp.float32)

    def backward_pair(number, state):
        grad_query_acc, grad_memory = state
        side = query_side(number)
        offset = side[0]
        grad_keys = (
            jnp.einsum("chqk,qchd->kchd", side[4], side[1], preferred_element_type=jnp.float32)
            * scale
        )
        grad_values = jnp.einsum(
            "chqk,qchd->kchd",
            side[3].astype(jnp.bfloat16),
            side[2],
            preferred_element_type=jnp.float32,
        )
        grad_memory = add_lanes(
            grad_memory, grad_keys.reshape(key_count, clips, lane_width), offset
        )
        grad_memory = add_lanes(
            grad_memory, grad_values.reshape(key_count, clips, lane_width), width + offset
        )
        return (add_lanes(grad_query_acc, side[6], offset), grad_memory)

    grad_query_full, grad_memory_all = lax.fori_loop(
        0,
        pair_count,
        backward_pair,
        (zero_query, jnp.zeros((key_count, clips, 2 * width), jnp.float32)),
    )
    grad_memory_own = lax.psum_scatter(
        grad_memory_all, ("freq", "tm"), scatter_dimension=0, tiled=True
    )
    grad_query_low = grad_query_full.reshape(row_count, width).astype(jnp.bfloat16)
    grad_memory_low = grad_memory_own.reshape(row_count, 2 * width).astype(jnp.bfloat16)
    grad_joint = jnp.concatenate([grad_query_low, grad_memory_low], axis=1)
    grad_joint_part = matmul_tn(normed1_low, grad_joint)
    grad_bias_cols = jnp.stack(
        [
            jnp.sum(grad_query_low.astype(jnp.float32), axis=0),
            jnp.sum(grad_memory_low[:, width:].astype(jnp.float32), axis=0),
        ],
        axis=1,
    )
    grad_normed1 = matmul_nt(grad_joint, joint_proj)
    grad_in_part, grad_gain_attn, grad_shift_attn = ln1_back(grad_normed1)
    grad_patches = (grad_middle + grad_in_part).astype(jnp.bfloat16).reshape(slots, clips, width)
    shares = (
        lax.psum_scatter(
            grad_joint_part.astype(jnp.bfloat16), ("freq", "tm"), scatter_dimension=0, tiled=True
        ).astype(jnp.float32),
        lax.psum_scatter(
            grad_bias_cols.astype(jnp.bfloat16), ("freq", "tm"), scatter_dimension=0, tiled=True
        ).astype(jnp.float32),
        lax.psum_scatter(
            grad_outp_part.astype(jnp.bfloat16), ("freq", "tm"), scatter_dimension=0, tiled=True
        ).astype(jnp.float32),
        lax.psum_scatter(
            grad_outb_attn.astype(jnp.bfloat16), ("freq", "tm"), scatter_dimension=0, tiled=True
        ).astype(jnp.float32),
        lax.psum_scatter(
            grad_gain_attn.astype(jnp.bfloat16), ("freq", "tm"), scatter_dimension=0, tiled=True
        ).astype(jnp.float32),
        lax.psum_scatter(
            grad_shift_attn.astype(jnp.bfloat16), ("freq", "tm"), scatter_dimension=0, tiled=True
        ).astype(jnp.float32),
        lax.psum_scatter(
            grad_up_part.astype(jnp.bfloat16), ("freq", "tm"), scatter_dimension=0, tiled=True
        ).astype(jnp.float32),
        lax.psum_scatter(
            grad_upb_part.astype(jnp.bfloat16), ("freq", "tm"), scatter_dimension=0, tiled=True
        ).astype(jnp.float32),
        lax.psum_scatter(
            grad_down_part.astype(jnp.bfloat16), ("freq", "tm"), scatter_dimension=0, tiled=True
        ).astype(jnp.float32),
        lax.psum_scatter(
            grad_outb_mlp.astype(jnp.bfloat16), ("freq", "tm"), scatter_dimension=0, tiled=True
        ).astype(jnp.float32),
        lax.psum_scatter(
            grad_gain_mlp.astype(jnp.bfloat16), ("freq", "tm"), scatter_dimension=0, tiled=True
        ).astype(jnp.float32),
        lax.psum_scatter(
            grad_shift_mlp.astype(jnp.bfloat16), ("freq", "tm"), scatter_dimension=0, tiled=True
        ).astype(jnp.float32),
    )
    summed_all = (
        lax.psum(shares[0].astype(jnp.bfloat16), "dp").astype(jnp.float32),
        lax.psum(shares[1].astype(jnp.bfloat16), "dp").astype(jnp.float32),
        lax.psum(shares[2].astype(jnp.bfloat16), "dp").astype(jnp.float32),
        lax.psum(shares[3].astype(jnp.bfloat16), "dp").astype(jnp.float32),
        lax.psum(shares[4].astype(jnp.bfloat16), "dp").astype(jnp.float32),
        lax.psum(shares[5].astype(jnp.bfloat16), "dp").astype(jnp.float32),
        lax.psum(shares[6].astype(jnp.bfloat16), "dp").astype(jnp.float32),
        lax.psum(shares[7].astype(jnp.bfloat16), "dp").astype(jnp.float32),
        lax.psum(shares[8].astype(jnp.bfloat16), "dp").astype(jnp.float32),
        lax.psum(shares[9].astype(jnp.bfloat16), "dp").astype(jnp.float32),
        lax.psum(shares[10].astype(jnp.bfloat16), "dp").astype(jnp.float32),
        lax.psum(shares[11].astype(jnp.bfloat16), "dp").astype(jnp.float32),
    )
    attn_summed = summed_all[:6]
    mlp_summed = summed_all[6:]
    grad_norm_gain = jnp.stack([attn_summed[4], mlp_summed[4]])
    grad_norm_shift = jnp.stack([attn_summed[5], mlp_summed[5]])
    grad_out_bias = jnp.stack([attn_summed[3], mlp_summed[3]])
    grad_proj_bias = jnp.transpose(attn_summed[1])
    return (
        output,
        grad_patches,
        grad_norm_gain,
        grad_norm_shift,
        attn_summed[0],
        grad_proj_bias,
        attn_summed[2],
        mlp_summed[0],
        mlp_summed[1],
        mlp_summed[2],
        grad_out_bias,
    )


def solution(mesh):
    return jax.shard_map(
        per_device,
        mesh=mesh,
        in_specs=(
            P(("freq", "tm"), "dp", None),
            P(),
            P(),
            P(),
            P(),
            P(),
            P(),
            P(),
            P(),
            P(),
            P(),
            P(("freq", "tm"), "dp", None),
        ),
        out_specs=(
            P(("freq", "tm"), "dp", None),
            P(("freq", "tm"), "dp", None),
            P(None, ("freq", "tm")),
            P(None, ("freq", "tm")),
            P(("freq", "tm"), None),
            P(None, ("freq", "tm")),
            P(("freq", "tm"), None),
            P(("freq", "tm"), None),
            P(("freq", "tm")),
            P(("freq", "tm"), None),
            P(None, ("freq", "tm")),
        ),
        check_vma=False,
    )
```

profile of v0, /device:TPU:0, one launch (start us, length us, event | category | flops | bytes accessed | tf_op | source)
XLA Modules:
  0.0 1730.8 jit_solution(16705769092683540999)
XLA Ops:
  44.6 144.3 %all-gather.2.cloned.1.call-done = bf16[1312,8,1536]{2,1,0:T(8,128)(2,1)} async-done(((bf16[164,8,1536]{2,1,0:T(8,128)(2,1)}), bf16[1312,8,1536]{2,1,0:T(8,128)(2,1)}) %all-gather.2.cloned.1.call-update) | async-done | bytes 32243728 | tf_op jit(solution)/shard_map/all_gather | solution.py:136
  188.8 42.4 %copy.42 = bf16[1312,8,1536]{0,2,1:T(8,128)(2,1)} copy(bf16[1312,8,1536]{2,1,0:T(8,128)(2,1)} %all-gather.2.cloned.1.call-done) | data formatting | bytes 64487424 | tf_op jit(solution)/shard_map/while | solution.py:163
  231.9 122.6 %while.34 = (s32[]{:T(128)}, bf16[164,8,768]{2,1,0:T(8,128)(2,1)}, f32[164,8,12]{0,2,1:T(8,128)}, bf16[1312,8,1536]{0,2,1:T(8,128)(2,1)}, bf16[164,8,768]{0,2,1:...) while((s32[]{:T(128)}, bf16[164,8,768]{2,1,0:T(8,128)(2,1)}, ...), condition=%wide.region_6.7_spmd, body=%wide.region_3.6_spmd.sunk | while | flops 922637760 | bytes 60295916 | solution.py:163
  360.4 45.5 %multiply_convert_fusion.1 = (bf16[1312,3072]{1,0:T(8,128)(2,1)}, f32[1312,3072]{1,0:T(8,128)}, f32[1312,3072]{1,0:T(8,128)}) fusion(f32[3072]{0:T(1024)S(1)} %copy-done.41, bf16[768,3072]{1,0:T(8,128)(2,1)S(1)} %bitcast.204, f32[1312,768]{1,0:T(8,128)S(1)} %get-tuple-element.504, f32[768]{0:T(1024)S(1)} %copy-done.46, f32[768]{0:T(1024)S(1)} %copy-done.39, ...), kind=kOutput, calls=%fused_computation.34 | convolution fusion | flops 6461841408 | bytes 49082624 | tf_op jit(solution)/shard_map/dot_general | solution.py:39
  405.9 21.6 %fusion.75 = (bf16[3072]{0:T(1024)(128)(2,1)}, bf16[1312,3072]{1,0:T(8,128)(2,1)}) fusion(f32[1312,3072]{1,0:T(8,128)} %get-tuple-element.492, bf16[3072,768]{1,0:T(8,128)(2,1)} %param.25, bf16[164,8,768]{2,1,0:T(8,128)(2,1)} %param.27, f32[1312]{0:T(1024)S(1)} %copy-done.22, f32[1312,3072]{1,0:T(8,128)} %get-tuple-element.505, f32[3072]{0:T(1024)} %convert_element_type.229), kind=kOutput, calls=%fused_computation.178 | convolution fusion | flops 6258299904 | bytes 47062144 | tf_op jit(solution)/shard_map/dot_general | solution.py:49
  427.5 14.1 multiply_reduce_fusion.1
  450.7 21.7 %broadcast_in_dim.96 = f32[1312,8,1536]{0,2,1:T(8,128)} broadcast(f32[]{:T(128)} %constant.301.clone.1), dimensions={} | broadcast | bytes 64487428 | tf_op jit(solution)/shard_map/broadcast_in_dim | solution.py:253
  472.4 478.9 %while.35 = (s32[]{:T(128)}, f32[164,8,768]{2,1,0:T(8,128)}, f32[1312,8,1536]{0,2,1:T(8,128)}, bf16[1312,8,1536]{0,2,1:T(8,128)(2,1)}, bf16[164,8,768]{0,2,1:T(8...) while((s32[]{:T(128)}, f32[164,8,768]{2,1,0:T(8,128)}, ...), condition=%wide.region_14.15_spmd, body=%wide.region_12.14_spmd.sunk | while | flops 2238668288 | bytes 267073456 | solution.py:249
  495.3 11.0 multiply_reduce_fusion.5
  575.1 11.0 multiply_reduce_fusion.5
  894.0 11.0 multiply_reduce_fusion.5
  951.3 67.7 %copy.49 = f32[1312,8,1536]{2,1,0:T(8,128)} copy(f32[1312,8,1536]{0,2,1:T(8,128)} %get-tuple-element.368) | data formatting | bytes 128974848 | tf_op jit(solution)/shard_map/while | solution.py:249
  1024.4 12.6 convolution_convert_fusion.2
  1037.8 15.0 convolution_convert_fusion.1
  1057.2 334.1 %reduce-scatter.9.cloned.1.call-done = f32[164,8,1536]{2,1,0:T(8,128)} async-done(((f32[1312,8,1536]{2,1,0:T(8,128)}), f32[164,8,1536]{2,1,0:T(8,128)}) %reduce-scatter.9.cloned.1.call-update) | async-done | bytes 8060944 | tf_op jit(solution)/shard_map/reduce_scatter | solution.py:255
  1414.0 11.5 fusion.40
  1428.0 11.0 fusion.69
  1445.5 27.6 %all-reduce.7 = (bf16[768]{0:T(1024)(128)(2,1)}, bf16[768]{0:T(1024)(128)(2,1)}, bf16[768]{0:T(1024)(128)(2,1)}, bf16[768]{0:T(1024)(128)(2,1)}, bf16[3072]{0:T(...) all-reduce(bf16[768]{0:T(1024)(128)(2,1)} %get-tuple-element.425, ...), channel_id=4, replica_groups=mesh['dp'=4,'freq'=2,'tm'=4] {'freq','tm'}, use_global_device_ids=true, to_apply=%region_22.23.clone | all-reduce | flops 7680 | bytes 30720
  1474.4 15.6 reduce-scatter.17.cloned.1.call-done
  1490.0 57.2 %reduce-scatter.15.cloned.1.call-done = bf16[96,3072]{1,0:T(8,128)(2,1)} async-done(((bf16[768,3072]{1,0:T(8,128)(2,1)}), bf16[96,3072]{1,0:T(8,128)(2,1)}) %reduce-scatter.15.cloned.1.call-update) | async-done | bytes 589840 | tf_op jit(solution)/shard_map/reduce_scatter | solution.py:291
  1547.2 51.9 %reduce-scatter.11.cloned.1.call-done = bf16[96,2304]{1,0:T(8,128)(2,1)} async-done(((bf16[768,2304]{1,0:T(8,128)(2,1)}), bf16[96,2304]{1,0:T(8,128)(2,1)}) %reduce-scatter.11.cloned.1.call-update) | async-done | bytes 442384 | tf_op jit(solution)/shard_map/reduce_scatter | solution.py:273
  1614.1 22.4 %reduce-scatter.19.cloned.1.call-done = bf16[96,2]{1,0:T(8,128)(2,1)} async-done(((bf16[768,2]{1,0:T(8,128)(2,1)}), bf16[96,2]{1,0:T(8,128)(2,1)}) %reduce-scatter.19.cloned.1.call-update) | async-done | bytes 400
  1637.3 12.7 all-reduce.8
  1654.9 60.9 %all-reduce.12.cloned.1.call-done = (bf16[96,2304]{1,0:T(8,128)(2,1)}, bf16[96,768]{1,0:T(8,128)(2,1)}, bf16[96,3072]{1,0:T(8,128)(2,1)}, bf16[384,768]{1,0:T(8,128)(2,1)}) async-done(((bf16[96,2304]{1,0:T(8,128)(2,1)}, bf16[96,768]{1,0:T(8,128)(2,1)}, bf16[96,3072]{1,0:T(8,128)(2,1)}, bf16[384,768]{1,0:T(8,128)(2,1)}), (bf16[96,2304]{1,0:T(8,128)(2,1)}, bf16[96,768]{1,0:T(8,128)(2,1)}, ...) | async-done | bytes 1769488 | tf_op jit(solution)/shard_map/psum | solution.py:311
  (460 shorter events, 690.8 us)
Async XLA Ops:
  7.2 181.6 %all-gather.2.cloned.1.call-start = ((), (), s32[]{:S(2)}) async-start(), calls=%async_computation.6 | async-start | bytes 36274176 | tf_op jit(solution)/shard_map/all_gather | solution.py:136
  10.9 14.7 copy-start.20
  30.7 1360.5 %reduce-scatter.9.cloned.1.call-start = ((), (), s32[]{:S(2)}) async-start(), calls=%async_computation.7 | async-start | bytes 72548352 | tf_op jit(solution)/shard_map/reduce_scatter | solution.py:255
  359.1 46.8 %copy-start.9 = (f32[1312,768]{1,0:T(8,128)}, f32[1312,768]{1,0:T(8,128)S(1)}, u32[]{:S(2)}) copy-start(f32[1312,768]{1,0:T(8,128)S(1)} %get-tuple-element.504) | copy-start | bytes 12091396
  359.2 82.5 %copy-start.31 = (f32[1312]{0:T(1024)}, f32[1312]{0:T(1024)S(1)}, u32[]{:S(2)}) copy-start(f32[1312]{0:T(1024)S(1)} %broadcast_multiply_fusion.1) | copy-start | bytes 15748
  359.8 46.1 %copy-start.35 = (f32[1312]{0:T(1024)}, f32[1312]{0:T(1024)S(1)}, u32[]{:S(2)}) copy-start(f32[1312]{0:T(1024)S(1)} %fusion.60) | copy-start | bytes 15748
  360.4 45.5 %copy-start.22 = (f32[1312]{0:T(1024)S(1)}, f32[1312]{0:T(1024)}, u32[]{:S(2)}) copy-start(f32[1312]{0:T(1024)} %convert_element_type.232) | copy-start | bytes 15748
  427.5 14.2 copy-start.10
  427.5 14.2 copy-start.36
  427.5 14.2 copy-start.40
  450.7 21.7 %copy-start.15 = (f32[1312]{0:T(1024)S(1)}, f32[1312]{0:T(1024)}, u32[]{:S(2)}) copy-start(f32[1312]{0:T(1024)} %get-tuple-element.731) | copy-start | bytes 15748
  487.6 18.7 %copy-start.2 = (bf16[1312,8,128]{0,2,1:T(8,128)(2,1)}, bf16[1312,8,128]{0,2,1:T(8,128)(2,1)S(1)}, u32[]{:S(2)}) copy-start(bf16[1312,8,128]{0,2,1:T(8,128)(2,1)S(1)} %get-tuple-element.610) | copy-start | bytes 8060932 | tf_op jit(solution)/shard_map/while
  567.4 18.7 %copy-start.2 = (bf16[1312,8,128]{0,2,1:T(8,128)(2,1)}, bf16[1312,8,128]{0,2,1:T(8,128)(2,1)S(1)}, u32[]{:S(2)}) copy-start(bf16[1312,8,128]{0,2,1:T(8,128)(2,1)S(1)} %get-tuple-element.610) | copy-start | bytes 8060932 | tf_op jit(solution)/shard_map/while
  647.2 18.7 %copy-start.2 = (bf16[1312,8,128]{0,2,1:T(8,128)(2,1)}, bf16[1312,8,128]{0,2,1:T(8,128)(2,1)S(1)}, u32[]{:S(2)}) copy-start(bf16[1312,8,128]{0,2,1:T(8,128)(2,1)S(1)} %get-tuple-element.610) | copy-start | bytes 8060932 | tf_op jit(solution)/shard_map/while
  726.9 18.7 %copy-start.2 = (bf16[1312,8,128]{0,2,1:T(8,128)(2,1)}, bf16[1312,8,128]{0,2,1:T(8,128)(2,1)S(1)}, u32[]{:S(2)}) copy-start(bf16[1312,8,128]{0,2,1:T(8,128)(2,1)S(1)} %get-tuple-element.610) | copy-start | bytes 8060932 | tf_op jit(solution)/shard_map/while
  806.6 18.7 %copy-start.2 = (bf16[1312,8,128]{0,2,1:T(8,128)(2,1)}, bf16[1312,8,128]{0,2,1:T(8,128)(2,1)S(1)}, u32[]{:S(2)}) copy-start(bf16[1312,8,128]{0,2,1:T(8,128)(2,1)S(1)} %get-tuple-element.610) | copy-start | bytes 8060932 | tf_op jit(solution)/shard_map/while
  886.3 18.7 %copy-start.2 = (bf16[1312,8,128]{0,2,1:T(8,128)(2,1)}, bf16[1312,8,128]{0,2,1:T(8,128)(2,1)S(1)}, u32[]{:S(2)}) copy-start(bf16[1312,8,128]{0,2,1:T(8,128)(2,1)S(1)} %get-tuple-element.610) | copy-start | bytes 8060932 | tf_op jit(solution)/shard_map/while
  1019.1 455.3 %reduce-scatter.13.cloned.1.call-start = ((), (), s32[]{:S(2)}) async-start(), calls=%async_computation.9 | async-start | bytes 1327104 | tf_op jit(solution)/shard_map/reduce_scatter | solution.py:279
  1024.4 465.6 %reduce-scatter.17.cloned.1.call-start = ((), (), s32[]{:S(2)}) async-start(), calls=%async_computation.11 | async-start | bytes 5308416 | tf_op jit(solution)/shard_map/reduce_scatter | solution.py:297
  1037.1 510.1 %reduce-scatter.15.cloned.1.call-start = ((), (), s32[]{:S(2)}) async-start(), calls=%async_computation.10 | async-start | bytes 5308416 | tf_op jit(solution)/shard_map/reduce_scatter | solution.py:291
  1052.8 546.3 %reduce-scatter.11.cloned.1.call-start = ((), (), s32[]{:S(2)}) async-start(), calls=%async_computation.8 | async-start | bytes 3981312 | tf_op jit(solution)/shard_map/reduce_scatter | solution.py:273
  1057.2 340.0 %copy-start.21 = (f32[1312]{0:T(1024)S(1)}, f32[1312]{0:T(1024)}, u32[]{:S(2)}) copy-start(f32[1312]{0:T(1024)} %copy-done.20) | copy-start | bytes 15748
  1406.1 230.3 %reduce-scatter.19.cloned.1.call-start = ((), (), s32[]{:S(2)}) async-start(), calls=%async_computation.12 | async-start | bytes 221184
  1439.7 276.1 %all-reduce.12.cloned.1.call-start = ((), (), s32[]{:S(2)}) async-start(), calls=%async_computation.13 | async-start | bytes 3538944 | tf_op jit(solution)/shard_map/psum | solution.py:311
  (89 other events, 544.4 us)
Sparse Core Ops, SparseCore 0:
  30.8 157.9 all-gather.1
  1019.2 372.0 reduce-scatter.8
  1395.1 36.7 reduce-scatter.12
  1435.6 54.3 reduce-scatter.16
  1493.3 53.8 reduce-scatter.14
  1550.9 48.0 reduce-scatter.10
  1602.9 33.4 reduce-scatter.18
  1639.1 76.5 all-reduce.11
where the time goes:
time: 1740 us; the launch traced here: 1730 us
  waiting for transfers between devices  686 us (39%)
  matrix products  397 us (23%)
  local copies, waits for them, and re-layouts  349 us (20%)
  other arithmetic  239 us (14%)
  blocking collectives  40.3 us (2%)
    reduce_scatter x1, waiting for transfers between devices, per_device(): lax.psum_scatter(grad_memory_all, ('freq', 'tm'), scatter_dimension=0, ti...  334 us
    all_gather x1, waiting for transfers between devices, per_device(): all_memory = lax.all_gather(key_value, ('freq', 'tm'), axis=0, tiled=True)  144 us
    dynamic_update_slice x12, other arithmetic, add_lanes(): return lax.dynamic_update_slice_in_dim(target, current + addend, offset, 2)  78.9 us
    dynamic_slice x36, local copies, waits for them, and re-layouts, head_pair(): section = lax.dynamic_slice_in_dim(array, offset, lane_width, 2)  78.8 us
    dot_general x4, matrix products, matmul(): return jnp.dot(left, right, preferred_element_type=jnp.float32)  68.4 us
    while x1, local copies, waits for them, and re-layouts, per_device(): lax.fori_loop(0, pair_count, backward_pair, (zero_query, jnp.zeros((key_c...  67.7 us
    dot_general x6, matrix products, pair_probs(): jnp.einsum('qchd,kchd->chqk', query_pair, key_pair, preferred_element_typ...  66.2 us
    convert_element_type x6, other arithmetic, query_side(): grad_scores = (probability * (grad_probs - delta)).astype(jnp.bfloat16)  62.9 us
  transfers between devices with their start and end apart: 8, of which 7 were waited for; matrix products, arithmetic and copies ran while one was open for 7% of the time, Pallas kernels for 0%

commit v1 on v0

--- a/solution.py
+++ b/solution.py
@@ -3,6 +3,8 @@
 import jax
 import jax.numpy as jnp
 from jax import lax
+from jax.experimental import pallas as pl
+from jax.experimental.pallas import tpu as pltpu
 from jax.sharding import PartitionSpec as P
 
 HEADS = 12
@@ -70,7 +72,7 @@
     return jnp.exp(scores - jnp.transpose(log_pair, (1, 2, 0))[..., None])
 
 
-def per_device(
+def per_device_gathered(
     patches,
     col_counts,
     norm_gain,
@@ -342,9 +344,293 @@
     )
 
 
+LOG2E = 1.4426950408889634
+LANES = 128
+F32 = jnp.float32
+BF16 = jnp.bfloat16
+
+
+def attention_forward_kernel(q_ref, k_ref, v_ref, live_ref, o_ref, rn_ref, p_ref, qs, vt, ot, sa, sb):
+    tokens = q_ref.shape[0]
+    lane = lax.broadcasted_iota(jnp.int32, (tokens, LANES), 1)
+    query = q_ref[...].astype(F32) * (1.0 / math.sqrt(DH))
+    qs[0:tokens, :] = jnp.where(lane < DH, query, 0.0).astype(BF16)
+    qs[tokens : 2 * tokens, :] = jnp.where(lane < DH, 0.0, query).astype(BF16)
+    live = live_ref[0:1, :]
+    vt[0:LANES, :] = (jnp.transpose(v_ref[...].astype(F32)) * live).astype(BF16)
+    vt[LANES : LANES + 16, :] = jnp.broadcast_to(live, (16, tokens)).astype(BF16)
+
+    def scores(head):
+        return matmul_nt(k_ref[...], qs[head * tokens : (head + 1) * tokens, :])
+
+    def finish(head, score):
+        highest = jnp.max(score, axis=0, keepdims=True)
+        weight = jnp.exp2(score * LOG2E - highest * LOG2E).astype(BF16)
+        p_ref[0, :, head * tokens : (head + 1) * tokens] = weight
+        ot[:, head * tokens : (head + 1) * tokens] = matmul(vt[...], weight)
+
+    sa[...] = scores(0)
+    sb[...] = scores(1)
+    finish(0, sa[...])
+    finish(1, sb[...])
+    row = lax.broadcasted_iota(jnp.int32, (LANES, tokens), 0)
+    inverse = jnp.where(
+        row < DH,
+        jnp.broadcast_to(1.0 / ot[LANES : LANES + 1, 0:tokens], (LANES, tokens)),
+        jnp.broadcast_to(1.0 / ot[LANES : LANES + 1, tokens : 2 * tokens], (LANES, tokens)),
+    )
+    mixed = jnp.where(row < DH, ot[0:LANES, 0:tokens], ot[0:LANES, tokens : 2 * tokens]) * inverse
+    o_ref[...] = jnp.transpose(mixed).astype(BF16)
+    rn_ref[...] = jnp.transpose(inverse)
+
+
+def attention_forward(query, keys, memory, live_row):
+    tokens, width = query.shape
+    pairs = width // LANES
+    block = pl.BlockSpec((tokens, LANES), lambda pair: (0, pair))
+    return pl.pallas_call(
+        attention_forward_kernel,
+        grid=(pairs,),
+        in_specs=[block, block, block, pl.BlockSpec((8, tokens), lambda pair: (0, 0))],
+        out_specs=[block, block, pl.BlockSpec((1, tokens, 2 * tokens), lambda pair: (pair, 0, 0))],
+        out_shape=[
+            jax.ShapeDtypeStruct((tokens, width), BF16),
+            jax.ShapeDtypeStruct((tokens, width), F32),
+            jax.ShapeDtypeStruct((pairs, tokens, 2 * tokens), BF16),
+        ],
+        scratch_shapes=[
+            pltpu.VMEM((2 * tokens, LANES), BF16),
+            pltpu.VMEM((LANES + 16, tokens), BF16),
+            pltpu.VMEM((LANES + 16, 2 * tokens), F32),
+            pltpu.VMEM((tokens, tokens), F32),
+            pltpu.VMEM((tokens, tokens), F32),
+        ],
+        compiler_params=pltpu.CompilerParams(vmem_limit_bytes=60 << 20),
+        cost_estimate=pl.CostEstimate(
+            flops=8 * pairs * tokens * tokens * LANES,
+            transcendentals=2 * pairs * tokens * tokens,
+            bytes_accessed=4 * pairs * tokens * tokens,
+        ),
+    )(query, keys, memory, live_row)
+
+
+def attention_backward_kernel(
+    q_ref, k_ref, v_ref, o_ref, do_ref, rn_ref, live_ref, keep_ref, p_ref,
+    dq_ref, dk_ref, dv_ref, qs, gs, kt, dqt, delta,
+):
+    tokens = q_ref.shape[0]
+    scale = 1.0 / math.sqrt(DH)
+    lane = lax.broadcasted_iota(jnp.int32, (tokens, LANES), 1)
+    query = q_ref[...].astype(F32) * scale
+    qs[0:tokens, :] = jnp.where(lane < DH, query, 0.0).astype(BF16)
+    qs[tokens : 2 * tokens, :] = jnp.where(lane < DH, 0.0, query).astype(BF16)
+    grad = do_ref[...].astype(F32) * rn_ref[...]
+    gs[0:tokens, :] = jnp.where(lane < DH, grad, 0.0).astype(BF16)
+    gs[tokens : 2 * tokens, :] = jnp.where(lane < DH, 0.0, grad).astype(BF16)
+    kt[...] = (jnp.transpose(k_ref[...].astype(F32)) * (live_ref[0:1, :] * scale)).astype(BF16)
+    product = jnp.transpose(grad * o_ref[...].astype(F32))
+    for head in range(2):
+        total = jnp.sum(product[head * DH : (head + 1) * DH], axis=0, keepdims=True)
+        delta[:, head * tokens : (head + 1) * tokens] = jnp.broadcast_to(total, (8, tokens))
+    grad_keys = grad_values = None
+    for head in range(2):
+        span = slice(head * tokens, (head + 1) * tokens)
+        weight = p_ref[0, :, span]
+        grad_weight = matmul_nt(v_ref[...], gs[span, :])
+        grad_score = (weight.astype(F32) * (grad_weight - delta[0:1, span])).astype(BF16)
+        dqt[:, span] = matmul(kt[...], grad_score)
+        part_values = matmul(weight, gs[span, :])
+        part_keys = matmul(grad_score, qs[span, :])
+        grad_values = part_values if grad_values is None else grad_values + part_values
+        grad_keys = part_keys if grad_keys is None else grad_keys + part_keys
+    row = lax.broadcasted_iota(jnp.int32, (LANES, tokens), 0)
+    dq_ref[...] = jnp.transpose(
+        jnp.where(row < DH, dqt[:, 0:tokens], dqt[:, tokens : 2 * tokens])
+    ).astype(BF16)
+    keep = keep_ref[...] > 0
+    dk_ref[...] = jnp.where(keep, grad_keys, 0.0).astype(BF16)
+    dv_ref[...] = jnp.where(keep, grad_values, 0.0).astype(BF16)
+
+
+def attention_backward(query, keys, memory, mixed, grad_mixed, inverse, live_row, live_lanes, weights):
+    tokens, width = query.shape
+    pairs = width // LANES
+    block = pl.BlockSpec((tokens, LANES), lambda pair: (0, pair))
+    return pl.pallas_call(
+        attention_backward_kernel,
+        grid=(pairs,),
+        in_specs=[block] * 6
+        + [
+            pl.BlockSpec((8, tokens), lambda pair: (0, 0)),
+            pl.BlockSpec((tokens, LANES), lambda pair: (0, 0)),
+            pl.BlockSpec((1, tokens, 2 * tokens), lambda pair: (pair, 0, 0)),
+        ],
+        out_specs=[block] * 3,
+        out_shape=[jax.ShapeDtypeStruct((tokens, width), BF16)] * 3,
+        scratch_shapes=[
+            pltpu.VMEM((2 * tokens, LANES), BF16),
+            pltpu.VMEM((2 * tokens, LANES), BF16),
+            pltpu.VMEM((LANES, tokens), BF16),
+            pltpu.VMEM((LANES, 2 * tokens), F32),
+            pltpu.VMEM((8, 2 * tokens), F32),
+        ],
+        compiler_params=pltpu.CompilerParams(vmem_limit_bytes=60 << 20),
+        cost_estimate=pl.CostEstimate(
+            flops=16 * pairs * tokens * tokens * LANES,
+            transcendentals=0,
+            bytes_accessed=4 * pairs * tokens * tokens,
+        ),
+    )(query, keys, memory, mixed, grad_mixed, inverse, live_row, live_lanes, weights)
+
+
+def per_device(
+    patches,
+    col_counts,
+    norm_gain,
+    norm_shift,
+    joint_proj,
+    proj_bias,
+    out_proj,
+    up_proj,
+    up_bias,
+    down_proj,
+    out_bias,
+    cotangent,
+):
+    slots, clips, width = patches.shape
+    group = ("freq", "tm")
+    freq_size = lax.axis_size("freq")
+    time_size = lax.axis_size("tm")
+    members = freq_size * time_size
+    freq_rows = FREQ_ROWS // freq_size
+    cap_cols = (slots - 2) // freq_rows
+    padded = -(-slots // 16) * 16
+    tokens = members * padded
+
+    def to_clip(array):
+        blocks = jnp.pad(jnp.transpose(array, (1, 0, 2)), ((0, 0), (0, padded - slots), (0, 0)))
+        return lax.all_to_all(blocks, group, 0, 0, tiled=True).reshape(tokens, width)
+
+    def to_slots(array):
+        blocks = lax.all_to_all(array.reshape(members, padded, width), group, 0, 0, tiled=True)
+        return jnp.transpose(blocks[:, :slots], (1, 0, 2))
+
+    token_ids = jnp.arange(tokens, dtype=jnp.int32)
+    block_ids = token_ids // padded
+    live = live_slots(
+        col_counts,
+        token_ids % padded,
+        block_ids // time_size,
+        block_ids % time_size,
+        freq_rows,
+        cap_cols,
+    ) & (token_ids % padded < slots)
+    live_full = live.astype(F32)
+    row_live = live_full[:, None]
+    live_row = jnp.broadcast_to(live_full[None, :], (8, tokens))
+    live_lanes = jnp.broadcast_to(row_live, (tokens, LANES))
+
+    gain_full = norm_gain.astype(F32)
+    shift_full = norm_shift.astype(F32)
+    bias_full = proj_bias.astype(F32)
+    outb_full = out_bias.astype(F32)
+    upb_full = up_bias.astype(F32)
+
+    inputs = to_clip(patches).astype(F32)
+    grad_out_low = to_clip(cotangent)
+    normed1, ln1_back = jax.vjp(norm_rows, inputs, gain_full[0], shift_full[0])
+    normed1_low = normed1.astype(BF16)
+    joint = matmul(normed1_low, joint_proj)
+    query_low = (joint[:, :width] + bias_full[0]).astype(BF16)
+    keys_low = joint[:, width : 2 * width].astype(BF16)
+    memory_low = (joint[:, 2 * width :] + bias_full[1]).astype(BF16)
+    keys_low = jnp.where(row_live > 0, keys_low, keys_low[0:1])
+    mixed_low, inverse, weights = attention_forward(query_low, keys_low, memory_low, live_row)
+
+    middle = inputs + matmul(mixed_low, out_proj) + outb_full[0]
+    normed2, ln2_back = jax.vjp(norm_rows, middle, gain_full[1], shift_full[1])
+    normed2_low = normed2.astype(BF16)
+    pre_act = matmul(normed2_low, up_proj) + upb_full
+    activated, gelu_back = jax.vjp(gelu_exact, pre_act)
+    hidden_low = activated.astype(BF16)
+    final = middle + matmul(hidden_low, down_proj) + outb_full[1]
+    output = to_slots((final * row_live).astype(BF16))
+    grad_out_rows = grad_out_low.astype(F32) * row_live
+    grad_out_low = grad_out_rows.astype(BF16)
+    grad_down_part = matmul_tn(hidden_low, grad_out_low)
+    grad_outb_mlp = jnp.sum(grad_out_rows, axis=0)
+    grad_hidden = matmul_nt(grad_out_low, down_proj)
+    grad_pre_low = gelu_back(grad_hidden)[0].astype(BF16)
+    grad_up_part = matmul_tn(normed2_low, grad_pre_low)
+    grad_upb_part = jnp.sum(grad_pre_low.astype(F32), axis=0)
+    grad_normed2 = matmul_nt(grad_pre_low, up_proj)
+    grad_mid_part, grad_gain_mlp, grad_shift_mlp = ln2_back(grad_normed2)
+    grad_middle = grad_out_rows + grad_mid_part
+    grad_branch = grad_middle.astype(BF16)
+    grad_outp_part = matmul_tn(mixed_low, grad_branch)
+    grad_outb_attn = jnp.sum(grad_branch.astype(F32), axis=0)
+    grad_mixed_low = matmul_nt(grad_branch, out_proj).astype(BF16)
+
+    grad_query_low, grad_keys_low, grad_values_low = attention_backward(
+        query_low, keys_low, memory_low, mixed_low, grad_mixed_low, inverse, live_row, live_lanes, weights
+    )
+    grad_joint = jnp.concatenate([grad_query_low, grad_keys_low, grad_values_low], axis=1)
+    grad_joint_part = matmul_tn(normed1_low, grad_joint)
+    grad_normed1 = matmul_nt(grad_joint, joint_proj)
+    grad_in_part, grad_gain_attn, grad_shift_attn = ln1_back(grad_normed1)
+    grad_patches = to_slots((grad_middle + grad_in_part).astype(BF16))
+
+    def share(part):
+        return lax.psum_scatter(part.astype(BF16), group, scatter_dimension=0, tiled=True)
+
+    small = jnp.concatenate(
+        [
+            part.reshape(members, -1)
+            for part in (
+                grad_gain_attn,
+                grad_gain_mlp,
+                grad_shift_attn,
+                grad_shift_mlp,
+                jnp.sum(grad_query_low.astype(F32), axis=0),
+                jnp.sum(grad_values_low.astype(F32), axis=0),
+                grad_outb_attn,
+                grad_outb_mlp,
+                grad_upb_part,
+            )
+        ],
+        axis=1,
+    )
+    down_sum, up_sum, outp_sum, joint_sum, small_sum = (
+        lax.psum(share(part), "dp").astype(F32)
+        for part in (grad_down_part, grad_up_part, grad_outp_part, grad_joint_part, small)
+    )
+    chunk = width // members
+    pieces = [small_sum[0, 2 * i * chunk : 2 * (i + 1) * chunk].reshape(2, chunk) for i in range(4)]
+    return (
+        output,
+        grad_patches,
+        pieces[0],
+        pieces[1],
+        joint_sum,
+        pieces[2],
+        outp_sum,
+        up_sum,
+        small_sum[0, 8 * chunk :],
+        down_sum,
+        pieces[3],
+    )
+
+
+def plan(patches, *others):
+    members = lax.axis_size("freq") * lax.axis_size("tm")
+    if patches.shape[1] == members:
+        return per_device(patches, *others)
+    return per_device_gathered(patches, *others)
+
+
 def solution(mesh):
     return jax.shard_map(
-        per_device,
+        plan,
         mesh=mesh,
         in_specs=(
             P(("freq", "tm"), "dp", None),

time: 1740 us -> 586 us (0.34)
  waiting for transfers between devices: 686 us -> 142 us
  local copies, waits for them, and re-layouts: 349 us -> 48.3 us
  matrix products: 397 us -> 159 us
  other arithmetic: 239 us -> 47.4 us
  Pallas kernels: 0 us -> 108 us
  starting transfers between devices: 1.11 us -> 19.2 us
    reduce_scatter x5 -> x4, waiting for transfers between devices: 459 us -> 98.3 us  [share(): lax.psum_scatter(part.astype(BF16), group, scatter_dimension=0, tiled=True)]
    dot_general x42 -> x0, matrix products: 237 us -> none  [the longest x6 66.2 us: pair_probs(): jnp.einsum('qchd,kchd->chqk', query_pair, key_pair, preferred_element_typ...]
    all_gather x1 -> x0, waiting for transfers between devices: 144 us -> none  [per_device(): all_memory = lax.all_gather(key_value, ('freq', 'tm'), axis=0, tiled=True)]
    while x123 -> x0, local copies, waits for them, and re-layouts: 136 us -> none  [the longest x1 67.7 us: per_device(): lax.fori_loop(0, pair_count, backward_pair, (zero_query, jnp.zeros((key_c...]
    pallas_call x0 -> x2, Pallas kernels: none -> 108 us  [the longest x1 59.1 us: attention_backward(): pl.pallas_call(attention_backward_kernel, grid=(pairs,), in_specs=[block]...]
    dynamic_slice x48 -> x0, local copies, waits for them, and re-layouts: 105 us -> none  [the longest x36 78.8 us: head_pair(): section = lax.dynamic_slice_in_dim(array, offset, lane_width, 2)]
    dynamic_update_slice x18 -> x0, other arithmetic: 86.9 us -> none  [the longest x12 78.9 us: add_lanes(): return lax.dynamic_update_slice_in_dim(target, current + addend, offset, 2)]
    convert_element_type x19 -> x15, other arithmetic: 83 us -> 22.1 us  [the longest x5 7.09 us: per_device(): lax.psum(share(part), 'dp').astype(F32)]
  transfers between devices with their start and end apart: 8 -> 9, of which waited for: 7 -> 5; matrix products, arithmetic and copies ran while one was open for 7% -> 32% of each run, Pallas kernels for 0% -> 19%
where the time goes in v1:
time: 586 us; the launch traced here: 578 us
  matrix products  159 us (27%)
  waiting for transfers between devices  142 us (24%)
  Pallas kernels  108 us (18%)
  local copies, waits for them, and re-layouts  48.3 us (8%)
  other arithmetic  47.4 us (8%)
  blocking collectives  39.4 us (7%)
  starting transfers between devices  19.2 us (3%)
  between operations  14.6 us (2%)
    reduce_scatter x4, waiting for transfers between devices, share(): lax.psum_scatter(part.astype(BF16), group, scatter_dimension=0, tiled=True)  98.3 us
    dot_general x4, matrix products, matmul(): return jnp.dot(left, right, preferred_element_type=jnp.float32)  70.5 us
    pallas_call x1, Pallas kernels, attention_backward(): pl.pallas_call(attention_backward_kernel, grid=(pairs,), in_specs=[block]...  59.1 us
    dot_general x4, matrix products, matmul_nt(): lax.dot_general(left, right, (((1,), (1,)), ((), ())), preferred_element_...  51.7 us
    pallas_call x1, Pallas kernels, attention_forward(): pl.pallas_call(attention_forward_kernel, grid=(pairs,), in_specs=[block,...  48.9 us
    dot_general x4, matrix products, matmul_tn(): lax.dot_general(left, right, (((0,), (0,)), ((), ())), preferred_element_...  36.7 us
    unnamed x1, blocking collectives  27.4 us
    all_to_all x2, waiting for transfers between devices, to_clip(): lax.all_to_all(blocks, group, 0, 0, tiled=True).reshape(tokens, width)  18.3 us
  transfers between devices with their start and end apart: 9, of which 5 were waited for; matrix products, arithmetic and copies ran while one was open for 32% of the time, Pallas kernels for 19%

profile of v1, /device:TPU:0, one launch (start us, length us, event | category | flops | bytes accessed | tf_op | source)
XLA Modules:
  0.0 577.6 jit_solution(8442818810180974357)
XLA Ops:
  10.8 5.2 all-to-all-start
  24.6 18.3 %all-to-all-done = bf16[8,176,768]{2,1,0:T(8,128)(2,1)} async-done(((bf16[8,176,768]{2,1,0:T(8,128)(2,1)}), bf16[8,176,768]{2,1,0:T(8,128)(2,1)}, u32[]{:S(2)}, u32[]{:S(2)}) %all-to-all-start) | async-done | bytes 2162720 | tf_op jit(solution)/shard_map/all_to_all | solution.py:512
  42.9 4.4 all-to-all-start.2
  58.7 5.3 fusion.64
  68.9 48.9 %shard_map.203 = (bf16[1408,768]{1,0:T(8,128)(2,1)}, f32[1408,768]{1,0:T(8,128)}, bf16[6,1408,2816]{2,1,0:T(8,128)(2,1)}) custom-call(bf16[1408,768]{1,0:T(8,128)(2,1)} %get-tuple-element.88.q_ref, bf16[1408,768]{1,0:T(8,128)(2,1)} %slice_select_fusion.k_ref, bf16[1408,768]{1,0:T(8,128)(2,1)} %get-tuple-element.87.v_ref, f32[8,1408]{1,0:T(8,128)} %broadcast_in_dim.67.live_ref), custom_call_target="tpu_custom_call" | custom-call | flops 12180258816 | bytes 47579136 | tf_op jit(solution)/shard_map/pallas_call | solution.py:391
  117.9 4.8 fusion.65
  125.0 48.2 %multiply_convert_fusion = (bf16[1408,3072]{1,0:T(8,128)(2,1)}, f32[1408,3072]{1,0:T(8,128)}, f32[1408,3072]{1,0:T(8,128)}) fusion(f32[3072]{0:T(1024)S(1)} %copy-done.29, bf16[768,3072]{1,0:T(8,128)(2,1)S(1)} %bitcast.82, f32[1408,768]{1,0:T(8,128)S(1)} %get-tuple-element.96, f32[768]{0:T(1024)S(1)} %copy-done.34, f32[768]{0:T(1024)S(1)} %copy-done.25, ...), kind=kOutput, calls=%fused_computation.3 | convolution fusion | flops 6934659072 | bytes 52327424 | tf_op jit(solution)/shard_map/dot_general | solution.py:41
  175.4 23.0 %fusion.66 = (bf16[3072]{0:T(1024)(128)(2,1)}, bf16[1408,3072]{1,0:T(8,128)(2,1)}) fusion(f32[1408,3072]{1,0:T(8,128)} %get-tuple-element.84, bf16[1408,768]{1,0:T(8,128)(2,1)S(1)} %fusion.20, bf16[3072,768]{1,0:T(8,128)(2,1)} %param.21, f32[1408,3072]{1,0:T(8,128)} %get-tuple-element.97, f32[3072]{0:T(1024)S(1)} %copy-done.30), kind=kOutput, calls=%fused_computation.157 | convolution fusion | flops 6712980480 | bytes 50153472 | tf_op jit(solution)/shard_map/dot_general | solution.py:51
  198.4 13.5 %multiply_reduce_fusion.1 = (bf16[768]{0:T(1024)(128)(2,1)}, f32[1408]{0:T(1024)S(1)}, bf16[768]{0:T(1024)(128)(2,1)}, f32[1408,768]{1,0:T(8,128)S(1)}) fusion(f32[1408,768]{1,0:T(8,128)S(1)} %bitcast.76, f32[1408]{0:T(1024)S(1)} %copy-done.24, f32[1408]{0:T(1024)S(1)} %broadcast_multiply_fusion, f32[768]{0:T(1024)S(1)} %copy-done.26, ...), kind=kOutput, calls=%fused_computation.44 | convolution fusion | flops 6652425216 | bytes 22043136 | tf_op jit(solution)/shard_map/dot_general | solution.py:51
  222.2 5.1 convolution_convert_fusion.3.do_ref
  228.9 59.1 %shard_map.204 = (bf16[1408,768]{1,0:T(8,128)(2,1)}, bf16[1408,768]{1,0:T(8,128)(2,1)}, bf16[1408,768]{1,0:T(8,128)(2,1)}) custom-call(bf16[1408,768]{1,0:T(8,128)(2,1)} %get-tuple-element.88.q_ref, bf16[1408,768]{1,0:T(8,128)(2,1)} %slice_select_fusion.k_ref, bf16[1408,768]{1,0:T(8,128)(2,1)} %get-tuple-element.87.v_ref, ...), custom_call_target="tpu_custom_call" | custom-call | flops 24360517632 | bytes 47579136 | tf_op jit(solution)/shard_map/pallas_call | solution.py:459
  295.0 7.2 %convolution_convert_fusion.1 = bf16[768,2304]{1,0:T(8,128)(2,1)} fusion(bf16[1408,768]{1,0:T(8,128)(2,1)S(1)} %copy-done.5, bf16[1408,2304]{1,0:T(8,128)(2,1)S(1)} %get-tuple-element.90), kind=kOutput, calls=%fused_computation.20 | convolution fusion | flops 4984602624 | bytes 12189696 | tf_op jit(solution)/shard_map/dot_general | solution.py:45
  302.3 13.9 %convolution_convert_fusion.2 = bf16[768,3072]{1,0:T(8,128)(2,1)} fusion(bf16[1408,3072]{1,0:T(8,128)(2,1)} %get-tuple-element.101, f32[1408,768]{1,0:T(8,128)} %copy-done.2, f32[768]{0:T(1024)} %get-tuple-element.67, f32[768]{0:T(1024)} %get-tuple-element.103, f32[1408]{0:T(1024)} %copy-done.23, f32[1408]{0:T(1024)S(1)} %broadcast_multiply_fusion), kind=kOutput, calls=%fused_computation.21 | convolution fusion | flops 6651543552 | bytes 17712128 | tf_op jit(solution)/shard_map/dot_general | solution.py:45
  316.3 12.5 %convolution_convert_fusion = bf16[3072,768]{1,0:T(8,128)(2,1)} fusion(bf16[1408,3072]{1,0:T(8,128)(2,1)} %get-tuple-element.83, bf16[1408,768]{1,0:T(8,128)(2,1)} %copy-done.6), kind=kOutput, calls=%fused_computation.19 | convolution fusion | flops 6646136832 | bytes 15532032 | tf_op jit(solution)/shard_map/dot_general | solution.py:45
  329.5 10.0 %fusion.56 = (bf16[768]{0:T(1024)(128)(2,1)}, f32[1408]{0:T(1024)S(1)}, f32[1408,768]{1,0:T(8,128)S(1)}) fusion(f32[768]{0:T(1024)} %get-tuple-element.102, f32[1408]{0:T(1024)S(1)} %copy-done.12, bf16[8,176,768]{2,1,0:T(8,128)(2,1)} %all-to-all-done, bf16[1408,2304]{1,0:T(8,128)(2,1)} %copy-done.9, bf16[768,2304]{1,0:T(8,128)(2,1)S(1)} %copy-done), kind=kOutput, calls=%fused_computation.150 | convolution fusion | flops 4989318656 | bytes 16530944 | tf_op jit(solution)/shard_map/dot_general | solution.py:51
  343.8 5.9 %add_convert_fusion.1 = bf16[1408,768]{1,0:T(8,128)(2,1)} fusion(f32[1408,768]{1,0:T(8,128)} %copy-done.1, bf16[8,176,768]{2,1,0:T(8,128)(2,1)} %all-to-all-done.2, f32[1408]{0:T(1024)S(1)} %negate_multiply_fusion.1, f32[1408]{0:T(1024)S(1)} %copy-done.16, f32[1408]{0:T(1024)S(1)} %get-tuple-element.86, f32[1408]{0:T(1024)S(1)} %multiply_multiply_fusion.5, ...), kind=kLoop, calls=%fused_computation.45 | loop fusion | flops 15138816 | bytes 15175680 | tf_op jit(solution)/shard_map/convert_element_type | solution.py:581
  349.7 4.7 all-to-all-start.3
  354.4 12.3 %multiply_convert_fusion.1 = bf16[1408,768]{1,0:T(8,128)(2,1)} fusion(f32[1408,768]{1,0:T(8,128)} %copy-done.2, bf16[1408,3072]{1,0:T(8,128)(2,1)} %get-tuple-element.83, bf16[3072,768]{1,0:T(8,128)(2,1)} %param.21, f32[1408]{0:T(1024)S(1)} %get-tuple-element.86, f32[768]{0:T(1024)S(1)} %copy-done.33), kind=kOutput, calls=%fused_computation.48 | convolution fusion | flops 6648102912 | bytes 19866112 | tf_op jit(solution)/shard_map/dot_general | solution.py:41
  366.7 14.5 %all-to-all-done.3 = bf16[8,176,768]{2,1,0:T(8,128)(2,1)} async-done(((bf16[8,176,768]{2,1,0:T(8,128)(2,1)}), bf16[8,176,768]{2,1,0:T(8,128)(2,1)}, u32[]{:S(2)}, u32[]{:S(2)}) %all-to-all-start.3) | async-done | bytes 2162720 | tf_op jit(solution)/shard_map/all_to_all | solution.py:515
  385.6 41.0 %reduce-scatter.9.cloned.1.call-done = bf16[96,3072]{1,0:T(8,128)(2,1)} async-done(((bf16[768,3072]{1,0:T(8,128)(2,1)}), bf16[96,3072]{1,0:T(8,128)(2,1)}) %reduce-scatter.9.cloned.1.call-update) | async-done | bytes 589840 | tf_op jit(solution)/shard_map/reduce_scatter | solution.py:584
  426.6 57.2 %reduce-scatter.11.cloned.1.call-done = bf16[384,768]{1,0:T(8,128)(2,1)} async-done(((bf16[3072,768]{1,0:T(8,128)(2,1)}), bf16[384,768]{1,0:T(8,128)(2,1)}) %reduce-scatter.11.cloned.1.call-update) | async-done | bytes 589840 | tf_op jit(solution)/shard_map/reduce_scatter | solution.py:584
  500.3 27.4 %all-reduce.2 = bf16[8,1152]{1,0:T(8,128)(2,1)} all-reduce(bf16[8,1152]{1,0:T(8,128)(2,1)} %concatenate.8), channel_id=2, replica_groups=mesh['dp'=4,'freq'=2,'tm'=4] {'freq','tm'}, use_global_device_ids=true, to_apply=%region_18.19.clone | all-reduce | flops 9216 | bytes 36864
  529.0 12.1 %psum.35 = bf16[1,1152]{1,0:T(2,128)(2,1)S(1)} all-reduce(bf16[1,1152]{1,0:T(2,128)(2,1)S(1)} %constant_dynamic-slice_fusion), channel_id=1, replica_groups=mesh['dp'=4,'freq'=2,'tm'=4] {'dp'}, use_global_device_ids=true, to_apply=%region_19.20 | all-reduce | flops 1152 | bytes 4608 | tf_op jit(solution)/shard_map/psum | solution.py:604
  553.1 10.7 %all-reduce.6.cloned.1.call-done = (bf16[96,2304]{1,0:T(8,128)(2,1)}, bf16[96,768]{1,0:T(8,128)(2,1)}, bf16[96,3072]{1,0:T(8,128)(2,1)}, bf16[384,768]{1,0:T(8,128)(2,1)}) async-done(((bf16[96,2304]{1,0:T(8,128)(2,1)}, bf16[96,768]{1,0:T(8,128)(2,1)}, bf16[96,3072]{1,0:T(8,128)(2,1)}, bf16[384,768]{1,0:T(8,128)(2,1)}), (bf16[96,2304]{1,0:T(8,128)(2,1)}, bf16[96,768]{1,0:T(8,128)(2,1)}, ...) | async-done | bytes 1769488 | tf_op jit(solution)/shard_map/psum | solution.py:604
  (178 shorter events, 97.9 us)
Async XLA Ops:
  7.2 51.5 %copy-start = (bf16[768,2304]{1,0:T(8,128)(2,1)S(1)}, bf16[768,2304]{1,0:T(8,128)(2,1)}, u32[]{:S(2)}) copy-start(bf16[768,2304]{1,0:T(8,128)(2,1)} %param.16) | copy-start | bytes 10616836
  9.3 8.1 %copy-start.32 = (bf16[3072]{0:T(1024)(128)(2,1)S(1)}, bf16[3072]{0:T(1024)(128)(2,1)}, u32[]{:S(2)}) copy-start(bf16[3072]{0:T(1024)(128)(2,1)} %param.20) | copy-start | bytes 18436
  10.8 32.1 %all-to-all-start = ((bf16[8,176,768]{2,1,0:T(8,128)(2,1)}), bf16[8,176,768]{2,1,0:T(8,128)(2,1)}, u32[]{:S(2)}, u32[]{:S(2)}) async-start(bf16[8,176,768]{2,1,0:T(8,128)(2,1)} %pad.7), calls=%async_computation | async-start | bytes 4325376 | tf_op jit(solution)/shard_map/all_to_all | solution.py:512
  16.0 7.3 %copy-start.38 = (s32[4]{0:T(128)S(1)}, s32[4]{0:T(128)}, u32[]{:S(2)}) copy-start(s32[4]{0:T(128)} %param.13) | copy-start | bytes 52
  42.9 130.3 %all-to-all-start.2 = ((bf16[8,176,768]{2,1,0:T(8,128)(2,1)}), bf16[8,176,768]{2,1,0:T(8,128)(2,1)}, u32[]{:S(2)}, u32[]{:S(2)}) async-start(bf16[8,176,768]{2,1,0:T(8,128)(2,1)} %pad.8), calls=%async_computation.2 | async-start | bytes 4325376 | tf_op jit(solution)/shard_map/all_to_all | solution.py:512
  47.3 338.3 %reduce-scatter.7.cloned.1.call-start = ((), (), s32[]{:S(2)}) async-start(), calls=%async_computation.9 | async-start | bytes 1327104 | tf_op jit(solution)/shard_map/reduce_scatter | solution.py:584
  50.7 13.2 %copy-start.11 = (f32[1408]{0:T(1024)}, f32[1408]{0:T(1024)S(1)}, u32[]{:S(2)}) copy-start(f32[1408]{0:T(1024)S(1)} %div.100) | copy-start | bytes 16900
  68.9 48.9 %copy-start.35 = (f32[768]{0:T(1024)S(1)}, f32[768]{0:T(1024)}, u32[]{:S(2)}) copy-start(f32[768]{0:T(1024)} %get-tuple-element.64) | copy-start | bytes 9220
  173.2 25.2 %slice-start = ((s8[4325376]{0:T(1024)(128)(4,1)}), s8[4194304]{0:T(1024)(128)(4,1)S(1)}, s32[]{:S(2)}) async-start(s8[4325376]{0:T(1024)(128)(4,1)} %bitcast.75), calls=%async_computation.13 | async-start | bytes 8388608
  175.4 23.0 %copy-start.6 = (bf16[1408,768]{1,0:T(8,128)(2,1)}, bf16[1408,768]{1,0:T(8,128)(2,1)S(1)}, u32[]{:S(2)}) copy-start(bf16[1408,768]{1,0:T(8,128)(2,1)S(1)} %fusion.20) | copy-start | bytes 6488068
  175.4 23.0 %slice-start.1 = ((s8[4325376]{0:T(1024)(128)(4,1)}), s8[131072]{0:T(1024)(128)(4,1)S(1)}, s32[]{:S(2)}) async-start(s8[4325376]{0:T(1024)(128)(4,1)} %bitcast.75), calls=%async_computation.14 | async-start | bytes 262144
  175.4 23.0 %copy-start.24 = (f32[1408]{0:T(1024)S(1)}, f32[1408]{0:T(1024)}, u32[]{:S(2)}) copy-start(f32[1408]{0:T(1024)} %copy-done.23) | copy-start | bytes 16900
  175.4 23.0 %copy-start.26 = (f32[768]{0:T(1024)S(1)}, f32[768]{0:T(1024)}, u32[]{:S(2)}) copy-start(f32[768]{0:T(1024)} %get-tuple-element.103) | copy-start | bytes 9220
  198.4 13.5 %copy-start.18 = (f32[1408]{0:T(1024)S(1)}, f32[1408]{0:T(1024)}, u32[]{:S(2)}) copy-start(f32[1408]{0:T(1024)} %copy-done.17) | copy-start | bytes 16900
  227.4 158.3 %reduce-scatter.5.cloned.1.call-start = ((), (), s32[]{:S(2)}) async-start(), calls=%async_computation.8 | async-start | bytes 3981312 | tf_op jit(solution)/shard_map/reduce_scatter | solution.py:584
  302.2 124.4 %reduce-scatter.9.cloned.1.call-start = ((), (), s32[]{:S(2)}) async-start(), calls=%async_computation.10 | async-start | bytes 5308416 | tf_op jit(solution)/shard_map/reduce_scatter | solution.py:584
  316.2 167.7 %reduce-scatter.11.cloned.1.call-start = ((), (), s32[]{:S(2)}) async-start(), calls=%async_computation.11 | async-start | bytes 5308416 | tf_op jit(solution)/shard_map/reduce_scatter | solution.py:584
  329.5 10.1 %copy-start.19 = (f32[1408]{0:T(1024)S(1)}, f32[1408]{0:T(1024)}, u32[]{:S(2)}) copy-start(f32[1408]{0:T(1024)} %add.226) | copy-start | bytes 16900
  329.5 10.1 %copy-start.14 = (f32[1408]{0:T(1024)S(1)}, f32[1408]{0:T(1024)}, u32[]{:S(2)}) copy-start(f32[1408]{0:T(1024)} %copy-done.13) | copy-start | bytes 16900
  329.5 10.1 %copy-start.22 = (f32[768]{0:T(1024)S(1)}, f32[768]{0:T(1024)}, u32[]{:S(2)}) copy-start(f32[768]{0:T(1024)} %get-tuple-element.102) | copy-start | bytes 9220
  349.7 31.5 %all-to-all-start.3 = ((bf16[8,176,768]{2,1,0:T(8,128)(2,1)}), bf16[8,176,768]{2,1,0:T(8,128)(2,1)}, u32[]{:S(2)}, u32[]{:S(2)}) async-start(bf16[8,176,768]{2,1,0:T(8,128)(2,1)} %bitcast.77), calls=%async_computation.3 | async-start | bytes 4325376 | tf_op jit(solution)/shard_map/all_to_all | solution.py:515
  366.7 117.2 %copy-start.21 = (s32[1408]{0:T(1024)S(1)}, s32[1408]{0:T(1024)}, u32[]{:S(2)}) copy-start(s32[1408]{0:T(1024)} %copy-done.20) | copy-start | bytes 16900
  381.2 168.5 %all-to-all-start.1 = ((bf16[8,176,768]{2,1,0:T(8,128)(2,1)}), bf16[8,176,768]{2,1,0:T(8,128)(2,1)}, u32[]{:S(2)}, u32[]{:S(2)}) async-start(bf16[8,176,768]{2,1,0:T(8,128)(2,1)} %bitcast.80), calls=%async_computation.1 | async-start | bytes 4325376 | tf_op jit(solution)/shard_map/all_to_all | solution.py:515
  385.5 178.2 %all-reduce.6.cloned.1.call-start = ((), (), s32[]{:S(2)}) async-start(), calls=%async_computation.12 | async-start | bytes 3538944 | tf_op jit(solution)/shard_map/psum | solution.py:604
  (29 other events, 99.8 us)
Sparse Core Ops, SparseCore 0:
  227.5 38.8 reduce-scatter.6
  302.4 50.2 reduce-scatter.4
  356.5 70.0 reduce-scatter.8
  429.9 53.8 reduce-scatter.10
  486.6 77.1 all-reduce.5

commit v2 on v1

--- a/solution.py
+++ b/solution.py
@@ -1,3 +1,4 @@
+import functools
 import math
 
 import jax
@@ -348,31 +349,108 @@
 LANES = 128
 F32 = jnp.float32
 BF16 = jnp.bfloat16
-
-
-def attention_forward_kernel(q_ref, k_ref, v_ref, live_ref, o_ref, rn_ref, p_ref, qs, vt, ot, sa, sb):
+VMEM_LIMIT = 62 << 20
+SAFE_RANGE = 100.0
+COLLECT_FLOPS = 40 * 10**9
+
+
+def normalize(values):
+    centered = values - jnp.mean(values, axis=-1, keepdims=True)
+    inverse = lax.rsqrt(jnp.mean(centered * centered, axis=-1, keepdims=True) + EPS)
+    return centered * inverse, inverse
+
+
+def norm_back(normed, inverse, incoming, gain):
+    scaled = incoming * gain
+    mean = jnp.mean(scaled, axis=-1, keepdims=True)
+    slope = jnp.mean(scaled * normed, axis=-1, keepdims=True)
+    return (scaled - mean - normed * slope) * inverse
+
+
+def column_sum(values):
+    return jnp.sum(values, axis=0, keepdims=True)
+
+
+def project_kernel(x_ref, live_ref, w_ref, vec_ref, n_ref, q_ref, k_ref, v_ref, first_key):
+    width = x_ref.shape[1]
+    normed, _ = normalize(x_ref[...].astype(F32))
+    low = (normed * vec_ref[0:1, :] + vec_ref[1:2, :]).astype(BF16)
+    n_ref[...] = low
+    q_ref[...] = (matmul(low, w_ref[:, 0:width]) + vec_ref[2:3, :]).astype(BF16)
+    keys = matmul(low, w_ref[:, width : 2 * width]).astype(BF16).astype(F32)
+
+    @pl.when(pl.program_id(0) == 0)
+    def _():
+        first_key[...] = jnp.broadcast_to(keys[0:1, :], first_key.shape)
+
+    k_ref[...] = jnp.where(live_ref[:, 0:1] > 0, keys, first_key[0:1, :]).astype(BF16)
+    v_ref[...] = (matmul(low, w_ref[:, 2 * width : 3 * width]) + vec_ref[3:4, :]).astype(BF16)
+
+
+def project(inputs, live_lanes, joint_proj, vectors, steps=4):
+    tokens, width = inputs.shape
+    rows = tokens // steps
+    block = pl.BlockSpec((rows, width), lambda step: (step, 0))
+    return pl.pallas_call(
+        project_kernel,
+        grid=(steps,),
+        in_specs=[
+            block,
+            pl.BlockSpec((rows, LANES), lambda step: (step, 0)),
+            pl.BlockSpec((width, 3 * width), lambda step: (0, 0), pipeline_mode=pl.Buffered(1)),
+            pl.BlockSpec((8, width), lambda step: (0, 0)),
+        ],
+        out_specs=[block] * 4,
+        out_shape=[jax.ShapeDtypeStruct((tokens, width), BF16)] * 4,
+        scratch_shapes=[pltpu.VMEM((8, width), F32)],
+        compiler_params=pltpu.CompilerParams(vmem_limit_bytes=VMEM_LIMIT),
+        cost_estimate=pl.CostEstimate(
+            flops=6 * tokens * width * width, transcendentals=tokens, bytes_accessed=10 * tokens * width
+        ),
+    )(inputs, live_lanes, joint_proj, vectors)
+
+
+def attention_forward_kernel(q_ref, k_ref, v_ref, live_ref, o_ref, rn_ref, p_ref, qs, vt, ot, sa):
     tokens = q_ref.shape[0]
     lane = lax.broadcasted_iota(jnp.int32, (tokens, LANES), 1)
     query = q_ref[...].astype(F32) * (1.0 / math.sqrt(DH))
+    keys = k_ref[...].astype(F32)
     qs[0:tokens, :] = jnp.where(lane < DH, query, 0.0).astype(BF16)
     qs[tokens : 2 * tokens, :] = jnp.where(lane < DH, 0.0, query).astype(BF16)
     live = live_ref[0:1, :]
     vt[0:LANES, :] = (jnp.transpose(v_ref[...].astype(F32)) * live).astype(BF16)
     vt[LANES : LANES + 16, :] = jnp.broadcast_to(live, (16, tokens)).astype(BF16)
 
-    def scores(head):
-        return matmul_nt(k_ref[...], qs[head * tokens : (head + 1) * tokens, :])
-
-    def finish(head, score):
-        highest = jnp.max(score, axis=0, keepdims=True)
-        weight = jnp.exp2(score * LOG2E - highest * LOG2E).astype(BF16)
-        p_ref[0, :, head * tokens : (head + 1) * tokens] = weight
-        ot[:, head * tokens : (head + 1) * tokens] = matmul(vt[...], weight)
-
-    sa[...] = scores(0)
-    sb[...] = scores(1)
-    finish(0, sa[...])
-    finish(1, sb[...])
+    def largest(values, head):
+        squares = jnp.where((lane < DH) == (head == 0), values * values, 0.0)
+        return jnp.max(jnp.sum(squares, axis=1, keepdims=True))
+
+    limit = (SAFE_RANGE / LOG2E) ** 2
+    bound = jnp.maximum(
+        largest(query, 0) * largest(keys, 0), largest(query, 1) * largest(keys, 1)
+    )
+    bounded = bound <= limit
+
+    def finish(span, weight):
+        p_ref[0, :, span] = weight
+        ot[:, span] = matmul(vt[...], weight)
+
+    @pl.when(bounded)
+    def _():
+        for head in range(2):
+            span = slice(head * tokens, (head + 1) * tokens)
+            finish(span, jnp.exp2(matmul_nt(k_ref[...], qs[span, :]) * LOG2E).astype(BF16))
+
+    @pl.when(jnp.logical_not(bounded))
+    def _():
+        for head in range(2):
+            for start in range(0, tokens, sa.shape[1]):
+                span = slice(head * tokens + start, head * tokens + start + sa.shape[1])
+                sa[...] = matmul_nt(k_ref[...], qs[span, :])
+                score = sa[...]
+                highest = jnp.max(score, axis=0, keepdims=True)
+                finish(span, jnp.exp2(score * LOG2E - highest * LOG2E).astype(BF16))
+
     row = lax.broadcasted_iota(jnp.int32, (LANES, tokens), 0)
     inverse = jnp.where(
         row < DH,
@@ -402,10 +480,9 @@
             pltpu.VMEM((2 * tokens, LANES), BF16),
             pltpu.VMEM((LANES + 16, tokens), BF16),
             pltpu.VMEM((LANES + 16, 2 * tokens), F32),
-            pltpu.VMEM((tokens, tokens), F32),
-            pltpu.VMEM((tokens, tokens), F32),
-        ],
-        compiler_params=pltpu.CompilerParams(vmem_limit_bytes=60 << 20),
+            pltpu.VMEM((tokens, LANES), F32),
+        ],
+        compiler_params=pltpu.CompilerParams(vmem_limit_bytes=VMEM_LIMIT),
         cost_estimate=pl.CostEstimate(
             flops=8 * pairs * tokens * tokens * LANES,
             transcendentals=2 * pairs * tokens * tokens,
@@ -415,8 +492,9 @@
 
 
 def attention_backward_kernel(
-    q_ref, k_ref, v_ref, o_ref, do_ref, rn_ref, live_ref, keep_ref, p_ref,
-    dq_ref, dk_ref, dv_ref, qs, gs, kt, dqt, delta,
+    q_ref, k_ref, v_ref, o_ref, do_ref, rn_ref, live_ref, keep_ref, p_ref, n_ref, wq_ref, wk_ref, wv_ref,
+    x_ref, res_ref, vec_ref, sums_ref, half_ref,
+    kept_ref, sent_ref, dx_ref, qs, gs, kt, dqt, delta, dj, dn, vecs,
 ):
     tokens = q_ref.shape[0]
     scale = 1.0 / math.sqrt(DH)
@@ -430,7 +508,7 @@
     kt[...] = (jnp.transpose(k_ref[...].astype(F32)) * (live_ref[0:1, :] * scale)).astype(BF16)
     product = jnp.transpose(grad * o_ref[...].astype(F32))
     for head in range(2):
-        total = jnp.sum(product[head * DH : (head + 1) * DH], axis=0, keepdims=True)
+        total = column_sum(product[head * DH : (head + 1) * DH])
         delta[:, head * tokens : (head + 1) * tokens] = jnp.broadcast_to(total, (8, tokens))
     grad_keys = grad_values = None
     for head in range(2):
@@ -444,43 +522,353 @@
         grad_values = part_values if grad_values is None else grad_values + part_values
         grad_keys = part_keys if grad_keys is None else grad_keys + part_keys
     row = lax.broadcasted_iota(jnp.int32, (LANES, tokens), 0)
-    dq_ref[...] = jnp.transpose(
-        jnp.where(row < DH, dqt[:, 0:tokens], dqt[:, tokens : 2 * tokens])
-    ).astype(BF16)
+    grad_query = jnp.transpose(jnp.where(row < DH, dqt[:, 0:tokens], dqt[:, tokens : 2 * tokens]))
     keep = keep_ref[...] > 0
-    dk_ref[...] = jnp.where(keep, grad_keys, 0.0).astype(BF16)
-    dv_ref[...] = jnp.where(keep, grad_values, 0.0).astype(BF16)
-
-
-def attention_backward(query, keys, memory, mixed, grad_mixed, inverse, live_row, live_lanes, weights):
+    dj[:, 0:LANES] = grad_query.astype(BF16)
+    dj[:, LANES : 2 * LANES] = jnp.where(keep, grad_keys, 0.0).astype(BF16)
+    dj[:, 2 * LANES : 3 * LANES] = jnp.where(keep, grad_values, 0.0).astype(BF16)
+    joint = dj[...]
+    grad_weights = matmul_tn(n_ref[...], joint).astype(BF16)
+    half = grad_weights.shape[0] // 2
+    first = half_ref[0] == 0
+    columns = pl.ds(pl.multiple_of(pl.program_id(0) * (3 * LANES), LANES), 3 * LANES)
+    kept_ref[:, columns] = jnp.where(first, grad_weights[:half], grad_weights[half:])
+    sent_ref[:, columns] = jnp.where(first, grad_weights[half:], grad_weights[:half])
+    sums = column_sum(joint.astype(F32))
+    columns = pl.ds(pl.multiple_of(pl.program_id(0) * LANES, LANES), LANES)
+    vecs[2:3, columns] = sums[:, 0:LANES]
+    vecs[3:4, columns] = sums[:, 2 * LANES : 3 * LANES]
+    weights = jnp.concatenate([wq_ref[...], wk_ref[...], wv_ref[...]], axis=1)
+    grad_normed = matmul_nt(joint, weights)
+
+    @pl.when(pl.program_id(0) == 0)
+    def _():
+        dn[...] = grad_normed
+
+    @pl.when(pl.program_id(0) > 0)
+    def _():
+        dn[...] += grad_normed
+
+    @pl.when(pl.program_id(0) == pl.num_programs(0) - 1)
+    def _():
+        vecs[0:2, :] = jnp.zeros((2, vecs.shape[1]), F32)
+        vecs[4:8, :] = sums_ref[0:4, :]
+        rows = 2 * LANES if tokens % (2 * LANES) == 0 else LANES
+
+        def chunk(index, _):
+            span = pl.ds(pl.multiple_of(index * rows, rows), rows)
+            normed, inverse = normalize(x_ref[span, :].astype(F32))
+            incoming = dn[span, :]
+            vecs[0:1, :] += column_sum(incoming * normed)
+            vecs[1:2, :] += column_sum(incoming)
+            back = norm_back(normed, inverse, incoming, vec_ref[0:1, :])
+            dx_ref[span, :] = (res_ref[span, :].astype(F32) + back).astype(BF16)
+            return 0
+
+        lax.fori_loop(0, tokens // rows, chunk, 0)
+        turned = jnp.transpose(jnp.concatenate([vecs[...]] * (LANES // 8), axis=0)).astype(BF16)
+        tail = kept_ref.shape[1] - LANES
+        kept_ref[:, tail:] = jnp.where(first, turned[:half], turned[half:])
+        sent_ref[:, tail:] = jnp.where(first, turned[half:], turned[:half])
+
+
+def attention_backward(
+    query, keys, memory, mixed, grad_mixed, inverse, live_row, live_lanes, weights, normed, joint_proj,
+    inputs, residual, vectors, vector_grads, own_half,
+):
     tokens, width = query.shape
     pairs = width // LANES
     block = pl.BlockSpec((tokens, LANES), lambda pair: (0, pair))
+    once = pl.Buffered(1)
+
+    def fixed(rows, columns):
+        return pl.BlockSpec((rows, columns), lambda pair: (0, 0), pipeline_mode=once)
+
+    def columns(part):
+        return pl.BlockSpec((width, LANES), lambda pair: (0, part * pairs + pair))
+
     return pl.pallas_call(
         attention_backward_kernel,
         grid=(pairs,),
         in_specs=[block] * 6
         + [
-            pl.BlockSpec((8, tokens), lambda pair: (0, 0)),
-            pl.BlockSpec((tokens, LANES), lambda pair: (0, 0)),
+            fixed(8, tokens),
+            fixed(tokens, LANES),
             pl.BlockSpec((1, tokens, 2 * tokens), lambda pair: (pair, 0, 0)),
-        ],
-        out_specs=[block] * 3,
-        out_shape=[jax.ShapeDtypeStruct((tokens, width), BF16)] * 3,
+            fixed(tokens, width),
+            columns(0),
+            columns(1),
+            columns(2),
+            fixed(tokens, width),
+            fixed(tokens, width),
+            fixed(8, width),
+            fixed(8, width),
+            pl.BlockSpec(memory_space=pltpu.SMEM),
+        ],
+        out_specs=[fixed(width // 2, 3 * width + LANES), fixed(width // 2, 3 * width + LANES), fixed(tokens, width)],
+        out_shape=[
+            jax.ShapeDtypeStruct((width // 2, 3 * width + LANES), BF16),
+            jax.ShapeDtypeStruct((width // 2, 3 * width + LANES), BF16),
+            jax.ShapeDtypeStruct((tokens, width), BF16),
+        ],
         scratch_shapes=[
             pltpu.VMEM((2 * tokens, LANES), BF16),
             pltpu.VMEM((2 * tokens, LANES), BF16),
             pltpu.VMEM((LANES, tokens), BF16),
             pltpu.VMEM((LANES, 2 * tokens), F32),
             pltpu.VMEM((8, 2 * tokens), F32),
-        ],
-        compiler_params=pltpu.CompilerParams(vmem_limit_bytes=60 << 20),
+            pltpu.VMEM((tokens, 3 * LANES), BF16),
+            pltpu.VMEM((tokens, width), F32),
+            pltpu.VMEM((8, width), F32),
+        ],
+        compiler_params=pltpu.CompilerParams(vmem_limit_bytes=VMEM_LIMIT),
         cost_estimate=pl.CostEstimate(
             flops=16 * pairs * tokens * tokens * LANES,
             transcendentals=0,
             bytes_accessed=4 * pairs * tokens * tokens,
         ),
-    )(query, keys, memory, mixed, grad_mixed, inverse, live_row, live_lanes, weights)
+    )(
+        query, keys, memory, mixed, grad_mixed, inverse, live_row, live_lanes, weights, normed,
+        joint_proj, joint_proj, joint_proj, inputs, residual, vectors, vector_grads,
+        own_half,
+    )
+
+
+def feed_forward_kernel(
+    x_ref, mixed_ref, cot_ref, live_ref, wo_ref, vec_ref, up_ref, down_ref, bias_ref,
+    out_ref, branch_ref, gm_ref, packed_ref, ds_ref,
+    normed, grad_out, middle, acc, acc_grad, hidden, grad_pre, down_buf, up_buf, down_sem, up_sem,
+):
+    step = pl.program_id(0)
+    last = pl.num_programs(0) - 1
+    tokens, width = x_ref.shape
+    units = up_ref.shape[1]
+    rows = tokens // 4
+    block = tokens // out_ref.shape[0]
+
+    @pl.when(step == 0)
+    def _():
+        def chunk(index, _):
+            span = pl.ds(pl.multiple_of(index * rows, 32), rows)
+            values = x_ref[span, :].astype(F32) + matmul(mixed_ref[span, :], wo_ref[...]) + vec_ref[2:3, :]
+            middle[span, :] = values
+            acc[span, :] = values + vec_ref[3:4, :]
+            unit, _ = normalize(values)
+            normed[span, :] = (unit * vec_ref[0:1, :] + vec_ref[1:2, :]).astype(BF16)
+            grad_out[span, :] = (cot_ref[span, :].astype(F32) * live_ref[span, 0:1]).astype(BF16)
+            acc_grad[span, :] = jnp.zeros((rows, width), F32)
+            return 0
+
+        lax.fori_loop(0, 4, chunk, 0)
+
+    up = up_ref[...]
+    down = down_ref[...]
+    grad_bias = jnp.zeros((1, units), F32)
+    half = tokens // 2
+    for start in (0, half):
+        span = slice(start, start + half)
+        pre_act = matmul(normed[span, :], up) + bias_ref[0:1, :]
+        grad_hidden = matmul_nt(grad_out[span, :], down)
+        cumulative = 0.5 + 0.5 * lax.erf(pre_act * math.sqrt(0.5))
+        density = jnp.exp2(pre_act * pre_act * (-0.5 * LOG2E)) * (1.0 / math.sqrt(2.0 * math.pi))
+        low = (pre_act * cumulative).astype(BF16)
+        grad_low = (grad_hidden * (cumulative + pre_act * density)).astype(BF16)
+        grad_bias = grad_bias + column_sum(grad_low.astype(F32))
+        hidden[span, :] = low
+        grad_pre[span, :] = grad_low
+        acc[span, :] += matmul(low, down)
+        acc_grad[span, :] += matmul_nt(grad_low, up)
+    slot = lax.rem(step, 2)
+    _, cuts, quarters, share, _ = down_buf.shape
+    own = units // cuts
+    for cut in range(cuts):
+        sums = jnp.broadcast_to(grad_bias[:, cut * own : (cut + 1) * own], (16, own)).astype(BF16)
+        out_ref[step * cuts + cut, block + share : block + share + 16, 0:own] = sums
+        out_ref[step * cuts + cut, block + share : block + share + 16, own:width] = jnp.zeros((16, width - own), BF16)
+
+    def copies(at, slot):
+        return (
+            pltpu.make_async_copy(
+                down_buf.at[slot], packed_ref.at[pl.ds(at * cuts, cuts), pl.ds(0, quarters)], down_sem.at[slot]
+            ),
+            pltpu.make_async_copy(up_buf.at[slot], packed_ref.at[:, quarters + at], up_sem.at[slot]),
+        )
+
+    @pl.when(step >= 2)
+    def _():
+        for copy in copies(step - 2, slot):
+            copy.wait()
+
+    grad_down = matmul_tn(hidden[...], grad_out[...]).astype(BF16)
+    for cut in range(cuts):
+        for quarter in range(quarters):
+            base = (cut * quarters + quarter) * share
+            down_buf[slot, cut, quarter] = grad_down[base : base + share]
+    grad_up = matmul_tn(normed[...], grad_pre[...]).astype(BF16)
+    for member in range(width // share):
+        up_buf[slot, member] = grad_up[member * share : (member + 1) * share]
+    for copy in copies(step, slot):
+        copy.start()
+
+    @pl.when(step == last)
+    def _():
+        ds_ref[...] = jnp.zeros_like(ds_ref)
+
+        def chunk(index, _):
+            span = pl.ds(pl.multiple_of(index * rows, 32), rows)
+            final = (acc[span, :] * live_ref[span, 0:1]).astype(BF16)
+            for part in range(rows // block):
+                out_ref[index * (rows // block) + part, 0:block, :] = final[part * block : (part + 1) * block]
+            unit, inverse = normalize(middle[span, :])
+            incoming = acc_grad[span, :]
+            start = grad_out[span, :].astype(F32)
+            branch = (start + norm_back(unit, inverse, incoming, vec_ref[0:1, :])).astype(BF16)
+            branch_ref[span, :] = branch
+            gm_ref[span, :] = matmul_nt(branch, wo_ref[...]).astype(BF16)
+            ds_ref[0:1, :] += column_sum(incoming * unit)
+            ds_ref[1:2, :] += column_sum(incoming)
+            ds_ref[2:3, :] += column_sum(branch.astype(F32))
+            ds_ref[3:4, :] += column_sum(start)
+            return 0
+
+        lax.fori_loop(0, 4, chunk, 0)
+        grad_outp = matmul_tn(mixed_ref[...], branch_ref[...]).astype(BF16)
+        for member in range(width // share):
+            out_ref[member, block : block + share, :] = grad_outp[member * share : (member + 1) * share]
+        for copy in copies(step - 1, 1 - slot):
+            copy.wait()
+        for copy in copies(step, slot):
+            copy.wait()
+
+
+def feed_forward(inputs, mixed, cotangent, live_lanes, out_proj, vectors, up_proj, up_bias, down_proj, members):
+    tokens, width = inputs.shape
+    hidden_units = up_proj.shape[1]
+    steps = hidden_units // width
+    share = width // members
+    cuts = members // steps
+    quarters = hidden_units // members // share
+    once = pl.Buffered(1)
+
+    def fixed(rows, columns):
+        return pl.BlockSpec((rows, columns), lambda step: (0, 0), pipeline_mode=once)
+
+    return pl.pallas_call(
+        feed_forward_kernel,
+        grid=(steps,),
+        in_specs=[
+            fixed(tokens, width),
+            fixed(tokens, width),
+            fixed(tokens, width),
+            fixed(tokens, LANES),
+            fixed(width, width),
+            fixed(8, width),
+            pl.BlockSpec((width, width), lambda step: (0, step)),
+            pl.BlockSpec((width, width), lambda step: (step, 0)),
+            pl.BlockSpec((8, width), lambda step: (0, step)),
+        ],
+        out_specs=[
+            pl.BlockSpec((members, tokens // members + share + 16, width), lambda step: (0, 0, 0), pipeline_mode=once),
+            fixed(tokens, width),
+            fixed(tokens, width),
+            pl.BlockSpec(memory_space=pl.ANY),
+            fixed(8, width),
+        ],
+        out_shape=[
+            jax.ShapeDtypeStruct((members, tokens // members + share + 16, width), BF16),
+            jax.ShapeDtypeStruct((tokens, width), BF16),
+            jax.ShapeDtypeStruct((tokens, width), BF16),
+            jax.ShapeDtypeStruct((members, quarters + steps, share, width), BF16),
+            jax.ShapeDtypeStruct((8, width), F32),
+        ],
+        scratch_shapes=[
+            pltpu.VMEM((tokens, width), BF16),
+            pltpu.VMEM((tokens, width), BF16),
+            pltpu.VMEM((tokens, width), F32),
+            pltpu.VMEM((tokens, width), F32),
+            pltpu.VMEM((tokens, width), F32),
+            pltpu.VMEM((tokens, width), BF16),
+            pltpu.VMEM((tokens, width), BF16),
+            pltpu.VMEM((2, cuts, quarters, share, width), BF16),
+            pltpu.VMEM((2, members, share, width), BF16),
+            pltpu.SemaphoreType.DMA((2,)),
+            pltpu.SemaphoreType.DMA((2,)),
+        ],
+        compiler_params=pltpu.CompilerParams(vmem_limit_bytes=VMEM_LIMIT),
+        cost_estimate=pl.CostEstimate(
+            flops=12 * tokens * width * hidden_units + 6 * tokens * width * width,
+            transcendentals=2 * tokens * hidden_units,
+            bytes_accessed=12 * tokens * width + 8 * width * hidden_units,
+        ),
+    )(inputs, mixed, cotangent, live_lanes, out_proj, vectors, up_proj, down_proj, up_bias)
+
+
+def collect_joint_kernel(own_ref, *refs):
+    pieces, (joint_ref, gain_ref, shift_ref, bias_ref, branch_ref, columns) = refs[:-6], refs[-6:]
+    rows = pieces[0].shape[0]
+    width = joint_ref.shape[1] // 3
+    own = own_ref[0]
+    columns[...] = jnp.zeros_like(columns)
+    for place in range(len(pieces)):
+        piece = pieces[place][...]
+        for other in range(1, len(pieces)):
+            piece = jnp.where(own == other, pieces[place ^ other][...], piece)
+        piece = piece.astype(F32)
+        span = slice(place * rows, (place + 1) * rows)
+        for pair in range(width // LANES):
+            for part in range(3):
+                at = (pair * 3 + part) * LANES
+                to = part * width + pair * LANES
+                joint_ref[span, to : to + LANES] = piece[:, at : at + LANES]
+        columns[span, :] = piece[:, 3 * width :]
+    turned = jnp.transpose(columns[...])
+    share = gain_ref.shape[1]
+    gain_ref[0:1, :] = turned[0:1, 0:share]
+    gain_ref[1:2, :] = turned[4:5, 0:share]
+    shift_ref[0:1, :] = turned[1:2, 0:share]
+    shift_ref[1:2, :] = turned[5:6, 0:share]
+    bias_ref[...] = turned[2:4, 0:share]
+    branch_ref[...] = turned[6:8, 0:share]
+
+
+def collect_joint(own, pieces, share):
+    width = (pieces[0].shape[1] - LANES) // 3
+    vmem = pl.BlockSpec(memory_space=pltpu.VMEM)
+    return pl.pallas_call(
+        collect_joint_kernel,
+        in_specs=[pl.BlockSpec(memory_space=pltpu.SMEM)] + [vmem] * len(pieces),
+        out_specs=[vmem] * 5,
+        out_shape=[jax.ShapeDtypeStruct((share, 3 * width), F32)] + [jax.ShapeDtypeStruct((2, share), F32)] * 4,
+        scratch_shapes=[pltpu.VMEM((LANES, LANES), F32)],
+    )(own, *pieces)
+
+
+def collect_mlp_kernel(rows_ref, sums_ref, down_ref, up_ref, outp_ref, bias_ref):
+    own, width = down_ref.shape
+    share = outp_ref.shape[0]
+    down_ref[...] = rows_ref[0:own, :].astype(F32)
+    for part in range(own // share):
+        rows = slice(own + part * share, own + (part + 1) * share)
+        up_ref[:, part * width : (part + 1) * width] = rows_ref[rows, :].astype(F32)
+    outp_ref[...] = sums_ref[0:share, :].astype(F32)
+    bias_ref[...] = sums_ref[share : share + 16, 0:own].astype(F32)[0:1, :]
+
+
+def collect_mlp(rows, sums, share):
+    own, width = rows.shape[0] // 2, rows.shape[1]
+    vmem = pl.BlockSpec(memory_space=pltpu.VMEM)
+    return pl.pallas_call(
+        collect_mlp_kernel,
+        in_specs=[vmem] * 2,
+        out_specs=[vmem] * 4,
+        out_shape=[
+            jax.ShapeDtypeStruct((own, width), F32),
+            jax.ShapeDtypeStruct((share, own // share * width), F32),
+            jax.ShapeDtypeStruct((share, width), F32),
+            jax.ShapeDtypeStruct((1, own), F32),
+        ],
+        cost_estimate=pl.CostEstimate(flops=COLLECT_FLOPS, transcendentals=0, bytes_accessed=4 * rows.size),
+    )(rows, sums)
 
 
 def per_device(
@@ -501,11 +889,15 @@
     group = ("freq", "tm")
     freq_size = lax.axis_size("freq")
     time_size = lax.axis_size("tm")
+    groups = lax.axis_size("dp")
     members = freq_size * time_size
     freq_rows = FREQ_ROWS // freq_size
     cap_cols = (slots - 2) // freq_rows
     padded = -(-slots // 16) * 16
     tokens = members * padded
+    pairs = width // LANES
+    share = width // members
+    hidden_units = up_proj.shape[1]
 
     def to_clip(array):
         blocks = jnp.pad(jnp.transpose(array, (1, 0, 2)), ((0, 0), (0, padded - slots), (0, 0)))
@@ -526,98 +918,71 @@
         cap_cols,
     ) & (token_ids % padded < slots)
     live_full = live.astype(F32)
-    row_live = live_full[:, None]
     live_row = jnp.broadcast_to(live_full[None, :], (8, tokens))
-    live_lanes = jnp.broadcast_to(row_live, (tokens, LANES))
-
-    gain_full = norm_gain.astype(F32)
-    shift_full = norm_shift.astype(F32)
-    bias_full = proj_bias.astype(F32)
-    outb_full = out_bias.astype(F32)
-    upb_full = up_bias.astype(F32)
-
-    inputs = to_clip(patches).astype(F32)
-    grad_out_low = to_clip(cotangent)
-    normed1, ln1_back = jax.vjp(norm_rows, inputs, gain_full[0], shift_full[0])
-    normed1_low = normed1.astype(BF16)
-    joint = matmul(normed1_low, joint_proj)
-    query_low = (joint[:, :width] + bias_full[0]).astype(BF16)
-    keys_low = joint[:, width : 2 * width].astype(BF16)
-    memory_low = (joint[:, 2 * width :] + bias_full[1]).astype(BF16)
-    keys_low = jnp.where(row_live > 0, keys_low, keys_low[0:1])
-    mixed_low, inverse, weights = attention_forward(query_low, keys_low, memory_low, live_row)
-
-    middle = inputs + matmul(mixed_low, out_proj) + outb_full[0]
-    normed2, ln2_back = jax.vjp(norm_rows, middle, gain_full[1], shift_full[1])
-    normed2_low = normed2.astype(BF16)
-    pre_act = matmul(normed2_low, up_proj) + upb_full
-    activated, gelu_back = jax.vjp(gelu_exact, pre_act)
-    hidden_low = activated.astype(BF16)
-    final = middle + matmul(hidden_low, down_proj) + outb_full[1]
-    output = to_slots((final * row_live).astype(BF16))
-    grad_out_rows = grad_out_low.astype(F32) * row_live
-    grad_out_low = grad_out_rows.astype(BF16)
-    grad_down_part = matmul_tn(hidden_low, grad_out_low)
-    grad_outb_mlp = jnp.sum(grad_out_rows, axis=0)
-    grad_hidden = matmul_nt(grad_out_low, down_proj)
-    grad_pre_low = gelu_back(grad_hidden)[0].astype(BF16)
-    grad_up_part = matmul_tn(normed2_low, grad_pre_low)
-    grad_upb_part = jnp.sum(grad_pre_low.astype(F32), axis=0)
-    grad_normed2 = matmul_nt(grad_pre_low, up_proj)
-    grad_mid_part, grad_gain_mlp, grad_shift_mlp = ln2_back(grad_normed2)
-    grad_middle = grad_out_rows + grad_mid_part
-    grad_branch = grad_middle.astype(BF16)
-    grad_outp_part = matmul_tn(mixed_low, grad_branch)
-    grad_outb_attn = jnp.sum(grad_branch.astype(F32), axis=0)
-    grad_mixed_low = matmul_nt(grad_branch, out_proj).astype(BF16)
-
-    grad_query_low, grad_keys_low, grad_values_low = attention_backward(
-        query_low, keys_low, memory_low, mixed_low, grad_mixed_low, inverse, live_row, live_lanes, weights
-    )
-    grad_joint = jnp.concatenate([grad_query_low, grad_keys_low, grad_values_low], axis=1)
-    grad_joint_part = matmul_tn(normed1_low, grad_joint)
-    grad_normed1 = matmul_nt(grad_joint, joint_proj)
-    grad_in_part, grad_gain_attn, grad_shift_attn = ln1_back(grad_normed1)
-    grad_patches = to_slots((grad_middle + grad_in_part).astype(BF16))
-
-    def share(part):
-        return lax.psum_scatter(part.astype(BF16), group, scatter_dimension=0, tiled=True)
-
-    small = jnp.concatenate(
-        [
-            part.reshape(members, -1)
-            for part in (
-                grad_gain_attn,
-                grad_gain_mlp,
-                grad_shift_attn,
-                grad_shift_mlp,
-                jnp.sum(grad_query_low.astype(F32), axis=0),
-                jnp.sum(grad_values_low.astype(F32), axis=0),
-                grad_outb_attn,
-                grad_outb_mlp,
-                grad_upb_part,
-            )
-        ],
-        axis=1,
-    )
-    down_sum, up_sum, outp_sum, joint_sum, small_sum = (
-        lax.psum(share(part), "dp").astype(F32)
-        for part in (grad_down_part, grad_up_part, grad_outp_part, grad_joint_part, small)
-    )
-    chunk = width // members
-    pieces = [small_sum[0, 2 * i * chunk : 2 * (i + 1) * chunk].reshape(2, chunk) for i in range(4)]
+    live_lanes = jnp.broadcast_to(live_full[:, None], (tokens, LANES))
+
+    def rows_of(*vectors):
+        stacked = jnp.stack(vectors).astype(F32)
+        return jnp.pad(stacked, ((0, 8 - len(vectors)), (0, 0)))
+
+    vectors1 = rows_of(norm_gain[0], norm_shift[0], proj_bias[0], proj_bias[1])
+    vectors2 = rows_of(norm_gain[1], norm_shift[1], out_bias[0], out_bias[1])
+    bias_rows = jnp.broadcast_to(up_bias.astype(F32)[None, :], (8, hidden_units))
+
+    inputs = to_clip(patches)
+    cot = to_clip(cotangent)
+    normed1, query, keys, memory = project(inputs, live_lanes, joint_proj, vectors1)
+    mixed, inverse, weights = attention_forward(query, keys, memory, live_row)
+    blocks, branch, grad_mixed, packed, vector_grads = feed_forward(
+        inputs, mixed, cot, live_lanes, out_proj, vectors2, up_proj, bias_rows, down_proj, members
+    )
+    own = hidden_units // members
+    mlp_rows = lax.psum_scatter(packed.reshape(members, 2 * own, width), group, scatter_dimension=0, tiled=True)[0]
+    moved = lax.all_to_all(blocks, group, 0, 0, tiled=True)
+
+    own_half = lax.axis_index("freq")
+    own_group = lax.axis_index("dp")
+    kept, sent, grad_tokens = attention_backward(
+        query, keys, memory, mixed, grad_mixed, inverse, live_row, live_lanes, weights, normed1, joint_proj,
+        inputs, branch, vectors1, vector_grads, own_half.reshape(1),
+    )
+    kept, sent, moved = lax.optimization_barrier((kept, sent, moved))
+    got = lax.ppermute(sent, "freq", [(0, 1), (1, 0)])
+    outp_rows = jnp.sum(moved[:, padded:].astype(F32), axis=0).astype(BF16)
+    joint_half = (kept.astype(F32) + got.astype(F32)).astype(BF16).reshape(time_size, share, kept.shape[1])
+    joint_half, mlp_rows, outp_rows = lax.optimization_barrier((joint_half, mlp_rows, outp_rows))
+    mlp_sum, outp_sum = lax.psum((mlp_rows, outp_rows), "dp")
+    arrived = lax.all_to_all(joint_half, "tm", 0, 0, tiled=True)
+    joint_rows = jnp.sum(arrived.astype(F32), axis=0).astype(BF16)
+    joint_rows, grad_tokens, moved = lax.optimization_barrier((joint_rows, grad_tokens, moved))
+
+    def to_group(array, distance):
+        return lax.ppermute(array, "dp", [(i, i ^ distance) for i in range(groups)])
+
+    cut = joint_rows.reshape(groups, share // groups, kept.shape[1])
+    piece = lax.dynamic_index_in_dim(cut, own_group, 0, False).astype(F32)
+    for distance in range(1, groups):
+        piece += to_group(lax.dynamic_index_in_dim(cut, own_group ^ distance, 0, False), distance).astype(F32)
+    piece = piece.astype(BF16)
+    pieces = [piece] + [to_group(piece, distance) for distance in range(1, groups)]
+    output = jnp.transpose(moved[:, :slots], (1, 0, 2))
+    grad_patches = to_slots(grad_tokens)
+
+    pieces[1], mlp_sum, outp_sum = lax.optimization_barrier((pieces[1], mlp_sum, outp_sum))
+    down_sum, up_sum, outp_sum, up_bias_sum = collect_mlp(mlp_sum, outp_sum, share)
+    joint_sum, gain_sum, shift_sum, bias_sum, branch_sum = collect_joint(own_group.reshape(1), pieces, share)
     return (
         output,
         grad_patches,
-        pieces[0],
-        pieces[1],
+        gain_sum,
+        shift_sum,
         joint_sum,
-        pieces[2],
+        bias_sum,
         outp_sum,
         up_sum,
-        small_sum[0, 8 * chunk :],
+        up_bias_sum[0],
         down_sum,
-        pieces[3],
+        branch_sum,
     )
 
 

time: 586 us -> 367 us (0.63)
  matrix products: 159 us -> 0 us
  Pallas kernels: 108 us -> 200 us
  waiting for transfers between devices: 142 us -> 91.9 us
  blocking collectives: 39.4 us -> 0 us
  other arithmetic: 47.4 us -> 8.53 us
  local copies, waits for them, and re-layouts: 48.3 us -> 15.3 us
  starting transfers between devices: 19.2 us -> 32.5 us
    dot_general x12 -> x0, matrix products: 159 us -> none  [the longest x4 70.5 us: matmul(): return jnp.dot(left, right, preferred_element_type=jnp.float32)]
    reduce_scatter x4 -> x1, waiting for transfers between devices: 98.3 us -> 0.01 us  [per_device(): lax.psum_scatter(packed.reshape(members, 2 * own, width), group, scatter_...]
    pallas_call x0 -> x4, Pallas kernels: none -> 80.2 us  [the longest x1 63.5 us: feed_forward(): pl.pallas_call(feed_forward_kernel, grid=(steps,), in_specs=[fixed(tokens...]
    unnamed x1 -> x0, blocking collectives: 27.4 us -> none
    pallas_call x1, Pallas kernels: 59.1 us -> 84.1 us  [attention_backward(): pl.pallas_call(attention_backward_kernel, grid=(pairs,), in_specs=[block]...]
    all_to_all x0 -> x2, waiting for transfers between devices: none -> 22.3 us  [the longest x1 22.3 us: per_device(): arrived = lax.all_to_all(joint_half, 'tm', 0, 0, tiled=True)]
    psum x1, waiting for transfers between devices: 10.7 us -> 32.8 us  [per_device(): mlp_sum, outp_sum = lax.psum((mlp_rows, outp_rows), 'dp')]
    reduce_sum x9 -> x2, other arithmetic: 21.7 us -> 2.55 us  [the longest x1 2.24 us: per_device(): outp_rows = jnp.sum(moved[:, padded:].astype(F32), axis=0).astype(BF16)]
  transfers between devices with their start and end apart: 9 -> 14, of which waited for: 5 -> 7; matrix products, arithmetic and copies ran while one was open for 32% -> 5% of each run, Pallas kernels for 19% -> 38%
where the time goes in v2:
time: 367 us; the launch traced here: 363 us
  Pallas kernels  200 us (54%)
  waiting for transfers between devices  91.9 us (25%)
  starting transfers between devices  32.5 us (9%)
  local copies, waits for them, and re-layouts  15.3 us (4%)
  between operations  14.5 us (4%)
  other arithmetic  8.53 us (2%)
    pallas_call x1, Pallas kernels, attention_backward(): pl.pallas_call(attention_backward_kernel, grid=(pairs,), in_specs=[block]...  84.1 us
    pallas_call x1, Pallas kernels, feed_forward(): pl.pallas_call(feed_forward_kernel, grid=(steps,), in_specs=[fixed(tokens...  63.5 us
    pallas_call x1, Pallas kernels, attention_forward(): pl.pallas_call(attention_forward_kernel, grid=(pairs,), in_specs=[block,...  35.6 us
    psum x1, waiting for transfers between devices, per_device(): mlp_sum, outp_sum = lax.psum((mlp_rows, outp_rows), 'dp')  32.8 us
    all_to_all x2, waiting for transfers between devices, to_clip(): lax.all_to_all(blocks, group, 0, 0, tiled=True).reshape(tokens, width)  22.5 us
    all_to_all x1, waiting for transfers between devices, per_device(): arrived = lax.all_to_all(joint_half, 'tm', 0, 0, tiled=True)  22.3 us
    ppermute x6, waiting for transfers between devices, to_group(): return lax.ppermute(array, 'dp', [(i, i ^ distance) for i in range(groups)])  12.1 us
    pallas_call x1, Pallas kernels, project(): pl.pallas_call(project_kernel, grid=(steps,), in_specs=[block, pl.BlockSp...  11.7 us
  transfers between devices with their start and end apart: 14, of which 7 were waited for; matrix products, arithmetic and copies ran while one was open for 5% of the time, Pallas kernels for 38%

profile of v2, /device:TPU:0, one launch (start us, length us, event | category | flops | bytes accessed | tf_op | source)
XLA Modules:
  0.0 362.7 jit_solution(15190893429817865266)
XLA Ops:
  7.2 1.9 copy.38
  10.6 5.2 %all-to-all-start = ((bf16[8,176,768]{2,1,0:T(8,128)(2,1)}), bf16[8,176,768]{2,1,0:T(8,128)(2,1)S(1)}, u32[]{:S(2)}, u32[]{:S(2)}) async-start(bf16[8,176,768]{2,1,0:T(8,128)(2,1)} %pad.18), calls=%async_computation | async-start | bytes 4325376 | tf_op jit(solution)/shard_map/all_to_all | solution.py:904
  15.8 1.9 copy.37
  20.1 22.5 %all-to-all-done = bf16[8,176,768]{2,1,0:T(8,128)(2,1)S(1)} async-done(((bf16[8,176,768]{2,1,0:T(8,128)(2,1)}), bf16[8,176,768]{2,1,0:T(8,128)(2,1)S(1)}, u32[]{:S(2)}, u32[]{:S(2)}) %all-to-all-start) | async-done | bytes 2162720 | tf_op jit(solution)/shard_map/all_to_all | solution.py:904
  42.6 4.4 %all-to-all-start.1 = ((bf16[8,176,768]{2,1,0:T(8,128)(2,1)}), bf16[8,176,768]{2,1,0:T(8,128)(2,1)}, u32[]{:S(2)}, u32[]{:S(2)}) async-start(bf16[8,176,768]{2,1,0:T(8,128)(2,1)} %pad.21), calls=%async_computation.1 | async-start | bytes 4325376 | tf_op jit(solution)/shard_map/all_to_all | solution.py:904
  48.8 11.7 %shard_map.203 = (bf16[1408,768]{1,0:T(8,128)(2,1)}, bf16[1408,768]{1,0:T(8,128)(2,1)}, bf16[1408,768]{1,0:T(8,128)(2,1)}, bf16[1408,768]{1,0:T(8,128)(2,1)}) custom-call(bf16[1408,768]{1,0:T(8,128)(2,1)} %bitcast.33, f32[1408,128]{1,0:T(8,128)} %broadcast_in_dim.20.live_ref.keep_ref, bf16[768,2304]{1,0:T(8,128)(2,1)} %wv_ref.1, f32[8,768]{1,0:T(8,128)} %fusion.11.vec_ref), custom_call_target="tpu_custom_call" | custom-call | flops 4982833152 | bytes 10813440 | tf_op jit(solution)/shard_map/pallas_call | solution.py:394
  61.2 35.6 %shard_map.204 = (bf16[1408,768]{1,0:T(8,128)(2,1)}, f32[1408,768]{1,0:T(8,128)}, bf16[6,1408,2816]{2,1,0:T(8,128)(2,1)}) custom-call(bf16[1408,768]{1,0:T(8,128)(2,1)} %get-tuple-element.47.q_ref, bf16[1408,768]{1,0:T(8,128)(2,1)} %get-tuple-element.48.k_ref, bf16[1408,768]{1,0:T(8,128)(2,1)} %get-tuple-element.49.v_ref, f32[8,1408]{1,0:T(8,128)} %broadcast_in_dim.21.live_ref), custom_call_target="tpu_custom_call" | custom-call | flops 12180258816 | bytes 47579136 | tf_op jit(solution)/shard_map/pallas_call | solution.py:469
  97.5 63.5 %shard_map.205 = (bf16[8,288,768]{2,1,0:T(8,128)(2,1)}, bf16[1408,768]{1,0:T(8,128)(2,1)}, bf16[1408,768]{1,0:T(8,128)(2,1)}, bf16[8,8,96,768]{3,2,1,0:T(8,128)(2,1)}, f32[8,768]{1,0:T(8,128)}) custom-call(bf16[1408,768]{1,0:T(8,128)(2,1)} %bitcast.34, bf16[1408,768]{1,0:T(8,128)(2,1)} %get-tuple-element.50.mixed_ref.o_ref, ...), custom_call_target="tpu_custom_call" | custom-call | flops 44845498368 | bytes 31850496 | tf_op jit(solution)/shard_map/pallas_call | solution.py:756
  161.0 4.5 %all-to-all-start.2 = ((bf16[8,288,768]{2,1,0:T(8,128)(2,1)}), bf16[8,288,768]{2,1,0:T(8,128)(2,1)}, u32[]{:S(2)}, u32[]{:S(2)}) async-start(bf16[8,288,768]{2,1,0:T(8,128)(2,1)} %get-tuple-element.59), calls=%async_computation.2 | async-start | bytes 7077888 | tf_op jit(solution)/shard_map/all_to_all | solution.py:941
  165.5 84.1 %shard_map.206 = (bf16[384,2432]{1,0:T(8,128)(2,1)}, bf16[384,2432]{1,0:T(8,128)(2,1)}, bf16[1408,768]{1,0:T(8,128)(2,1)}) custom-call(bf16[1408,768]{1,0:T(8,128)(2,1)} %get-tuple-element.47.q_ref, bf16[1408,768]{1,0:T(8,128)(2,1)} %get-tuple-element.48.k_ref, bf16[1408,768]{1,0:T(8,128)(2,1)} %get-tuple-element.49.v_ref, ...), custom_call_target="tpu_custom_call" | custom-call | flops 24360517632 | bytes 47579136 | tf_op jit(solution)/shard_map/pallas_call | solution.py:590
  250.3 2.2 slice_reduce_fusion
  254.0 3.3 add_convert_fusion
  257.2 4.0 %all-to-all-start.3 = ((bf16[4,96,2432]{2,1,0:T(8,128)(2,1)}), bf16[4,96,2432]{2,1,0:T(8,128)(2,1)S(1)}, u32[]{:S(2)}, u32[]{:S(2)}) async-start(bf16[4,96,2432]{2,1,0:T(8,128)(2,1)} %bitcast.31), calls=%async_computation.4 | async-start | bytes 3735552 | tf_op jit(solution)/shard_map/all_to_all | solution.py:955
  262.0 22.3 %all-to-all-done.3 = bf16[4,96,2432]{2,1,0:T(8,128)(2,1)S(1)} async-done(((bf16[4,96,2432]{2,1,0:T(8,128)(2,1)}), bf16[4,96,2432]{2,1,0:T(8,128)(2,1)S(1)}, u32[]{:S(2)}, u32[]{:S(2)}) %all-to-all-start.3) | async-done | bytes 1867808 | tf_op jit(solution)/shard_map/all_to_all | solution.py:955
  286.2 2.6 collective-permute-start.2
  289.1 3.6 all-to-all-start.4
  292.7 5.7 %collective-permute-done.1 = bf16[24,2432]{1,0:T(8,128)(2,1)S(1)} collective-permute-done((bf16[24,2432]{1,0:T(8,128)(2,1)S(1)}, bf16[24,2432]{1,0:T(8,128)(2,1)S(1)}, u32[]{:S(2)}, u32[]{:S(2)}) %collective-permute-start.1) | collective-permute-done | bytes 116768 | tf_op jit(solution)/shard_map/ppermute | solution.py:960
  298.4 4.3 %collective-permute-done.2 = bf16[24,2432]{1,0:T(8,128)(2,1)S(1)} collective-permute-done((bf16[24,2432]{1,0:T(8,128)(2,1)S(1)}, bf16[24,2432]{1,0:T(8,128)(2,1)S(1)}, u32[]{:S(2)}, u32[]{:S(2)}) %collective-permute-start.2) | collective-permute-done | bytes 116768 | tf_op jit(solution)/shard_map/ppermute | solution.py:960
  302.7 2.1 collective-permute-done.3
  304.9 3.3 collective-permute-start.4
  311.6 2.4 collective-permute-start.6
  314.0 32.8 %all-reduce.7.cloned.1.call-done = (bf16[768,768]{1,0:T(8,128)(2,1)}, bf16[112,768]{1,0:T(8,128)(2,1)}) async-done(((bf16[768,768]{1,0:T(8,128)(2,1)}, bf16[112,768]{1,0:T(8,128)(2,1)}), (bf16[768,768]{1,0:T(8,128)(2,1)}, bf16[112,768]{1,0:T(8,128)(2,1)})) %all-reduce.7.cloned.1.call-update) | async-done | bytes 1351696 | tf_op jit(solution)/shard_map/psum | solution.py:954
  346.9 2.9 shard_map.208
  351.7 2.1 shard_map.207
  (57 shorter events, 19.1 us)
Async XLA Ops:
  10.6 32.0 %all-to-all-start = ((bf16[8,176,768]{2,1,0:T(8,128)(2,1)}), bf16[8,176,768]{2,1,0:T(8,128)(2,1)S(1)}, u32[]{:S(2)}, u32[]{:S(2)}) async-start(bf16[8,176,768]{2,1,0:T(8,128)(2,1)} %pad.18), calls=%async_computation | async-start | bytes 4325376 | tf_op jit(solution)/shard_map/all_to_all | solution.py:904
  17.8 1.6 copy-start.5
  17.8 1.6 copy-start.6
  17.8 1.6 copy-start.8
  17.8 2.2 copy-start.10
  20.1 26.9 %copy-start.9 = (bf16[2,768]{1,0:T(2,128)(2,1)S(1)}, bf16[2,768]{1,0:T(2,128)(2,1)}, u32[]{:S(2)}) copy-start(bf16[2,768]{1,0:T(2,128)(2,1)} %param.22) | copy-start | bytes 9220
  42.6 4.4 %copy-start = (bf16[8,176,768]{2,1,0:T(8,128)(2,1)}, bf16[8,176,768]{2,1,0:T(8,128)(2,1)S(1)}, u32[]{:S(2)}) copy-start(bf16[8,176,768]{2,1,0:T(8,128)(2,1)S(1)} %all-to-all-done) | copy-start | bytes 6488068
  42.6 54.2 %all-to-all-start.1 = ((bf16[8,176,768]{2,1,0:T(8,128)(2,1)}), bf16[8,176,768]{2,1,0:T(8,128)(2,1)}, u32[]{:S(2)}, u32[]{:S(2)}) async-start(bf16[8,176,768]{2,1,0:T(8,128)(2,1)} %pad.21), calls=%async_computation.1 | async-start | bytes 4325376 | tf_op jit(solution)/shard_map/all_to_all | solution.py:904
  47.0 210.2 %reduce-scatter.2.cloned.1.call-start = ((), (), s32[]{:S(2)}) async-start(), calls=%async_computation.6 | async-start | bytes 10616832 | tf_op jit(solution)/shard_map/reduce_scatter | solution.py:940
  61.2 35.6 %copy-start.7 = (bf16[3072]{0:T(1024)(128)(2,1)S(1)}, bf16[3072]{0:T(1024)(128)(2,1)}, u32[]{:S(2)}) copy-start(bf16[3072]{0:T(1024)(128)(2,1)} %param.20) | copy-start | bytes 18436
  161.0 88.6 %all-to-all-start.2 = ((bf16[8,288,768]{2,1,0:T(8,128)(2,1)}), bf16[8,288,768]{2,1,0:T(8,128)(2,1)}, u32[]{:S(2)}, u32[]{:S(2)}) async-start(bf16[8,288,768]{2,1,0:T(8,128)(2,1)} %get-tuple-element.59), calls=%async_computation.2 | async-start | bytes 7077888 | tf_op jit(solution)/shard_map/all_to_all | solution.py:941
  249.7 4.3 %collective-permute-start = (bf16[384,2432]{1,0:T(8,128)(2,1)}, bf16[384,2432]{1,0:T(8,128)(2,1)S(1)}, u32[]{:S(2)}, u32[]{:S(2)}) collective-permute-start(bf16[384,2432]{1,0:T(8,128)(2,1)} %get-tuple-element.61), channel_id=1, source_target_pairs={{0,4},{4,0},{1,5},{5,1},{2,6},{6,2},{3,7},{7,3},{8,12},{12,8},{9,1... | collective-permute-start | bytes 5603336 | tf_op jit(solution)/shard_map/ppermute | solution.py:950
  257.2 27.1 %all-to-all-start.3 = ((bf16[4,96,2432]{2,1,0:T(8,128)(2,1)}), bf16[4,96,2432]{2,1,0:T(8,128)(2,1)S(1)}, u32[]{:S(2)}, u32[]{:S(2)}) async-start(bf16[4,96,2432]{2,1,0:T(8,128)(2,1)} %bitcast.31), calls=%async_computation.4 | async-start | bytes 3735552 | tf_op jit(solution)/shard_map/all_to_all | solution.py:955
  261.3 85.6 %all-reduce.7.cloned.1.call-start = ((), (), s32[]{:S(2)}) async-start(), calls=%async_computation.7 | async-start | bytes 2703360 | tf_op jit(solution)/shard_map/psum | solution.py:954
  284.6 13.7 %collective-permute-start.1 = (bf16[24,2432]{1,0:T(8,128)(2,1)S(1)}, bf16[24,2432]{1,0:T(8,128)(2,1)S(1)}, u32[]{:S(2)}, u32[]{:S(2)}) collective-permute-start(bf16[24,2432]{1,0:T(8,128)(2,1)S(1)} %get-tuple-element.118), channel_id=1, source_target_pairs={{0,8},{8,0},{16,24},{24,16},{1,9},{9,1},{17,25},{25,17},{2,10},{10... | collective-permute-start | bytes 350216 | tf_op jit(solution)/shard_map/ppermute | solution.py:960
  286.2 16.5 %collective-permute-start.2 = (bf16[24,2432]{1,0:T(8,128)(2,1)S(1)}, bf16[24,2432]{1,0:T(8,128)(2,1)S(1)}, u32[]{:S(2)}, u32[]{:S(2)}) collective-permute-start(bf16[24,2432]{1,0:T(8,128)(2,1)S(1)} %get-tuple-element.120), channel_id=1, source_target_pairs={{0,16},{8,24},{16,0},{24,8},{1,17},{9,25},{17,1},{25,9},{2,18},{10... | collective-permute-start | bytes 350216 | tf_op jit(solution)/shard_map/ppermute | solution.py:960
  288.8 16.0 %collective-permute-start.3 = (bf16[24,2432]{1,0:T(8,128)(2,1)S(1)}, bf16[24,2432]{1,0:T(8,128)(2,1)S(1)}, u32[]{:S(2)}, u32[]{:S(2)}) collective-permute-start(bf16[24,2432]{1,0:T(8,128)(2,1)S(1)} %get-tuple-element.119), channel_id=1, source_target_pairs={{0,24},{8,16},{16,8},{24,0},{1,25},{9,17},{17,9},{25,1},{2,26},{10... | collective-permute-start | bytes 350216 | tf_op jit(solution)/shard_map/ppermute | solution.py:960
  289.1 64.7 %all-to-all-start.4 = ((bf16[8,176,768]{2,1,0:T(8,128)(2,1)}), bf16[8,176,768]{2,1,0:T(8,128)(2,1)S(1)}, u32[]{:S(2)}, u32[]{:S(2)}) async-start(bf16[8,176,768]{2,1,0:T(8,128)(2,1)} %bitcast.32), calls=%async_computation.5 | async-start | bytes 4325376 | tf_op jit(solution)/shard_map/all_to_all | solution.py:907
  304.9 6.7 %copy-start.1 = (bf16[24,2432]{1,0:T(8,128)(2,1)}, bf16[24,2432]{1,0:T(8,128)(2,1)S(1)}, u32[]{:S(2)}) copy-start(bf16[24,2432]{1,0:T(8,128)(2,1)S(1)} %fusion.2.refs_0_) | copy-start | bytes 350212
  304.9 41.9 %collective-permute-start.4 = (bf16[24,2432]{1,0:T(8,128)(2,1)S(1)}, bf16[24,2432]{1,0:T(8,128)(2,1)S(1)}, u32[]{:S(2)}, u32[]{:S(2)}) collective-permute-start(bf16[24,2432]{1,0:T(8,128)(2,1)S(1)} %fusion.2.refs_0_), channel_id=1, source_target_pairs={{0,8},{8,0},{16,24},{24,16},{1,9},{9,1},{17,25},{25,17},{2,10},{10... | collective-permute-start | bytes 350216 | tf_op jit(solution)/shard_map/ppermute | solution.py:960
  311.6 39.4 %collective-permute-start.5 = (bf16[24,2432]{1,0:T(8,128)(2,1)S(1)}, bf16[24,2432]{1,0:T(8,128)(2,1)S(1)}, u32[]{:S(2)}, u32[]{:S(2)}) collective-permute-start(bf16[24,2432]{1,0:T(8,128)(2,1)S(1)} %fusion.2.refs_0_), channel_id=1, source_target_pairs={{0,16},{8,24},{16,0},{24,8},{1,17},{9,25},{17,1},{25,9},{2,18},{10... | collective-permute-start | bytes 350216 | tf_op jit(solution)/shard_map/ppermute | solution.py:960
  311.6 39.4 %collective-permute-start.6 = (bf16[24,2432]{1,0:T(8,128)(2,1)S(1)}, bf16[24,2432]{1,0:T(8,128)(2,1)S(1)}, u32[]{:S(2)}, u32[]{:S(2)}) collective-permute-start(bf16[24,2432]{1,0:T(8,128)(2,1)S(1)} %fusion.2.refs_0_), channel_id=1, source_target_pairs={{0,24},{8,16},{16,8},{24,0},{1,25},{9,17},{17,9},{25,1},{2,26},{10... | collective-permute-start | bytes 350216 | tf_op jit(solution)/shard_map/ppermute | solution.py:960
  346.8 2.9 copy-start.2
  351.0 0.7 copy-start.4
  (1 other events, 0.6 us)
Sparse Core Ops, SparseCore 0:
  161.1 94.1 reduce-scatter.1
  265.1 81.6 all-reduce.6

commit v3 on v2

--- a/solution.py
+++ b/solution.py
@@ -351,7 +351,10 @@
 BF16 = jnp.bfloat16
 VMEM_LIMIT = 62 << 20
 SAFE_RANGE = 100.0
-COLLECT_FLOPS = 40 * 10**9
+CHUNKS = 4
+HALVES = 2
+SPAN = 1024
+COLLECT_FLOPS = 30 * 10**9
 
 
 def normalize(values):
@@ -367,13 +370,26 @@
     return (scaled - mean - normed * slope) * inverse
 
 
+def spans_of(tokens):
+    return [slice(at, min(at + SPAN, 2 * tokens)) for at in range(0, 2 * tokens, SPAN)]
+
+
 def column_sum(values):
     return jnp.sum(values, axis=0, keepdims=True)
 
 
-def project_kernel(x_ref, live_ref, w_ref, vec_ref, n_ref, q_ref, k_ref, v_ref, first_key):
-    width = x_ref.shape[1]
-    normed, _ = normalize(x_ref[...].astype(F32))
+def project_kernel(x_ref, live_ref, w_ref, vec_ref, rows_ref, n_ref, q_ref, k_ref, v_ref, first_key, rows):
+    blocks, slots, width = x_ref.shape
+    padded = rows.shape[0] // blocks
+
+    @pl.when(pl.program_id(0) == 0)
+    def _():
+        rows[...] = jnp.zeros_like(rows)
+
+    for block in range(blocks):
+        rows[block * padded : block * padded + slots] = x_ref[block].astype(F32)
+    rows_ref[...] = rows[...].astype(BF16)
+    normed, _ = normalize(rows[...])
     low = (normed * vec_ref[0:1, :] + vec_ref[1:2, :]).astype(BF16)
     n_ref[...] = low
     q_ref[...] = (matmul(low, w_ref[:, 0:width]) + vec_ref[2:3, :]).astype(BF16)
@@ -387,31 +403,48 @@
     v_ref[...] = (matmul(low, w_ref[:, 2 * width : 3 * width]) + vec_ref[3:4, :]).astype(BF16)
 
 
-def project(inputs, live_lanes, joint_proj, vectors, steps=4):
-    tokens, width = inputs.shape
+def project(blocks, live_lanes, joint_proj, vectors, steps=4):
+    members, slots, width = blocks.shape
+    tokens = live_lanes.shape[0]
     rows = tokens // steps
     block = pl.BlockSpec((rows, width), lambda step: (step, 0))
     return pl.pallas_call(
         project_kernel,
         grid=(steps,),
         in_specs=[
-            block,
+            pl.BlockSpec((members // steps, slots, width), lambda step: (step, 0, 0)),
             pl.BlockSpec((rows, LANES), lambda step: (step, 0)),
             pl.BlockSpec((width, 3 * width), lambda step: (0, 0), pipeline_mode=pl.Buffered(1)),
             pl.BlockSpec((8, width), lambda step: (0, 0)),
         ],
-        out_specs=[block] * 4,
-        out_shape=[jax.ShapeDtypeStruct((tokens, width), BF16)] * 4,
-        scratch_shapes=[pltpu.VMEM((8, width), F32)],
+        out_specs=[block] * 5,
+        out_shape=[jax.ShapeDtypeStruct((tokens, width), BF16)] * 5,
+        scratch_shapes=[pltpu.VMEM((8, width), F32), pltpu.VMEM((rows, width), F32)],
         compiler_params=pltpu.CompilerParams(vmem_limit_bytes=VMEM_LIMIT),
         cost_estimate=pl.CostEstimate(
             flops=6 * tokens * width * width, transcendentals=tokens, bytes_accessed=10 * tokens * width
         ),
-    )(inputs, live_lanes, joint_proj, vectors)
-
-
-def attention_forward_kernel(q_ref, k_ref, v_ref, live_ref, o_ref, rn_ref, p_ref, qs, vt, ot, sa):
+    )(blocks, live_lanes, joint_proj, vectors)
+
+
+def attention_forward_kernel(q_ref, k_ref, v_ref, live_ref, o_ref, rn_ref, p_ref, qs, vt, ot, sa, p_buf, p_sem):
     tokens = q_ref.shape[0]
+    pair = pl.program_id(0)
+    slot = lax.rem(pair, 2)
+    spans = spans_of(tokens)
+
+    def copy_of(pair, slot, index):
+        span = spans[index]
+        columns = pl.ds(span.start, span.stop - span.start)
+        return pltpu.make_async_copy(
+            p_buf.at[slot, :, columns], p_ref.at[pair, :, columns], p_sem.at[slot, index]
+        )
+
+    @pl.when(pair >= 2)
+    def _():
+        for index in range(len(spans)):
+            copy_of(pair - 2, slot, index).wait()
+
     lane = lax.broadcasted_iota(jnp.int32, (tokens, LANES), 1)
     query = q_ref[...].astype(F32) * (1.0 / math.sqrt(DH))
     keys = k_ref[...].astype(F32)
@@ -432,24 +465,25 @@
     bounded = bound <= limit
 
     def finish(span, weight):
-        p_ref[0, :, span] = weight
+        p_buf[slot, :, span] = weight
         ot[:, span] = matmul(vt[...], weight)
 
     @pl.when(bounded)
     def _():
-        for head in range(2):
-            span = slice(head * tokens, (head + 1) * tokens)
+        for index, span in enumerate(spans):
             finish(span, jnp.exp2(matmul_nt(k_ref[...], qs[span, :]) * LOG2E).astype(BF16))
+            copy_of(pair, slot, index).start()
 
     @pl.when(jnp.logical_not(bounded))
     def _():
-        for head in range(2):
-            for start in range(0, tokens, sa.shape[1]):
-                span = slice(head * tokens + start, head * tokens + start + sa.shape[1])
-                sa[...] = matmul_nt(k_ref[...], qs[span, :])
+        for index, span in enumerate(spans):
+            for start in range(span.start, span.stop, LANES):
+                part = slice(start, start + LANES)
+                sa[...] = matmul_nt(k_ref[...], qs[part, :])
                 score = sa[...]
                 highest = jnp.max(score, axis=0, keepdims=True)
-                finish(span, jnp.exp2(score * LOG2E - highest * LOG2E).astype(BF16))
+                finish(part, jnp.exp2(score * LOG2E - highest * LOG2E).astype(BF16))
+            copy_of(pair, slot, index).start()
 
     row = lax.broadcasted_iota(jnp.int32, (LANES, tokens), 0)
     inverse = jnp.where(
@@ -460,6 +494,13 @@
     mixed = jnp.where(row < DH, ot[0:LANES, 0:tokens], ot[0:LANES, tokens : 2 * tokens]) * inverse
     o_ref[...] = jnp.transpose(mixed).astype(BF16)
     rn_ref[...] = jnp.transpose(inverse)
+
+    @pl.when(pair == pl.num_programs(0) - 1)
+    def _():
+        for index in range(len(spans)):
+            copy_of(pair - 1, 1 - slot, index).wait()
+        for index in range(len(spans)):
+            copy_of(pair, slot, index).wait()
 
 
 def attention_forward(query, keys, memory, live_row):
@@ -470,7 +511,7 @@
         attention_forward_kernel,
         grid=(pairs,),
         in_specs=[block, block, block, pl.BlockSpec((8, tokens), lambda pair: (0, 0))],
-        out_specs=[block, block, pl.BlockSpec((1, tokens, 2 * tokens), lambda pair: (pair, 0, 0))],
+        out_specs=[block, block, pl.BlockSpec(memory_space=pl.ANY)],
         out_shape=[
             jax.ShapeDtypeStruct((tokens, width), BF16),
             jax.ShapeDtypeStruct((tokens, width), F32),
@@ -481,6 +522,8 @@
             pltpu.VMEM((LANES + 16, tokens), BF16),
             pltpu.VMEM((LANES + 16, 2 * tokens), F32),
             pltpu.VMEM((tokens, LANES), F32),
+            pltpu.VMEM((2, tokens, 2 * tokens), BF16),
+            pltpu.SemaphoreType.DMA((2, len(spans_of(tokens)))),
         ],
         compiler_params=pltpu.CompilerParams(vmem_limit_bytes=VMEM_LIMIT),
         cost_estimate=pl.CostEstimate(
@@ -492,11 +535,25 @@
 
 
 def attention_backward_kernel(
-    q_ref, k_ref, v_ref, o_ref, do_ref, rn_ref, live_ref, keep_ref, p_ref, n_ref, wq_ref, wk_ref, wv_ref,
-    x_ref, res_ref, vec_ref, sums_ref, half_ref,
-    kept_ref, sent_ref, dx_ref, qs, gs, kt, dqt, delta, dj, dn, vecs,
+    q_ref, k_ref, v_ref, o_ref, do_ref, rn_ref, live_ref, keep_ref, p_ref, n_ref, w_ref,
+    x_ref, res_ref, vec_ref, sums_ref, half_ref, out_ref,
+    kept_ref, sent_ref, rows_ref, qs, gs, kt, dqt, delta, dj, vecs, n_buf, w_buf, x_buf, res_buf, dx_buf, sem, dx_sem,
 ):
     tokens = q_ref.shape[0]
+    pair = pl.program_id(0)
+
+    late = [
+        pltpu.make_async_copy(source, target, sem.at[index])
+        for index, (source, target) in enumerate(
+            ((n_ref, n_buf), (w_ref, w_buf), (x_ref, x_buf), (res_ref, res_buf))
+        )
+    ]
+
+    @pl.when(pair == 0)
+    def _():
+        for copy in late:
+            copy.start()
+
     scale = 1.0 / math.sqrt(DH)
     lane = lax.broadcasted_iota(jnp.int32, (tokens, LANES), 1)
     query = q_ref[...].astype(F32) * scale
@@ -511,8 +568,7 @@
         total = column_sum(product[head * DH : (head + 1) * DH])
         delta[:, head * tokens : (head + 1) * tokens] = jnp.broadcast_to(total, (8, tokens))
     grad_keys = grad_values = None
-    for head in range(2):
-        span = slice(head * tokens, (head + 1) * tokens)
+    for span in spans_of(tokens):
         weight = p_ref[0, :, span]
         grad_weight = matmul_nt(v_ref[...], gs[span, :])
         grad_score = (weight.astype(F32) * (grad_weight - delta[0:1, span])).astype(BF16)
@@ -524,68 +580,75 @@
     row = lax.broadcasted_iota(jnp.int32, (LANES, tokens), 0)
     grad_query = jnp.transpose(jnp.where(row < DH, dqt[:, 0:tokens], dqt[:, tokens : 2 * tokens]))
     keep = keep_ref[...] > 0
-    dj[:, 0:LANES] = grad_query.astype(BF16)
-    dj[:, LANES : 2 * LANES] = jnp.where(keep, grad_keys, 0.0).astype(BF16)
-    dj[:, 2 * LANES : 3 * LANES] = jnp.where(keep, grad_values, 0.0).astype(BF16)
-    joint = dj[...]
-    grad_weights = matmul_tn(n_ref[...], joint).astype(BF16)
-    half = grad_weights.shape[0] // 2
-    first = half_ref[0] == 0
-    columns = pl.ds(pl.multiple_of(pl.program_id(0) * (3 * LANES), LANES), 3 * LANES)
-    kept_ref[:, columns] = jnp.where(first, grad_weights[:half], grad_weights[half:])
-    sent_ref[:, columns] = jnp.where(first, grad_weights[half:], grad_weights[:half])
-    sums = column_sum(joint.astype(F32))
-    columns = pl.ds(pl.multiple_of(pl.program_id(0) * LANES, LANES), LANES)
-    vecs[2:3, columns] = sums[:, 0:LANES]
-    vecs[3:4, columns] = sums[:, 2 * LANES : 3 * LANES]
-    weights = jnp.concatenate([wq_ref[...], wk_ref[...], wv_ref[...]], axis=1)
-    grad_normed = matmul_nt(joint, weights)
-
-    @pl.when(pl.program_id(0) == 0)
-    def _():
-        dn[...] = grad_normed
-
-    @pl.when(pl.program_id(0) > 0)
-    def _():
-        dn[...] += grad_normed
+    width = x_buf.shape[1]
+    parts = (
+        grad_query.astype(BF16),
+        jnp.where(keep, grad_keys, 0.0).astype(BF16),
+        jnp.where(keep, grad_values, 0.0).astype(BF16),
+    )
+    for part, value in enumerate(parts):
+        columns = pl.ds(pl.multiple_of(part * width + pl.program_id(0) * LANES, LANES), LANES)
+        dj[:, columns] = value
+        if part != 1:
+            columns = pl.ds(pl.multiple_of(pl.program_id(0) * LANES, LANES), LANES)
+            vecs[2 + part // 2 : 3 + part // 2, columns] = column_sum(value.astype(F32))
 
     @pl.when(pl.program_id(0) == pl.num_programs(0) - 1)
     def _():
-        vecs[0:2, :] = jnp.zeros((2, vecs.shape[1]), F32)
+        for copy in late:
+            copy.wait()
+        first = half_ref[0] == 0
+        half = width // 2
+        for part in range(3):
+            span = slice(part * width, (part + 1) * width)
+            grad_weights = matmul_tn(n_buf[...], dj[:, span]).astype(BF16)
+            kept_ref[:, span] = jnp.where(first, grad_weights[:half], grad_weights[half:])
+            sent_ref[:, span] = jnp.where(first, grad_weights[half:], grad_weights[:half])
         vecs[4:8, :] = sums_ref[0:4, :]
-        rows = 2 * LANES if tokens % (2 * LANES) == 0 else LANES
-
-        def chunk(index, _):
-            span = pl.ds(pl.multiple_of(index * rows, rows), rows)
-            normed, inverse = normalize(x_ref[span, :].astype(F32))
-            incoming = dn[span, :]
-            vecs[0:1, :] += column_sum(incoming * normed)
-            vecs[1:2, :] += column_sum(incoming)
+        rows = tokens // CHUNKS
+        block = tokens // rows_ref.shape[0]
+        stores = []
+        gain_sum = shift_sum = 0.0
+        for start in range(0, tokens, rows):
+            span = slice(start, start + rows)
+            incoming = matmul_nt(dj[span, :], w_buf[...])
+            normed, inverse = normalize(x_buf[span, :].astype(F32))
+            gain_sum += column_sum(incoming * normed)
+            shift_sum += column_sum(incoming)
             back = norm_back(normed, inverse, incoming, vec_ref[0:1, :])
-            dx_ref[span, :] = (res_ref[span, :].astype(F32) + back).astype(BF16)
-            return 0
-
-        lax.fori_loop(0, tokens // rows, chunk, 0)
+            grad_rows = (res_buf[span, :].astype(F32) + back).astype(BF16)
+            for part in range(rows // block):
+                dx_buf[start // block + part] = grad_rows[part * block : part * block + dx_buf.shape[1]]
+            stores.append(
+                pltpu.make_async_copy(
+                    dx_buf.at[pl.ds(start // block, rows // block)],
+                    rows_ref.at[pl.ds(start // block, rows // block), 0],
+                    dx_sem.at[start // rows],
+                )
+            )
+            stores[-1].start()
+        vecs[0:1, :] = gain_sum
+        vecs[1:2, :] = shift_sum
         turned = jnp.transpose(jnp.concatenate([vecs[...]] * (LANES // 8), axis=0)).astype(BF16)
         tail = kept_ref.shape[1] - LANES
         kept_ref[:, tail:] = jnp.where(first, turned[:half], turned[half:])
         sent_ref[:, tail:] = jnp.where(first, turned[half:], turned[:half])
+        for copy in stores:
+            copy.wait()
 
 
 def attention_backward(
     query, keys, memory, mixed, grad_mixed, inverse, live_row, live_lanes, weights, normed, joint_proj,
-    inputs, residual, vectors, vector_grads, own_half,
+    inputs, residual, vectors, vector_grads, own_half, output,
 ):
     tokens, width = query.shape
     pairs = width // LANES
     block = pl.BlockSpec((tokens, LANES), lambda pair: (0, pair))
     once = pl.Buffered(1)
+    anywhere = pl.BlockSpec(memory_space=pl.ANY)
 
     def fixed(rows, columns):
         return pl.BlockSpec((rows, columns), lambda pair: (0, 0), pipeline_mode=once)
-
-    def columns(part):
-        return pl.BlockSpec((width, LANES), lambda pair: (0, part * pairs + pair))
 
     return pl.pallas_call(
         attention_backward_kernel,
@@ -595,21 +658,20 @@
             fixed(8, tokens),
             fixed(tokens, LANES),
             pl.BlockSpec((1, tokens, 2 * tokens), lambda pair: (pair, 0, 0)),
-            fixed(tokens, width),
-            columns(0),
-            columns(1),
-            columns(2),
-            fixed(tokens, width),
-            fixed(tokens, width),
+            anywhere,
+            anywhere,
+            anywhere,
+            anywhere,
             fixed(8, width),
             fixed(8, width),
             pl.BlockSpec(memory_space=pltpu.SMEM),
+            anywhere,
         ],
-        out_specs=[fixed(width // 2, 3 * width + LANES), fixed(width // 2, 3 * width + LANES), fixed(tokens, width)],
+        out_specs=[fixed(width // 2, 3 * width + LANES), fixed(width // 2, 3 * width + LANES), anywhere],
         out_shape=[
             jax.ShapeDtypeStruct((width // 2, 3 * width + LANES), BF16),
             jax.ShapeDtypeStruct((width // 2, 3 * width + LANES), BF16),
-            jax.ShapeDtypeStruct((tokens, width), BF16),
+            jax.ShapeDtypeStruct(output.shape, BF16),
         ],
         scratch_shapes=[
             pltpu.VMEM((2 * tokens, LANES), BF16),
@@ -617,10 +679,17 @@
             pltpu.VMEM((LANES, tokens), BF16),
             pltpu.VMEM((LANES, 2 * tokens), F32),
             pltpu.VMEM((8, 2 * tokens), F32),
-            pltpu.VMEM((tokens, 3 * LANES), BF16),
-            pltpu.VMEM((tokens, width), F32),
+            pltpu.VMEM((tokens, 3 * width), BF16),
             pltpu.VMEM((8, width), F32),
+            pltpu.VMEM((tokens, width), BF16),
+            pltpu.VMEM((width, 3 * width), BF16),
+            pltpu.VMEM((tokens, width), BF16),
+            pltpu.VMEM((tokens, width), BF16),
+            pltpu.VMEM((output.shape[0],) + output.shape[2:], BF16),
+            pltpu.SemaphoreType.DMA((4,)),
+            pltpu.SemaphoreType.DMA((CHUNKS,)),
         ],
+        input_output_aliases={16: 2},
         compiler_params=pltpu.CompilerParams(vmem_limit_bytes=VMEM_LIMIT),
         cost_estimate=pl.CostEstimate(
             flops=16 * pairs * tokens * tokens * LANES,
@@ -629,27 +698,61 @@
         ),
     )(
         query, keys, memory, mixed, grad_mixed, inverse, live_row, live_lanes, weights, normed,
-        joint_proj, joint_proj, joint_proj, inputs, residual, vectors, vector_grads,
-        own_half,
+        joint_proj, inputs, residual, vectors, vector_grads,
+        own_half, output,
     )
 
 
 def feed_forward_kernel(
-    x_ref, mixed_ref, cot_ref, live_ref, wo_ref, vec_ref, up_ref, down_ref, bias_ref,
-    out_ref, branch_ref, gm_ref, packed_ref, ds_ref,
-    normed, grad_out, middle, acc, acc_grad, hidden, grad_pre, down_buf, up_buf, down_sem, up_sem,
+    x_hbm, mixed_hbm, cot_hbm, live_ref, wo_ref, vec_ref, up_ref, down_ref, bias_ref,
+    out_hbm, share_ref, branch_hbm, gm_hbm, packed_ref, ds_ref,
+    x_ref, mixed_ref, cot_ref, out_ref, branch_ref, gm_ref,
+    normed, grad_out, middle, acc, acc_grad, hidden, grad_pre, down_buf, up_buf, down_sem, up_sem, in_sem, out_sem,
 ):
     step = pl.program_id(0)
     last = pl.num_programs(0) - 1
     tokens, width = x_ref.shape
     units = up_ref.shape[1]
-    rows = tokens // 4
+    rows = tokens // CHUNKS
+
     block = tokens // out_ref.shape[0]
+    slots = out_ref.shape[1]
+    parts = rows // block
+
+    def rows_of_chunk(chunk):
+        return pl.ds(pl.multiple_of(chunk * rows, 32), rows)
+
+    def fetches(chunk):
+        span = rows_of_chunk(chunk)
+        pairs = ((x_hbm, x_ref), (mixed_hbm, mixed_ref), (cot_hbm, cot_ref))
+        return [
+            pltpu.make_async_copy(source.at[span], target.at[span], in_sem.at[chunk, index])
+            for index, (source, target) in enumerate(pairs)
+        ]
+
+    def stores(chunk):
+        span = rows_of_chunk(chunk)
+        return [
+            pltpu.make_async_copy(source.at[span], target.at[span], out_sem.at[chunk, index])
+            for index, (source, target) in enumerate(((branch_ref, branch_hbm), (gm_ref, gm_hbm)))
+        ] + [
+            pltpu.make_async_copy(
+                out_ref.at[pl.ds(chunk * parts, parts)],
+                out_hbm.at[pl.ds(chunk * parts, parts), 1],
+                out_sem.at[chunk, 2],
+            )
+        ]
 
     @pl.when(step == 0)
     def _():
-        def chunk(index, _):
-            span = pl.ds(pl.multiple_of(index * rows, 32), rows)
+        for chunk in range(CHUNKS):
+            for copy in fetches(chunk):
+                copy.start()
+
+        def chunk_step(chunk, _):
+            span = rows_of_chunk(chunk)
+            for copy in fetches(chunk):
+                copy.wait()
             values = x_ref[span, :].astype(F32) + matmul(mixed_ref[span, :], wo_ref[...]) + vec_ref[2:3, :]
             middle[span, :] = values
             acc[span, :] = values + vec_ref[3:4, :]
@@ -659,32 +762,34 @@
             acc_grad[span, :] = jnp.zeros((rows, width), F32)
             return 0
 
-        lax.fori_loop(0, 4, chunk, 0)
+        lax.fori_loop(0, CHUNKS, chunk_step, 0)
 
     up = up_ref[...]
     down = down_ref[...]
-    grad_bias = jnp.zeros((1, units), F32)
-    half = tokens // 2
-    for start in (0, half):
-        span = slice(start, start + half)
+    half = tokens // HALVES
+
+    def feed(index, grad_bias):
+        span = pl.ds(pl.multiple_of(index * half, 32), half)
         pre_act = matmul(normed[span, :], up) + bias_ref[0:1, :]
         grad_hidden = matmul_nt(grad_out[span, :], down)
         cumulative = 0.5 + 0.5 * lax.erf(pre_act * math.sqrt(0.5))
         density = jnp.exp2(pre_act * pre_act * (-0.5 * LOG2E)) * (1.0 / math.sqrt(2.0 * math.pi))
         low = (pre_act * cumulative).astype(BF16)
         grad_low = (grad_hidden * (cumulative + pre_act * density)).astype(BF16)
-        grad_bias = grad_bias + column_sum(grad_low.astype(F32))
         hidden[span, :] = low
         grad_pre[span, :] = grad_low
         acc[span, :] += matmul(low, down)
         acc_grad[span, :] += matmul_nt(grad_low, up)
+        return grad_bias + column_sum(grad_low.astype(F32))
+
+    grad_bias = lax.fori_loop(0, HALVES, feed, jnp.zeros((1, units), F32))
     slot = lax.rem(step, 2)
     _, cuts, quarters, share, _ = down_buf.shape
     own = units // cuts
     for cut in range(cuts):
         sums = jnp.broadcast_to(grad_bias[:, cut * own : (cut + 1) * own], (16, own)).astype(BF16)
-        out_ref[step * cuts + cut, block + share : block + share + 16, 0:own] = sums
-        out_ref[step * cuts + cut, block + share : block + share + 16, own:width] = jnp.zeros((16, width - own), BF16)
+        share_ref[step * cuts + cut, share : share + 16, 0:own] = sums
+        share_ref[step * cuts + cut, share : share + 16, own:width] = jnp.zeros((16, width - own), BF16)
 
     def copies(at, slot):
         return (
@@ -714,34 +819,39 @@
     def _():
         ds_ref[...] = jnp.zeros_like(ds_ref)
 
-        def chunk(index, _):
-            span = pl.ds(pl.multiple_of(index * rows, 32), rows)
+        def chunk_step(chunk, _):
+            span = rows_of_chunk(chunk)
             final = (acc[span, :] * live_ref[span, 0:1]).astype(BF16)
-            for part in range(rows // block):
-                out_ref[index * (rows // block) + part, 0:block, :] = final[part * block : (part + 1) * block]
+            for part in range(parts):
+                out_ref[chunk * parts + part] = final[part * block : part * block + slots]
             unit, inverse = normalize(middle[span, :])
             incoming = acc_grad[span, :]
             start = grad_out[span, :].astype(F32)
             branch = (start + norm_back(unit, inverse, incoming, vec_ref[0:1, :])).astype(BF16)
             branch_ref[span, :] = branch
             gm_ref[span, :] = matmul_nt(branch, wo_ref[...]).astype(BF16)
-            ds_ref[0:1, :] += column_sum(incoming * unit)
-            ds_ref[1:2, :] += column_sum(incoming)
-            ds_ref[2:3, :] += column_sum(branch.astype(F32))
-            ds_ref[3:4, :] += column_sum(start)
+            for copy in stores(chunk):
+                copy.start()
+            for place, term in enumerate((incoming * unit, incoming, branch.astype(F32), start)):
+                ds_ref[place : place + 1, :] += column_sum(term)
             return 0
 
-        lax.fori_loop(0, 4, chunk, 0)
+        lax.fori_loop(0, CHUNKS, chunk_step, 0)
         grad_outp = matmul_tn(mixed_ref[...], branch_ref[...]).astype(BF16)
         for member in range(width // share):
-            out_ref[member, block : block + share, :] = grad_outp[member * share : (member + 1) * share]
+            share_ref[member, 0:share, :] = grad_outp[member * share : (member + 1) * share]
+        for chunk in range(CHUNKS):
+            for copy in stores(chunk):
+                copy.wait()
         for copy in copies(step - 1, 1 - slot):
             copy.wait()
         for copy in copies(step, slot):
             copy.wait()
 
 
-def feed_forward(inputs, mixed, cotangent, live_lanes, out_proj, vectors, up_proj, up_bias, down_proj, members):
+def feed_forward(
+    inputs, mixed, cotangent, live_lanes, out_proj, vectors, up_proj, up_bias, down_proj, members, slots
+):
     tokens, width = inputs.shape
     hidden_units = up_proj.shape[1]
     steps = hidden_units // width
@@ -749,6 +859,7 @@
     cuts = members // steps
     quarters = hidden_units // members // share
     once = pl.Buffered(1)
+    anywhere = pl.BlockSpec(memory_space=pl.ANY)
 
     def fixed(rows, columns):
         return pl.BlockSpec((rows, columns), lambda step: (0, 0), pipeline_mode=once)
@@ -757,9 +868,9 @@
         feed_forward_kernel,
         grid=(steps,),
         in_specs=[
-            fixed(tokens, width),
-            fixed(tokens, width),
-            fixed(tokens, width),
+            anywhere,
+            anywhere,
+            anywhere,
             fixed(tokens, LANES),
             fixed(width, width),
             fixed(8, width),
@@ -768,20 +879,26 @@
             pl.BlockSpec((8, width), lambda step: (0, step)),
         ],
         out_specs=[
-            pl.BlockSpec((members, tokens // members + share + 16, width), lambda step: (0, 0, 0), pipeline_mode=once),
-            fixed(tokens, width),
-            fixed(tokens, width),
-            pl.BlockSpec(memory_space=pl.ANY),
+            anywhere,
+            pl.BlockSpec((members, share + 16, width), lambda step: (0, 0, 0), pipeline_mode=once),
+            anywhere,
+            anywhere,
+            anywhere,
             fixed(8, width),
         ],
         out_shape=[
-            jax.ShapeDtypeStruct((members, tokens // members + share + 16, width), BF16),
+            jax.ShapeDtypeStruct((members, 2, slots, width), BF16),
+            jax.ShapeDtypeStruct((members, share + 16, width), BF16),
             jax.ShapeDtypeStruct((tokens, width), BF16),
             jax.ShapeDtypeStruct((tokens, width), BF16),
             jax.ShapeDtypeStruct((members, quarters + steps, share, width), BF16),
             jax.ShapeDtypeStruct((8, width), F32),
         ],
-        scratch_shapes=[
+        scratch_shapes=[pltpu.VMEM((tokens, width), BF16)] * 3
+        + [
+            pltpu.VMEM((members, slots, width), BF16),
+            pltpu.VMEM((tokens, width), BF16),
+            pltpu.VMEM((tokens, width), BF16),
             pltpu.VMEM((tokens, width), BF16),
             pltpu.VMEM((tokens, width), BF16),
             pltpu.VMEM((tokens, width), F32),
@@ -793,6 +910,8 @@
             pltpu.VMEM((2, members, share, width), BF16),
             pltpu.SemaphoreType.DMA((2,)),
             pltpu.SemaphoreType.DMA((2,)),
+            pltpu.SemaphoreType.DMA((CHUNKS, 3)),
+            pltpu.SemaphoreType.DMA((CHUNKS, 3)),
         ],
         compiler_params=pltpu.CompilerParams(vmem_limit_bytes=VMEM_LIMIT),
         cost_estimate=pl.CostEstimate(
@@ -815,11 +934,7 @@
             piece = jnp.where(own == other, pieces[place ^ other][...], piece)
         piece = piece.astype(F32)
         span = slice(place * rows, (place + 1) * rows)
-        for pair in range(width // LANES):
-            for part in range(3):
-                at = (pair * 3 + part) * LANES
-                to = part * width + pair * LANES
-                joint_ref[span, to : to + LANES] = piece[:, at : at + LANES]
+        joint_ref[span, :] = piece[:, : 3 * width]
         columns[span, :] = piece[:, 3 * width :]
     turned = jnp.transpose(columns[...])
     share = gain_ref.shape[1]
@@ -840,6 +955,7 @@
         out_specs=[vmem] * 5,
         out_shape=[jax.ShapeDtypeStruct((share, 3 * width), F32)] + [jax.ShapeDtypeStruct((2, share), F32)] * 4,
         scratch_shapes=[pltpu.VMEM((LANES, LANES), F32)],
+        cost_estimate=pl.CostEstimate(flops=0, transcendentals=0, bytes_accessed=0),
     )(own, *pieces)
 
 
@@ -851,7 +967,7 @@
         rows = slice(own + part * share, own + (part + 1) * share)
         up_ref[:, part * width : (part + 1) * width] = rows_ref[rows, :].astype(F32)
     outp_ref[...] = sums_ref[0:share, :].astype(F32)
-    bias_ref[...] = sums_ref[share : share + 16, 0:own].astype(F32)[0:1, :]
+    bias_ref[...] = sums_ref[share : share + 16, 0:own].astype(F32)[0]
 
 
 def collect_mlp(rows, sums, share):
@@ -865,7 +981,7 @@
             jax.ShapeDtypeStruct((own, width), F32),
             jax.ShapeDtypeStruct((share, own // share * width), F32),
             jax.ShapeDtypeStruct((share, width), F32),
-            jax.ShapeDtypeStruct((1, own), F32),
+            jax.ShapeDtypeStruct((own,), F32),
         ],
         cost_estimate=pl.CostEstimate(flops=COLLECT_FLOPS, transcendentals=0, bytes_accessed=4 * rows.size),
     )(rows, sums)
@@ -900,12 +1016,7 @@
     hidden_units = up_proj.shape[1]
 
     def to_clip(array):
-        blocks = jnp.pad(jnp.transpose(array, (1, 0, 2)), ((0, 0), (0, padded - slots), (0, 0)))
-        return lax.all_to_all(blocks, group, 0, 0, tiled=True).reshape(tokens, width)
-
-    def to_slots(array):
-        blocks = lax.all_to_all(array.reshape(members, padded, width), group, 0, 0, tiled=True)
-        return jnp.transpose(blocks[:, :slots], (1, 0, 2))
+        return lax.all_to_all(array, group, 0, 0, tiled=True)
 
     token_ids = jnp.arange(tokens, dtype=jnp.int32)
     block_ids = token_ids // padded
@@ -929,12 +1040,14 @@
     vectors2 = rows_of(norm_gain[1], norm_shift[1], out_bias[0], out_bias[1])
     bias_rows = jnp.broadcast_to(up_bias.astype(F32)[None, :], (8, hidden_units))
 
-    inputs = to_clip(patches)
-    cot = to_clip(cotangent)
-    normed1, query, keys, memory = project(inputs, live_lanes, joint_proj, vectors1)
+    turned = jnp.transpose(cotangent, (1, 0, 2))
+    cot = to_clip(jnp.pad(turned, ((0, 0), (0, padded - slots), (0, 0)))).reshape(tokens, width)
+    inputs, normed1, query, keys, memory = project(
+        to_clip(jnp.transpose(patches, (1, 0, 2))), live_lanes, joint_proj, vectors1
+    )
     mixed, inverse, weights = attention_forward(query, keys, memory, live_row)
-    blocks, branch, grad_mixed, packed, vector_grads = feed_forward(
-        inputs, mixed, cot, live_lanes, out_proj, vectors2, up_proj, bias_rows, down_proj, members
+    output, blocks, branch, grad_mixed, packed, vector_grads = feed_forward(
+        inputs, mixed, cot, live_lanes, out_proj, vectors2, up_proj, bias_rows, down_proj, members, padded
     )
     own = hidden_units // members
     mlp_rows = lax.psum_scatter(packed.reshape(members, 2 * own, width), group, scatter_dimension=0, tiled=True)[0]
@@ -942,19 +1055,20 @@
 
     own_half = lax.axis_index("freq")
     own_group = lax.axis_index("dp")
-    kept, sent, grad_tokens = attention_backward(
+    kept, sent, token_rows = attention_backward(
         query, keys, memory, mixed, grad_mixed, inverse, live_row, live_lanes, weights, normed1, joint_proj,
         inputs, branch, vectors1, vector_grads, own_half.reshape(1),
+        output,
     )
     kept, sent, moved = lax.optimization_barrier((kept, sent, moved))
     got = lax.ppermute(sent, "freq", [(0, 1), (1, 0)])
-    outp_rows = jnp.sum(moved[:, padded:].astype(F32), axis=0).astype(BF16)
+    outp_rows = jnp.sum(moved.astype(F32), axis=0).astype(BF16)
     joint_half = (kept.astype(F32) + got.astype(F32)).astype(BF16).reshape(time_size, share, kept.shape[1])
     joint_half, mlp_rows, outp_rows = lax.optimization_barrier((joint_half, mlp_rows, outp_rows))
     mlp_sum, outp_sum = lax.psum((mlp_rows, outp_rows), "dp")
     arrived = lax.all_to_all(joint_half, "tm", 0, 0, tiled=True)
     joint_rows = jnp.sum(arrived.astype(F32), axis=0).astype(BF16)
-    joint_rows, grad_tokens, moved = lax.optimization_barrier((joint_rows, grad_tokens, moved))
+    joint_rows, token_rows = lax.optimization_barrier((joint_rows, token_rows))
 
     def to_group(array, distance):
         return lax.ppermute(array, "dp", [(i, i ^ distance) for i in range(groups)])
@@ -965,12 +1079,12 @@
         piece += to_group(lax.dynamic_index_in_dim(cut, own_group ^ distance, 0, False), distance).astype(F32)
     piece = piece.astype(BF16)
     pieces = [piece] + [to_group(piece, distance) for distance in range(1, groups)]
-    output = jnp.transpose(moved[:, :slots], (1, 0, 2))
-    grad_patches = to_slots(grad_tokens)
-
-    pieces[1], mlp_sum, outp_sum = lax.optimization_barrier((pieces[1], mlp_sum, outp_sum))
+    token_rows = lax.all_to_all(token_rows, group, 0, 0, tiled=True)
+    grad_patches, output = (jnp.transpose(token_rows[:, kind, :slots], (1, 0, 2)) for kind in range(2))
+
+    joint_sum, gain_sum, shift_sum, bias_sum, branch_sum = collect_joint(own_group.reshape(1), pieces, share)
+    joint_sum, mlp_sum, outp_sum = lax.optimization_barrier((joint_sum, mlp_sum, outp_sum))
     down_sum, up_sum, outp_sum, up_bias_sum = collect_mlp(mlp_sum, outp_sum, share)
-    joint_sum, gain_sum, shift_sum, bias_sum, branch_sum = collect_joint(own_group.reshape(1), pieces, share)
     return (
         output,
         grad_patches,
@@ -980,7 +1094,7 @@
         bias_sum,
         outp_sum,
         up_sum,
-        up_bias_sum[0],
+        up_bias_sum,
         down_sum,
         branch_sum,
     )

time: 367 us -> 347 us (0.946)
  Pallas kernels: 200 us -> 184 us
    psum x1, waiting for transfers between devices: 32.8 us -> 14.5 us  [per_device(): mlp_sum, outp_sum = lax.psum((mlp_rows, outp_rows), 'dp')]
    ppermute x6, waiting for transfers between devices: 12.1 us -> 28 us  [to_group(): return lax.ppermute(array, 'dp', [(i, i ^ distance) for i in range(groups)])]
    pallas_call x1, Pallas kernels: 84.1 us -> 70.6 us  [attention_backward(): pl.pallas_call(attention_backward_kernel, grid=(pairs,), in_specs=[block]...]
  transfers between devices with their start and end apart: 14 -> 14, of which waited for: 7 -> 8; matrix products, arithmetic and copies ran while one was open for 5% -> 3% of each run, Pallas kernels for 38% -> 35%
where the time goes in v3:
time: 347 us; the launch traced here: 344 us
  Pallas kernels  184 us (53%)
  waiting for transfers between devices  89.7 us (26%)
  starting transfers between devices  32.5 us (9%)
  local copies, waits for them, and re-layouts  17 us (5%)
  between operations  14.5 us (4%)
  other arithmetic  6.37 us (2%)
    pallas_call x1, Pallas kernels, attention_backward(): pl.pallas_call(attention_backward_kernel, grid=(pairs,), in_specs=[block]...  70.6 us
    pallas_call x1, Pallas kernels, feed_forward(): pl.pallas_call(feed_forward_kernel, grid=(steps,), in_specs=[anywhere, an...  62.5 us
    pallas_call x1, Pallas kernels, attention_forward(): pl.pallas_call(attention_forward_kernel, grid=(pairs,), in_specs=[block,...  33.5 us
    ppermute x6, waiting for transfers between devices, to_group(): return lax.ppermute(array, 'dp', [(i, i ^ distance) for i in range(groups)])  28 us
    all_to_all x1, waiting for transfers between devices, per_device(): arrived = lax.all_to_all(joint_half, 'tm', 0, 0, tiled=True)  22 us
    all_to_all x2, waiting for transfers between devices, to_clip(): return lax.all_to_all(array, group, 0, 0, tiled=True)  21.5 us
    psum x1, waiting for transfers between devices, per_device(): mlp_sum, outp_sum = lax.psum((mlp_rows, outp_rows), 'dp')  14.5 us
    pallas_call x1, Pallas kernels, project(): pl.pallas_call(project_kernel, grid=(steps,), in_specs=[pl.BlockSpec((mem...  12 us
  transfers between devices with their start and end apart: 14, of which 8 were waited for; matrix products, arithmetic and copies ran while one was open for 3% of the time, Pallas kernels for 35%

profile of v3, /device:TPU:0, one launch (start us, length us, event | category | flops | bytes accessed | tf_op | source)
XLA Modules:
  0.0 343.5 jit_solution(3463444669832475736)
XLA Ops:
  7.2 3.3 copy.39
  10.5 5.2 %all-to-all-start = ((bf16[8,164,768]{2,1,0:T(8,128)(2,1)}), bf16[8,164,768]{2,1,0:T(8,128)(2,1)S(1)}, u32[]{:S(2)}, u32[]{:S(2)}) async-start(bf16[8,164,768]{2,1,0:T(8,128)(2,1)} %bitcast.29), calls=%async_computation | async-start | bytes 4128768 | tf_op jit(solution)/shard_map/all_to_all | solution.py:1019
  19.9 21.5 %all-to-all-done.x_ref = bf16[8,164,768]{2,1,0:T(8,128)(2,1)S(1)} async-done(((bf16[8,164,768]{2,1,0:T(8,128)(2,1)}), bf16[8,164,768]{2,1,0:T(8,128)(2,1)S(1)}, u32[]{:S(2)}, u32[]{:S(2)}) %all-to-all-start) | async-done | bytes 2015264 | tf_op jit(solution)/shard_map/all_to_all | solution.py:1019
  42.7 4.4 %all-to-all-start.1 = ((bf16[8,176,768]{2,1,0:T(8,128)(2,1)}), bf16[8,176,768]{2,1,0:T(8,128)(2,1)}, u32[]{:S(2)}, u32[]{:S(2)}) async-start(bf16[8,176,768]{2,1,0:T(8,128)(2,1)} %pad.17), calls=%async_computation.1 | async-start | bytes 4325376 | tf_op jit(solution)/shard_map/all_to_all | solution.py:1019
  48.9 12.0 %shard_map.203 = (bf16[1408,768]{1,0:T(8,128)(2,1)}, bf16[1408,768]{1,0:T(8,128)(2,1)}, bf16[1408,768]{1,0:T(8,128)(2,1)}, bf16[1408,768]{1,0:T(8,128)(2,1)}, bf16[1408,768]{1,0:T(8,128)(2,1)}) custom-call(bf16[8,164,768]{2,1,0:T(8,128)(2,1)} %copy-done, f32[1408,128]{1,0:T(8,128)} %broadcast_in_dim.20.live_ref.keep_ref, bf16[768,2304]{1,0:T(8,128)(2,1)} %w_ref.3, ...), custom_call_target="tpu_custom_call" | custom-call | flops 4982833152 | bytes 10813440 | tf_op jit(solution)/shard_map/pallas_call | solution.py:411
  61.5 33.5 %shard_map.204 = (bf16[1408,768]{1,0:T(8,128)(2,1)}, f32[1408,768]{1,0:T(8,128)}, bf16[6,1408,2816]{2,1,0:T(8,128)(2,1)}) custom-call(bf16[1408,768]{1,0:T(8,128)(2,1)} %get-tuple-element.48.q_ref, bf16[1408,768]{1,0:T(8,128)(2,1)} %get-tuple-element.49.k_ref, bf16[1408,768]{1,0:T(8,128)(2,1)} %get-tuple-element.50.v_ref, f32[8,1408]{1,0:T(8,128)} %broadcast_in_dim.21.live_ref), custom_call_target="tpu_custom_call" | custom-call | flops 12180258816 | bytes 47579136 | tf_op jit(solution)/shard_map/pallas_call | solution.py:510
  95.6 62.5 %shard_map.205 = (bf16[8,2,176,768]{3,2,1,0:T(8,128)(2,1)}, bf16[8,112,768]{2,1,0:T(8,128)(2,1)}, bf16[1408,768]{1,0:T(8,128)(2,1)}, bf16[1408,768]{1,0:T(8,128)...) custom-call(bf16[1408,768]{1,0:T(8,128)(2,1)} %get-tuple-element.52.x_hbm.x_ref, ...), custom_call_target="tpu_custom_call" | custom-call | flops 44845498368 | bytes 31850496 | tf_op jit(solution)/shard_map/pallas_call | solution.py:867
  158.2 4.0 %all-to-all-start.2 = ((bf16[8,112,768]{2,1,0:T(8,128)(2,1)}), bf16[8,112,768]{2,1,0:T(8,128)(2,1)S(1)}, u32[]{:S(2)}, u32[]{:S(2)}) async-start(bf16[8,112,768]{2,1,0:T(8,128)(2,1)} %get-tuple-element.62), calls=%async_computation.2 | async-start | bytes 2752512 | tf_op jit(solution)/shard_map/all_to_all | solution.py:1054
  162.2 70.6 %shard_map.206 = (bf16[384,2432]{1,0:T(8,128)(2,1)}, bf16[384,2432]{1,0:T(8,128)(2,1)}, bf16[8,2,176,768]{3,2,1,0:T(8,128)(2,1)}) custom-call(bf16[1408,768]{1,0:T(8,128)(2,1)} %get-tuple-element.48.q_ref, bf16[1408,768]{1,0:T(8,128)(2,1)} %get-tuple-element.49.k_ref, bf16[1408,768]{1,0:T(8,128)(2,1)} %get-tuple-element.50.v_ref, ...), custom_call_target="tpu_custom_call", output_to_operand_aliasing={{2}: (16, {})} | custom-call | flops 24360517632 | bytes 47579136 | tf_op jit(solution)/shard_map/pallas_call | solution.py:653
  234.6 2.9 collective-permute-done
  237.5 3.7 %add_convert_fusion = bf16[384,2432]{1,0:T(8,128)(2,1)} fusion(bf16[384,2432]{1,0:T(8,128)(2,1)} %collective-permute-done, bf16[384,2432]{1,0:T(8,128)(2,1)} %get-tuple-element.63), kind=kLoop, calls=%fused_computation | loop fusion | flops 3735552 | bytes 5603328 | tf_op jit(solution)/shard_map/convert_element_type | solution.py:1066
  241.3 4.1 %all-to-all-start.3 = ((bf16[4,96,2432]{2,1,0:T(8,128)(2,1)}), bf16[4,96,2432]{2,1,0:T(8,128)(2,1)S(1)}, u32[]{:S(2)}, u32[]{:S(2)}) async-start(bf16[4,96,2432]{2,1,0:T(8,128)(2,1)} %bitcast.32), calls=%async_computation.4 | async-start | bytes 3735552 | tf_op jit(solution)/shard_map/all_to_all | solution.py:1069
  246.1 22.0 %all-to-all-done.3 = bf16[4,96,2432]{2,1,0:T(8,128)(2,1)S(1)} async-done(((bf16[4,96,2432]{2,1,0:T(8,128)(2,1)}), bf16[4,96,2432]{2,1,0:T(8,128)(2,1)S(1)}, u32[]{:S(2)}, u32[]{:S(2)}) %all-to-all-start.3) | async-done | bytes 1867808 | tf_op jit(solution)/shard_map/all_to_all | solution.py:1069
  268.4 4.6 %all-to-all-start.4 = ((bf16[8,2,176,768]{3,2,1,0:T(8,128)(2,1)}), bf16[8,2,176,768]{3,2,1,0:T(8,128)(2,1)}, u32[]{:S(2)}, u32[]{:S(2)}) async-start(bf16[8,2,176,768]{3,2,1,0:T(8,128)(2,1)} %get-tuple-element.69), calls=%async_computation.5 | async-start | bytes 8650752 | tf_op jit(solution)/shard_map/all_to_all | solution.py:1082
  274.7 2.8 collective-permute-start.2
  277.5 8.3 %collective-permute-done.1 = bf16[24,2432]{1,0:T(8,128)(2,1)S(1)} collective-permute-done((bf16[24,2432]{1,0:T(8,128)(2,1)S(1)}, bf16[24,2432]{1,0:T(8,128)(2,1)S(1)}, u32[]{:S(2)}, u32[]{:S(2)}) %collective-permute-start.1) | collective-permute-done | bytes 116768 | tf_op jit(solution)/shard_map/ppermute | solution.py:1074
  285.8 4.1 %collective-permute-done.3 = bf16[24,2432]{1,0:T(8,128)(2,1)S(1)} collective-permute-done((bf16[24,2432]{1,0:T(8,128)(2,1)S(1)}, bf16[24,2432]{1,0:T(8,128)(2,1)S(1)}, u32[]{:S(2)}, u32[]{:S(2)}) %collective-permute-start.3) | collective-permute-done | bytes 116768 | tf_op jit(solution)/shard_map/ppermute | solution.py:1074
  290.0 2.4 collective-permute-start.4
  292.4 2.4 collective-permute-start.6
  294.9 5.2 %collective-permute-done.4.refs_1_ = bf16[24,2432]{1,0:T(8,128)(2,1)S(1)} collective-permute-done((bf16[24,2432]{1,0:T(8,128)(2,1)S(1)}, bf16[24,2432]{1,0:T(8,128)(2,1)S(1)}, u32[]{:S(2)}, u32[]{:S(2)}) %collective-permute-start.4) | collective-permute-done | bytes 116768 | tf_op jit(solution)/shard_map/ppermute | solution.py:1074
  300.1 10.4 %collective-permute-done.5.refs_2_ = bf16[24,2432]{1,0:T(8,128)(2,1)S(1)} collective-permute-done((bf16[24,2432]{1,0:T(8,128)(2,1)S(1)}, bf16[24,2432]{1,0:T(8,128)(2,1)S(1)}, u32[]{:S(2)}, u32[]{:S(2)}) %collective-permute-start.5) | collective-permute-done | bytes 116768 | tf_op jit(solution)/shard_map/ppermute | solution.py:1074
  313.3 14.5 %all-reduce.6.cloned.1.call-done = (bf16[768,768]{1,0:T(8,128)(2,1)}, bf16[112,768]{1,0:T(8,128)(2,1)}) async-done(((bf16[768,768]{1,0:T(8,128)(2,1)}, bf16[112,768]{1,0:T(8,128)(2,1)}), (bf16[768,768]{1,0:T(8,128)(2,1)}, bf16[112,768]{1,0:T(8,128)(2,1)})) %all-reduce.6.cloned.1.call-update) | async-done | bytes 1351696 | tf_op jit(solution)/shard_map/psum | solution.py:1068
  327.8 2.8 shard_map.208
  330.7 2.5 slice_bitcast_fusion
  (54 shorter events, 19.3 us)
Async XLA Ops:
  10.5 30.9 %all-to-all-start = ((bf16[8,164,768]{2,1,0:T(8,128)(2,1)}), bf16[8,164,768]{2,1,0:T(8,128)(2,1)S(1)}, u32[]{:S(2)}, u32[]{:S(2)}) async-start(bf16[8,164,768]{2,1,0:T(8,128)(2,1)} %bitcast.29), calls=%async_computation | async-start | bytes 4128768 | tf_op jit(solution)/shard_map/all_to_all | solution.py:1019
  17.6 1.6 copy-start.5
  17.6 1.6 copy-start.6
  17.6 1.6 copy-start.8
  17.6 2.2 copy-start.10
  19.9 27.2 %copy-start.9 = (bf16[2,768]{1,0:T(2,128)(2,1)S(1)}, bf16[2,768]{1,0:T(2,128)(2,1)}, u32[]{:S(2)}) copy-start(bf16[2,768]{1,0:T(2,128)(2,1)} %param.22) | copy-start | bytes 9220
  41.4 1.3 copy-start
  42.7 52.3 %all-to-all-start.1 = ((bf16[8,176,768]{2,1,0:T(8,128)(2,1)}), bf16[8,176,768]{2,1,0:T(8,128)(2,1)}, u32[]{:S(2)}, u32[]{:S(2)}) async-start(bf16[8,176,768]{2,1,0:T(8,128)(2,1)} %pad.17), calls=%async_computation.1 | async-start | bytes 4325376 | tf_op jit(solution)/shard_map/all_to_all | solution.py:1019
  47.1 194.2 %reduce-scatter.2.cloned.1.call-start = ((), (), s32[]{:S(2)}) async-start(), calls=%async_computation.6 | async-start | bytes 10616832 | tf_op jit(solution)/shard_map/reduce_scatter | solution.py:1053
  61.5 33.5 %copy-start.7 = (bf16[3072]{0:T(1024)(128)(2,1)S(1)}, bf16[3072]{0:T(1024)(128)(2,1)}, u32[]{:S(2)}) copy-start(bf16[3072]{0:T(1024)(128)(2,1)} %param.20) | copy-start | bytes 18436
  158.2 74.7 %all-to-all-start.2 = ((bf16[8,112,768]{2,1,0:T(8,128)(2,1)}), bf16[8,112,768]{2,1,0:T(8,128)(2,1)S(1)}, u32[]{:S(2)}, u32[]{:S(2)}) async-start(bf16[8,112,768]{2,1,0:T(8,128)(2,1)} %get-tuple-element.62), calls=%async_computation.2 | async-start | bytes 2752512 | tf_op jit(solution)/shard_map/all_to_all | solution.py:1054
  232.9 4.6 %collective-permute-start = (bf16[384,2432]{1,0:T(8,128)(2,1)}, bf16[384,2432]{1,0:T(8,128)(2,1)}, u32[]{:S(2)}, u32[]{:S(2)}) collective-permute-start(bf16[384,2432]{1,0:T(8,128)(2,1)} %get-tuple-element.64), channel_id=1, source_target_pairs={{0,4},{4,0},{1,5},{5,1},{2,6},{6,2},{3,7},{7,3},{8,12},{12,8},{9,1... | collective-permute-start | bytes 5603336 | tf_op jit(solution)/shard_map/ppermute | solution.py:1064
  241.3 26.8 %all-to-all-start.3 = ((bf16[4,96,2432]{2,1,0:T(8,128)(2,1)}), bf16[4,96,2432]{2,1,0:T(8,128)(2,1)S(1)}, u32[]{:S(2)}, u32[]{:S(2)}) async-start(bf16[4,96,2432]{2,1,0:T(8,128)(2,1)} %bitcast.32), calls=%async_computation.4 | async-start | bytes 3735552 | tf_op jit(solution)/shard_map/all_to_all | solution.py:1069
  245.3 82.5 %all-reduce.6.cloned.1.call-start = ((), (), s32[]{:S(2)}) async-start(), calls=%async_computation.7 | async-start | bytes 2703360 | tf_op jit(solution)/shard_map/psum | solution.py:1068
  268.4 62.3 %all-to-all-start.4 = ((bf16[8,2,176,768]{3,2,1,0:T(8,128)(2,1)}), bf16[8,2,176,768]{3,2,1,0:T(8,128)(2,1)}, u32[]{:S(2)}, u32[]{:S(2)}) async-start(bf16[8,2,176,768]{3,2,1,0:T(8,128)(2,1)} %get-tuple-element.69), calls=%async_computation.5 | async-start | bytes 8650752 | tf_op jit(solution)/shard_map/all_to_all | solution.py:1082
  273.0 12.8 %collective-permute-start.1 = (bf16[24,2432]{1,0:T(8,128)(2,1)S(1)}, bf16[24,2432]{1,0:T(8,128)(2,1)S(1)}, u32[]{:S(2)}, u32[]{:S(2)}) collective-permute-start(bf16[24,2432]{1,0:T(8,128)(2,1)S(1)} %get-tuple-element.122), channel_id=1, source_target_pairs={{0,8},{8,0},{16,24},{24,16},{1,9},{9,1},{17,25},{25,17},{2,10},{10... | collective-permute-start | bytes 350216 | tf_op jit(solution)/shard_map/ppermute | solution.py:1074
  274.7 11.1 %collective-permute-start.2 = (bf16[24,2432]{1,0:T(8,128)(2,1)S(1)}, bf16[24,2432]{1,0:T(8,128)(2,1)S(1)}, u32[]{:S(2)}, u32[]{:S(2)}) collective-permute-start(bf16[24,2432]{1,0:T(8,128)(2,1)S(1)} %get-tuple-element.124), channel_id=1, source_target_pairs={{0,16},{8,24},{16,0},{24,8},{1,17},{9,25},{17,1},{25,9},{2,18},{10... | collective-permute-start | bytes 350216 | tf_op jit(solution)/shard_map/ppermute | solution.py:1074
  277.5 12.4 %collective-permute-start.3 = (bf16[24,2432]{1,0:T(8,128)(2,1)S(1)}, bf16[24,2432]{1,0:T(8,128)(2,1)S(1)}, u32[]{:S(2)}, u32[]{:S(2)}) collective-permute-start(bf16[24,2432]{1,0:T(8,128)(2,1)S(1)} %get-tuple-element.123), channel_id=1, source_target_pairs={{0,24},{8,16},{16,8},{24,0},{1,25},{9,17},{17,9},{25,1},{2,26},{10... | collective-permute-start | bytes 350216 | tf_op jit(solution)/shard_map/ppermute | solution.py:1074
  290.0 20.5 %copy-start.1 = (bf16[24,2432]{1,0:T(8,128)(2,1)}, bf16[24,2432]{1,0:T(8,128)(2,1)S(1)}, u32[]{:S(2)}) copy-start(bf16[24,2432]{1,0:T(8,128)(2,1)S(1)} %fusion.2.refs_0_) | copy-start | bytes 350212
  290.0 10.0 %collective-permute-start.4 = (bf16[24,2432]{1,0:T(8,128)(2,1)S(1)}, bf16[24,2432]{1,0:T(8,128)(2,1)S(1)}, u32[]{:S(2)}, u32[]{:S(2)}) collective-permute-start(bf16[24,2432]{1,0:T(8,128)(2,1)S(1)} %fusion.2.refs_0_), channel_id=1, source_target_pairs={{0,8},{8,0},{16,24},{24,16},{1,9},{9,1},{17,25},{25,17},{2,10},{10... | collective-permute-start | bytes 350216 | tf_op jit(solution)/shard_map/ppermute | solution.py:1074
  292.4 18.0 %collective-permute-start.5 = (bf16[24,2432]{1,0:T(8,128)(2,1)S(1)}, bf16[24,2432]{1,0:T(8,128)(2,1)S(1)}, u32[]{:S(2)}, u32[]{:S(2)}) collective-permute-start(bf16[24,2432]{1,0:T(8,128)(2,1)S(1)} %fusion.2.refs_0_), channel_id=1, source_target_pairs={{0,16},{8,24},{16,0},{24,8},{1,17},{9,25},{17,1},{25,9},{2,18},{10... | collective-permute-start | bytes 350216 | tf_op jit(solution)/shard_map/ppermute | solution.py:1074
  292.4 18.0 %collective-permute-start.6 = (bf16[24,2432]{1,0:T(8,128)(2,1)S(1)}, bf16[24,2432]{1,0:T(8,128)(2,1)S(1)}, u32[]{:S(2)}, u32[]{:S(2)}) collective-permute-start(bf16[24,2432]{1,0:T(8,128)(2,1)S(1)} %fusion.2.refs_0_), channel_id=1, source_target_pairs={{0,24},{8,16},{16,8},{24,0},{1,25},{9,17},{17,9},{25,1},{2,26},{10... | collective-permute-start | bytes 350216 | tf_op jit(solution)/shard_map/ppermute | solution.py:1074
  300.1 10.4 %copy-start.2 = (bf16[24,2432]{1,0:T(8,128)(2,1)}, bf16[24,2432]{1,0:T(8,128)(2,1)S(1)}, u32[]{:S(2)}) copy-start(bf16[24,2432]{1,0:T(8,128)(2,1)S(1)} %collective-permute-done.4.refs_1_) | copy-start | bytes 350212
  310.5 0.7 copy-start.4
  (1 other events, 0.6 us)
Sparse Core Ops, SparseCore 0:
  158.3 78.0 reduce-scatter.1
  249.2 78.5 all-reduce.5

commit v4 on v3

--- a/solution.py
+++ b/solution.py
@@ -476,13 +476,16 @@
 
     @pl.when(jnp.logical_not(bounded))
     def _():
-        for index, span in enumerate(spans):
-            for start in range(span.start, span.stop, LANES):
-                part = slice(start, start + LANES)
-                sa[...] = matmul_nt(k_ref[...], qs[part, :])
-                score = sa[...]
-                highest = jnp.max(score, axis=0, keepdims=True)
-                finish(part, jnp.exp2(score * LOG2E - highest * LOG2E).astype(BF16))
+        def column(index, _):
+            part = pl.ds(pl.multiple_of(index * LANES, LANES), LANES)
+            sa[...] = matmul_nt(k_ref[...], qs[part, :])
+            score = sa[...]
+            highest = jnp.max(score, axis=0, keepdims=True)
+            finish(part, jnp.exp2(score * LOG2E - highest * LOG2E).astype(BF16))
+            return 0
+
+        lax.fori_loop(0, 2 * tokens // LANES, column, 0)
+        for index in range(len(spans)):
             copy_of(pair, slot, index).start()
 
     row = lax.broadcasted_iota(jnp.int32, (LANES, tokens), 0)
@@ -1040,11 +1043,13 @@
     vectors2 = rows_of(norm_gain[1], norm_shift[1], out_bias[0], out_bias[1])
     bias_rows = jnp.broadcast_to(up_bias.astype(F32)[None, :], (8, hidden_units))
 
-    turned = jnp.transpose(cotangent, (1, 0, 2))
-    cot = to_clip(jnp.pad(turned, ((0, 0), (0, padded - slots), (0, 0)))).reshape(tokens, width)
-    inputs, normed1, query, keys, memory = project(
-        to_clip(jnp.transpose(patches, (1, 0, 2))), live_lanes, joint_proj, vectors1
-    )
+    arrived = to_clip(jnp.transpose(patches, (1, 0, 2)))
+    turned = jnp.pad(jnp.transpose(cotangent, (1, 0, 2)), ((0, 0), (0, padded - slots), (0, 0)))
+    turned, live_lanes, live_row, vectors1, vectors2, bias_rows = lax.optimization_barrier(
+        (turned, live_lanes, live_row, vectors1, vectors2, bias_rows)
+    )
+    cot = to_clip(turned).reshape(tokens, width)
+    inputs, normed1, query, keys, memory = project(arrived, live_lanes, joint_proj, vectors1)
     mixed, inverse, weights = attention_forward(query, keys, memory, live_row)
     output, blocks, branch, grad_mixed, packed, vector_grads = feed_forward(
         inputs, mixed, cot, live_lanes, out_proj, vectors2, up_proj, bias_rows, down_proj, members, padded

time: 347 us -> 353 us (1.017)
  Pallas kernels: 184 us -> 196 us
    pallas_call x1, Pallas kernels: 70.6 us -> 82.8 us  [attention_backward(): pl.pallas_call(attention_backward_kernel, grid=(pairs,), in_specs=[block]...]
  transfers between devices with their start and end apart: 14 -> 14, of which waited for: 8 -> 8; matrix products, arithmetic and copies ran while one was open for 3% -> 3% of each run, Pallas kernels for 35% -> 38%
where the time goes in v4:
time: 353 us; the launch traced here: 352 us
  Pallas kernels  196 us (56%)
  waiting for transfers between devices  86.9 us (25%)
  starting transfers between devices  32 us (9%)
  local copies, waits for them, and re-layouts  17 us (5%)
  between operations  14.5 us (4%)
  other arithmetic  5.77 us (2%)
    pallas_call x1, Pallas kernels, attention_backward(): pl.pallas_call(attention_backward_kernel, grid=(pairs,), in_specs=[block]...  82.8 us
    pallas_call x1, Pallas kernels, feed_forward(): pl.pallas_call(feed_forward_kernel, grid=(steps,), in_specs=[anywhere, an...  62.8 us
    pallas_call x1, Pallas kernels, attention_forward(): pl.pallas_call(attention_forward_kernel, grid=(pairs,), in_specs=[block,...  32.9 us
    ppermute x6, waiting for transfers between devices, to_group(): return lax.ppermute(array, 'dp', [(i, i ^ distance) for i in range(groups)])  27.8 us
    all_to_all x1, waiting for transfers between devices, per_device(): arrived = lax.all_to_all(joint_half, 'tm', 0, 0, tiled=True)  22.1 us
    all_to_all x2, waiting for transfers between devices, to_clip(): return lax.all_to_all(array, group, 0, 0, tiled=True)  19 us
    psum x1, waiting for transfers between devices, per_device(): mlp_sum, outp_sum = lax.psum((mlp_rows, outp_rows), 'dp')  14.4 us
    pallas_call x1, Pallas kernels, project(): pl.pallas_call(project_kernel, grid=(steps,), in_specs=[pl.BlockSpec((mem...  12 us
  transfers between devices with their start and end apart: 14, of which 8 were waited for; matrix products, arithmetic and copies ran while one was open for 3% of the time, Pallas kernels for 38%

profile of v4, /device:TPU:0, one launch (start us, length us, event | category | flops | bytes accessed | tf_op | source)
XLA Modules:
  0.0 351.7 jit_solution(15023173424552193199)
XLA Ops:
  7.2 3.3 copy.39
  10.5 5.2 %all-to-all-start = ((bf16[8,164,768]{2,1,0:T(8,128)(2,1)}), bf16[8,164,768]{2,1,0:T(8,128)(2,1)S(1)}, u32[]{:S(2)}, u32[]{:S(2)}) async-start(bf16[8,164,768]{2,1,0:T(8,128)(2,1)} %bitcast.29), calls=%async_computation | async-start | bytes 4128768 | tf_op jit(solution)/shard_map/all_to_all | solution.py:1022
  22.4 19.0 %all-to-all-done.x_ref = bf16[8,164,768]{2,1,0:T(8,128)(2,1)S(1)} async-done(((bf16[8,164,768]{2,1,0:T(8,128)(2,1)}), bf16[8,164,768]{2,1,0:T(8,128)(2,1)S(1)}, u32[]{:S(2)}, u32[]{:S(2)}) %all-to-all-start) | async-done | bytes 2015264 | tf_op jit(solution)/shard_map/all_to_all | solution.py:1022
  42.7 4.4 %all-to-all-start.1 = ((bf16[8,176,768]{2,1,0:T(8,128)(2,1)}), bf16[8,176,768]{2,1,0:T(8,128)(2,1)}, u32[]{:S(2)}, u32[]{:S(2)}) async-start(bf16[8,176,768]{2,1,0:T(8,128)(2,1)} %pad.17), calls=%async_computation.1 | async-start | bytes 4325376 | tf_op jit(solution)/shard_map/all_to_all | solution.py:1022
  47.2 12.0 %shard_map.203 = (bf16[1408,768]{1,0:T(8,128)(2,1)}, bf16[1408,768]{1,0:T(8,128)(2,1)}, bf16[1408,768]{1,0:T(8,128)(2,1)}, bf16[1408,768]{1,0:T(8,128)(2,1)}, bf16[1408,768]{1,0:T(8,128)(2,1)}) custom-call(bf16[8,164,768]{2,1,0:T(8,128)(2,1)} %copy-done, f32[1408,128]{1,0:T(8,128)} %broadcast_in_dim.20.live_ref.keep_ref, bf16[768,2304]{1,0:T(8,128)(2,1)} %w_ref.3, ...), custom_call_target="tpu_custom_call" | custom-call | flops 4982833152 | bytes 10813440 | tf_op jit(solution)/shard_map/pallas_call | solution.py:411
  59.2 32.9 %shard_map.204 = (bf16[1408,768]{1,0:T(8,128)(2,1)}, f32[1408,768]{1,0:T(8,128)}, bf16[6,1408,2816]{2,1,0:T(8,128)(2,1)}) custom-call(bf16[1408,768]{1,0:T(8,128)(2,1)} %get-tuple-element.56.q_ref, bf16[1408,768]{1,0:T(8,128)(2,1)} %get-tuple-element.57.k_ref, bf16[1408,768]{1,0:T(8,128)(2,1)} %get-tuple-element.58.v_ref, f32[8,1408]{1,0:T(8,128)} %broadcast_in_dim.21.live_ref), custom_call_target="tpu_custom_call" | custom-call | flops 12180258816 | bytes 47579136 | tf_op jit(solution)/shard_map/pallas_call | solution.py:513
  92.1 62.8 %shard_map.205 = (bf16[8,2,176,768]{3,2,1,0:T(8,128)(2,1)}, bf16[8,112,768]{2,1,0:T(8,128)(2,1)}, bf16[1408,768]{1,0:T(8,128)(2,1)}, bf16[1408,768]{1,0:T(8,128)...) custom-call(bf16[1408,768]{1,0:T(8,128)(2,1)} %get-tuple-element.61.x_hbm.x_ref, ...), custom_call_target="tpu_custom_call" | custom-call | flops 44845498368 | bytes 31850496 | tf_op jit(solution)/shard_map/pallas_call | solution.py:870
  155.0 4.0 %all-to-all-start.2 = ((bf16[8,112,768]{2,1,0:T(8,128)(2,1)}), bf16[8,112,768]{2,1,0:T(8,128)(2,1)S(1)}, u32[]{:S(2)}, u32[]{:S(2)}) async-start(bf16[8,112,768]{2,1,0:T(8,128)(2,1)} %get-tuple-element.74), calls=%async_computation.2 | async-start | bytes 2752512 | tf_op jit(solution)/shard_map/all_to_all | solution.py:1059
  159.0 82.8 %shard_map.206 = (bf16[384,2432]{1,0:T(8,128)(2,1)}, bf16[384,2432]{1,0:T(8,128)(2,1)}, bf16[8,2,176,768]{3,2,1,0:T(8,128)(2,1)}) custom-call(bf16[1408,768]{1,0:T(8,128)(2,1)} %get-tuple-element.56.q_ref, bf16[1408,768]{1,0:T(8,128)(2,1)} %get-tuple-element.57.k_ref, bf16[1408,768]{1,0:T(8,128)(2,1)} %get-tuple-element.58.v_ref, ...), custom_call_target="tpu_custom_call", output_to_operand_aliasing={{2}: (16, {})} | custom-call | flops 24360517632 | bytes 47579136 | tf_op jit(solution)/shard_map/pallas_call | solution.py:656
  243.1 3.0 collective-permute-done
  246.1 3.7 %add_convert_fusion = bf16[384,2432]{1,0:T(8,128)(2,1)} fusion(bf16[384,2432]{1,0:T(8,128)(2,1)} %collective-permute-done, bf16[384,2432]{1,0:T(8,128)(2,1)} %get-tuple-element.75), kind=kLoop, calls=%fused_computation | loop fusion | flops 3735552 | bytes 5603328 | tf_op jit(solution)/shard_map/convert_element_type | solution.py:1071
  249.8 4.0 %all-to-all-start.3 = ((bf16[4,96,2432]{2,1,0:T(8,128)(2,1)}), bf16[4,96,2432]{2,1,0:T(8,128)(2,1)S(1)}, u32[]{:S(2)}, u32[]{:S(2)}) async-start(bf16[4,96,2432]{2,1,0:T(8,128)(2,1)} %bitcast.32), calls=%async_computation.4 | async-start | bytes 3735552 | tf_op jit(solution)/shard_map/all_to_all | solution.py:1074
  254.6 22.1 %all-to-all-done.3 = bf16[4,96,2432]{2,1,0:T(8,128)(2,1)S(1)} async-done(((bf16[4,96,2432]{2,1,0:T(8,128)(2,1)}), bf16[4,96,2432]{2,1,0:T(8,128)(2,1)S(1)}, u32[]{:S(2)}, u32[]{:S(2)}) %all-to-all-start.3) | async-done | bytes 1867808 | tf_op jit(solution)/shard_map/all_to_all | solution.py:1074
  277.0 4.6 %all-to-all-start.4 = ((bf16[8,2,176,768]{3,2,1,0:T(8,128)(2,1)}), bf16[8,2,176,768]{3,2,1,0:T(8,128)(2,1)}, u32[]{:S(2)}, u32[]{:S(2)}) async-start(bf16[8,2,176,768]{3,2,1,0:T(8,128)(2,1)} %get-tuple-element.81), calls=%async_computation.5 | async-start | bytes 8650752 | tf_op jit(solution)/shard_map/all_to_all | solution.py:1087
  283.3 2.4 collective-permute-start.2
  286.1 7.9 %collective-permute-done.1 = bf16[24,2432]{1,0:T(8,128)(2,1)S(1)} collective-permute-done((bf16[24,2432]{1,0:T(8,128)(2,1)S(1)}, bf16[24,2432]{1,0:T(8,128)(2,1)S(1)}, u32[]{:S(2)}, u32[]{:S(2)}) %collective-permute-start.1) | collective-permute-done | bytes 116768 | tf_op jit(solution)/shard_map/ppermute | solution.py:1079
  294.0 4.1 %collective-permute-done.3 = bf16[24,2432]{1,0:T(8,128)(2,1)S(1)} collective-permute-done((bf16[24,2432]{1,0:T(8,128)(2,1)S(1)}, bf16[24,2432]{1,0:T(8,128)(2,1)S(1)}, u32[]{:S(2)}, u32[]{:S(2)}) %collective-permute-start.3) | collective-permute-done | bytes 116768 | tf_op jit(solution)/shard_map/ppermute | solution.py:1079
  298.2 2.4 collective-permute-start.4
  300.6 2.4 collective-permute-start.6
  303.1 5.3 %collective-permute-done.4.refs_1_ = bf16[24,2432]{1,0:T(8,128)(2,1)S(1)} collective-permute-done((bf16[24,2432]{1,0:T(8,128)(2,1)S(1)}, bf16[24,2432]{1,0:T(8,128)(2,1)S(1)}, u32[]{:S(2)}, u32[]{:S(2)}) %collective-permute-start.4) | collective-permute-done | bytes 116768 | tf_op jit(solution)/shard_map/ppermute | solution.py:1079
  308.4 10.4 %collective-permute-done.5.refs_2_ = bf16[24,2432]{1,0:T(8,128)(2,1)S(1)} collective-permute-done((bf16[24,2432]{1,0:T(8,128)(2,1)S(1)}, bf16[24,2432]{1,0:T(8,128)(2,1)S(1)}, u32[]{:S(2)}, u32[]{:S(2)}) %collective-permute-start.5) | collective-permute-done | bytes 116768 | tf_op jit(solution)/shard_map/ppermute | solution.py:1079
  321.6 14.4 %all-reduce.6.cloned.1.call-done = (bf16[768,768]{1,0:T(8,128)(2,1)}, bf16[112,768]{1,0:T(8,128)(2,1)}) async-done(((bf16[768,768]{1,0:T(8,128)(2,1)}, bf16[112,768]{1,0:T(8,128)(2,1)}), (bf16[768,768]{1,0:T(8,128)(2,1)}, bf16[112,768]{1,0:T(8,128)(2,1)})) %all-reduce.6.cloned.1.call-update) | async-done | bytes 1351696 | tf_op jit(solution)/shard_map/psum | solution.py:1073
  336.0 2.8 shard_map.208
  338.8 2.5 slice_bitcast_fusion
  (54 shorter events, 18.7 us)
Async XLA Ops:
  10.5 30.9 %all-to-all-start = ((bf16[8,164,768]{2,1,0:T(8,128)(2,1)}), bf16[8,164,768]{2,1,0:T(8,128)(2,1)S(1)}, u32[]{:S(2)}, u32[]{:S(2)}) async-start(bf16[8,164,768]{2,1,0:T(8,128)(2,1)} %bitcast.29), calls=%async_computation | async-start | bytes 4128768 | tf_op jit(solution)/shard_map/all_to_all | solution.py:1022
  17.6 1.6 copy-start.5
  17.6 1.6 copy-start.6
  17.6 1.6 copy-start.8
  17.6 1.6 copy-start.9
  17.6 2.3 copy-start.10
  17.6 4.1 %copy-start.7 = (bf16[3072]{0:T(1024)(128)(2,1)S(1)}, bf16[3072]{0:T(1024)(128)(2,1)}, u32[]{:S(2)}) copy-start(bf16[3072]{0:T(1024)(128)(2,1)} %param.20) | copy-start | bytes 18436
  41.4 1.3 copy-start
  42.7 49.4 %all-to-all-start.1 = ((bf16[8,176,768]{2,1,0:T(8,128)(2,1)}), bf16[8,176,768]{2,1,0:T(8,128)(2,1)}, u32[]{:S(2)}, u32[]{:S(2)}) async-start(bf16[8,176,768]{2,1,0:T(8,128)(2,1)} %pad.17), calls=%async_computation.1 | async-start | bytes 4325376 | tf_op jit(solution)/shard_map/all_to_all | solution.py:1022
  47.1 202.7 %reduce-scatter.2.cloned.1.call-start = ((), (), s32[]{:S(2)}) async-start(), calls=%async_computation.6 | async-start | bytes 10616832 | tf_op jit(solution)/shard_map/reduce_scatter | solution.py:1058
  155.0 86.9 %all-to-all-start.2 = ((bf16[8,112,768]{2,1,0:T(8,128)(2,1)}), bf16[8,112,768]{2,1,0:T(8,128)(2,1)S(1)}, u32[]{:S(2)}, u32[]{:S(2)}) async-start(bf16[8,112,768]{2,1,0:T(8,128)(2,1)} %get-tuple-element.74), calls=%async_computation.2 | async-start | bytes 2752512 | tf_op jit(solution)/shard_map/all_to_all | solution.py:1059
  241.8 4.2 %collective-permute-start = (bf16[384,2432]{1,0:T(8,128)(2,1)}, bf16[384,2432]{1,0:T(8,128)(2,1)}, u32[]{:S(2)}, u32[]{:S(2)}) collective-permute-start(bf16[384,2432]{1,0:T(8,128)(2,1)} %get-tuple-element.76), channel_id=1, source_target_pairs={{0,4},{4,0},{1,5},{5,1},{2,6},{6,2},{3,7},{7,3},{8,12},{12,8},{9,1... | collective-permute-start | bytes 5603336 | tf_op jit(solution)/shard_map/ppermute | solution.py:1069
  249.8 26.9 %all-to-all-start.3 = ((bf16[4,96,2432]{2,1,0:T(8,128)(2,1)}), bf16[4,96,2432]{2,1,0:T(8,128)(2,1)S(1)}, u32[]{:S(2)}, u32[]{:S(2)}) async-start(bf16[4,96,2432]{2,1,0:T(8,128)(2,1)} %bitcast.32), calls=%async_computation.4 | async-start | bytes 3735552 | tf_op jit(solution)/shard_map/all_to_all | solution.py:1074
  253.8 82.2 %all-reduce.6.cloned.1.call-start = ((), (), s32[]{:S(2)}) async-start(), calls=%async_computation.7 | async-start | bytes 2703360 | tf_op jit(solution)/shard_map/psum | solution.py:1073
  277.0 61.9 %all-to-all-start.4 = ((bf16[8,2,176,768]{3,2,1,0:T(8,128)(2,1)}), bf16[8,2,176,768]{3,2,1,0:T(8,128)(2,1)}, u32[]{:S(2)}, u32[]{:S(2)}) async-start(bf16[8,2,176,768]{3,2,1,0:T(8,128)(2,1)} %get-tuple-element.81), calls=%async_computation.5 | async-start | bytes 8650752 | tf_op jit(solution)/shard_map/all_to_all | solution.py:1087
  281.6 12.4 %collective-permute-start.1 = (bf16[24,2432]{1,0:T(8,128)(2,1)S(1)}, bf16[24,2432]{1,0:T(8,128)(2,1)S(1)}, u32[]{:S(2)}, u32[]{:S(2)}) collective-permute-start(bf16[24,2432]{1,0:T(8,128)(2,1)S(1)} %get-tuple-element.134), channel_id=1, source_target_pairs={{0,8},{8,0},{16,24},{24,16},{1,9},{9,1},{17,25},{25,17},{2,10},{10... | collective-permute-start | bytes 350216 | tf_op jit(solution)/shard_map/ppermute | solution.py:1079
  283.3 10.6 %collective-permute-start.2 = (bf16[24,2432]{1,0:T(8,128)(2,1)S(1)}, bf16[24,2432]{1,0:T(8,128)(2,1)S(1)}, u32[]{:S(2)}, u32[]{:S(2)}) collective-permute-start(bf16[24,2432]{1,0:T(8,128)(2,1)S(1)} %get-tuple-element.136), channel_id=1, source_target_pairs={{0,16},{8,24},{16,0},{24,8},{1,17},{9,25},{17,1},{25,9},{2,18},{10... | collective-permute-start | bytes 350216 | tf_op jit(solution)/shard_map/ppermute | solution.py:1079
  285.8 12.3 %collective-permute-start.3 = (bf16[24,2432]{1,0:T(8,128)(2,1)S(1)}, bf16[24,2432]{1,0:T(8,128)(2,1)S(1)}, u32[]{:S(2)}, u32[]{:S(2)}) collective-permute-start(bf16[24,2432]{1,0:T(8,128)(2,1)S(1)} %get-tuple-element.135), channel_id=1, source_target_pairs={{0,24},{8,16},{16,8},{24,0},{1,25},{9,17},{17,9},{25,1},{2,26},{10... | collective-permute-start | bytes 350216 | tf_op jit(solution)/shard_map/ppermute | solution.py:1079
  298.2 20.6 %copy-start.1 = (bf16[24,2432]{1,0:T(8,128)(2,1)}, bf16[24,2432]{1,0:T(8,128)(2,1)S(1)}, u32[]{:S(2)}) copy-start(bf16[24,2432]{1,0:T(8,128)(2,1)S(1)} %fusion.2.refs_0_) | copy-start | bytes 350212
  298.2 10.2 %collective-permute-start.4 = (bf16[24,2432]{1,0:T(8,128)(2,1)S(1)}, bf16[24,2432]{1,0:T(8,128)(2,1)S(1)}, u32[]{:S(2)}, u32[]{:S(2)}) collective-permute-start(bf16[24,2432]{1,0:T(8,128)(2,1)S(1)} %fusion.2.refs_0_), channel_id=1, source_target_pairs={{0,8},{8,0},{16,24},{24,16},{1,9},{9,1},{17,25},{25,17},{2,10},{10... | collective-permute-start | bytes 350216 | tf_op jit(solution)/shard_map/ppermute | solution.py:1079
  300.6 18.2 %collective-permute-start.5 = (bf16[24,2432]{1,0:T(8,128)(2,1)S(1)}, bf16[24,2432]{1,0:T(8,128)(2,1)S(1)}, u32[]{:S(2)}, u32[]{:S(2)}) collective-permute-start(bf16[24,2432]{1,0:T(8,128)(2,1)S(1)} %fusion.2.refs_0_), channel_id=1, source_target_pairs={{0,16},{8,24},{16,0},{24,8},{1,17},{9,25},{17,1},{25,9},{2,18},{10... | collective-permute-start | bytes 350216 | tf_op jit(solution)/shard_map/ppermute | solution.py:1079
  300.6 18.2 %collective-permute-start.6 = (bf16[24,2432]{1,0:T(8,128)(2,1)S(1)}, bf16[24,2432]{1,0:T(8,128)(2,1)S(1)}, u32[]{:S(2)}, u32[]{:S(2)}) collective-permute-start(bf16[24,2432]{1,0:T(8,128)(2,1)S(1)} %fusion.2.refs_0_), channel_id=1, source_target_pairs={{0,24},{8,16},{16,8},{24,0},{1,25},{9,17},{17,9},{25,1},{2,26},{10... | collective-permute-start | bytes 350216 | tf_op jit(solution)/shard_map/ppermute | solution.py:1079
  308.3 10.5 %copy-start.2 = (bf16[24,2432]{1,0:T(8,128)(2,1)}, bf16[24,2432]{1,0:T(8,128)(2,1)S(1)}, u32[]{:S(2)}) copy-start(bf16[24,2432]{1,0:T(8,128)(2,1)S(1)} %collective-permute-done.4.refs_1_) | copy-start | bytes 350212
  318.8 0.7 copy-start.4
  (1 other events, 0.6 us)
Sparse Core Ops, SparseCore 0:
  155.1 78.0 reduce-scatter.1
  257.7 78.2 all-reduce.5

commit v5 on v4

--- a/solution.py
+++ b/solution.py
@@ -354,6 +354,7 @@
 CHUNKS = 4
 HALVES = 2
 SPAN = 1024
+BACK_SPAN = 512
 COLLECT_FLOPS = 30 * 10**9
 
 
@@ -370,8 +371,8 @@
     return (scaled - mean - normed * slope) * inverse
 
 
-def spans_of(tokens):
-    return [slice(at, min(at + SPAN, 2 * tokens)) for at in range(0, 2 * tokens, SPAN)]
+def spans_of(tokens, size=SPAN):
+    return [slice(at, min(at + size, 2 * tokens)) for at in range(0, 2 * tokens, size)]
 
 
 def column_sum(values):
@@ -571,7 +572,7 @@
         total = column_sum(product[head * DH : (head + 1) * DH])
         delta[:, head * tokens : (head + 1) * tokens] = jnp.broadcast_to(total, (8, tokens))
     grad_keys = grad_values = None
-    for span in spans_of(tokens):
+    for span in spans_of(tokens, BACK_SPAN):
         weight = p_ref[0, :, span]
         grad_weight = matmul_nt(v_ref[...], gs[span, :])
         grad_score = (weight.astype(F32) * (grad_weight - delta[0:1, span])).astype(BF16)

time: 353 us -> 352 us (level)
  no operation moved by 1% of the time
where the time goes in v5:
time: 352 us; the launch traced here: 351 us
  Pallas kernels  194 us (55%)
  waiting for transfers between devices  86.8 us (25%)
  starting transfers between devices  32 us (9%)
  local copies, waits for them, and re-layouts  17 us (5%)
  between operations  14.5 us (4%)
  other arithmetic  5.77 us (2%)
    pallas_call x1, Pallas kernels, attention_backward(): pl.pallas_call(attention_backward_kernel, grid=(pairs,), in_specs=[block]...  81.8 us
    pallas_call x1, Pallas kernels, feed_forward(): pl.pallas_call(feed_forward_kernel, grid=(steps,), in_specs=[anywhere, an...  62.8 us
    pallas_call x1, Pallas kernels, attention_forward(): pl.pallas_call(attention_forward_kernel, grid=(pairs,), in_specs=[block,...  32.9 us
    ppermute x6, waiting for transfers between devices, to_group(): return lax.ppermute(array, 'dp', [(i, i ^ distance) for i in range(groups)])  27.7 us
    all_to_all x1, waiting for transfers between devices, per_device(): arrived = lax.all_to_all(joint_half, 'tm', 0, 0, tiled=True)  22.1 us
    all_to_all x2, waiting for transfers between devices, to_clip(): return lax.all_to_all(array, group, 0, 0, tiled=True)  19 us
    psum x1, waiting for transfers between devices, per_device(): mlp_sum, outp_sum = lax.psum((mlp_rows, outp_rows), 'dp')  14.4 us
    pallas_call x1, Pallas kernels, project(): pl.pallas_call(project_kernel, grid=(steps,), in_specs=[pl.BlockSpec((mem...  12 us
  transfers between devices with their start and end apart: 14, of which 8 were waited for; matrix products, arithmetic and copies ran while one was open for 3% of the time, Pallas kernels for 38%

profile of v5, /device:TPU:0, one launch (start us, length us, event | category | flops | bytes accessed | tf_op | source)
XLA Modules:
  0.0 350.7 jit_solution(18313910384445175430)
XLA Ops:
  7.2 3.3 copy.39
  10.5 5.2 %all-to-all-start = ((bf16[8,164,768]{2,1,0:T(8,128)(2,1)}), bf16[8,164,768]{2,1,0:T(8,128)(2,1)S(1)}, u32[]{:S(2)}, u32[]{:S(2)}) async-start(bf16[8,164,768]{2,1,0:T(8,128)(2,1)} %bitcast.29), calls=%async_computation | async-start | bytes 4128768 | tf_op jit(solution)/shard_map/all_to_all | solution.py:1023
  22.4 19.0 %all-to-all-done.x_ref = bf16[8,164,768]{2,1,0:T(8,128)(2,1)S(1)} async-done(((bf16[8,164,768]{2,1,0:T(8,128)(2,1)}), bf16[8,164,768]{2,1,0:T(8,128)(2,1)S(1)}, u32[]{:S(2)}, u32[]{:S(2)}) %all-to-all-start) | async-done | bytes 2015264 | tf_op jit(solution)/shard_map/all_to_all | solution.py:1023
  42.7 4.4 %all-to-all-start.1 = ((bf16[8,176,768]{2,1,0:T(8,128)(2,1)}), bf16[8,176,768]{2,1,0:T(8,128)(2,1)}, u32[]{:S(2)}, u32[]{:S(2)}) async-start(bf16[8,176,768]{2,1,0:T(8,128)(2,1)} %pad.17), calls=%async_computation.1 | async-start | bytes 4325376 | tf_op jit(solution)/shard_map/all_to_all | solution.py:1023
  47.2 12.0 %shard_map.203 = (bf16[1408,768]{1,0:T(8,128)(2,1)}, bf16[1408,768]{1,0:T(8,128)(2,1)}, bf16[1408,768]{1,0:T(8,128)(2,1)}, bf16[1408,768]{1,0:T(8,128)(2,1)}, bf16[1408,768]{1,0:T(8,128)(2,1)}) custom-call(bf16[8,164,768]{2,1,0:T(8,128)(2,1)} %copy-done, f32[1408,128]{1,0:T(8,128)} %broadcast_in_dim.20.live_ref.keep_ref, bf16[768,2304]{1,0:T(8,128)(2,1)} %w_ref.3, ...), custom_call_target="tpu_custom_call" | custom-call | flops 4982833152 | bytes 10813440 | tf_op jit(solution)/shard_map/pallas_call | solution.py:412
  59.2 32.9 %shard_map.204 = (bf16[1408,768]{1,0:T(8,128)(2,1)}, f32[1408,768]{1,0:T(8,128)}, bf16[6,1408,2816]{2,1,0:T(8,128)(2,1)}) custom-call(bf16[1408,768]{1,0:T(8,128)(2,1)} %get-tuple-element.56.q_ref, bf16[1408,768]{1,0:T(8,128)(2,1)} %get-tuple-element.57.k_ref, bf16[1408,768]{1,0:T(8,128)(2,1)} %get-tuple-element.58.v_ref, f32[8,1408]{1,0:T(8,128)} %broadcast_in_dim.21.live_ref), custom_call_target="tpu_custom_call" | custom-call | flops 12180258816 | bytes 47579136 | tf_op jit(solution)/shard_map/pallas_call | solution.py:514
  92.1 62.8 %shard_map.205 = (bf16[8,2,176,768]{3,2,1,0:T(8,128)(2,1)}, bf16[8,112,768]{2,1,0:T(8,128)(2,1)}, bf16[1408,768]{1,0:T(8,128)(2,1)}, bf16[1408,768]{1,0:T(8,128)...) custom-call(bf16[1408,768]{1,0:T(8,128)(2,1)} %get-tuple-element.61.x_hbm.x_ref, ...), custom_call_target="tpu_custom_call" | custom-call | flops 44845498368 | bytes 31850496 | tf_op jit(solution)/shard_map/pallas_call | solution.py:871
  155.0 4.0 %all-to-all-start.2 = ((bf16[8,112,768]{2,1,0:T(8,128)(2,1)}), bf16[8,112,768]{2,1,0:T(8,128)(2,1)S(1)}, u32[]{:S(2)}, u32[]{:S(2)}) async-start(bf16[8,112,768]{2,1,0:T(8,128)(2,1)} %get-tuple-element.74), calls=%async_computation.2 | async-start | bytes 2752512 | tf_op jit(solution)/shard_map/all_to_all | solution.py:1060
  159.0 81.8 %shard_map.206 = (bf16[384,2432]{1,0:T(8,128)(2,1)}, bf16[384,2432]{1,0:T(8,128)(2,1)}, bf16[8,2,176,768]{3,2,1,0:T(8,128)(2,1)}) custom-call(bf16[1408,768]{1,0:T(8,128)(2,1)} %get-tuple-element.56.q_ref, bf16[1408,768]{1,0:T(8,128)(2,1)} %get-tuple-element.57.k_ref, bf16[1408,768]{1,0:T(8,128)(2,1)} %get-tuple-element.58.v_ref, ...), custom_call_target="tpu_custom_call", output_to_operand_aliasing={{2}: (16, {})} | custom-call | flops 24360517632 | bytes 47579136 | tf_op jit(solution)/shard_map/pallas_call | solution.py:657
  242.1 2.9 collective-permute-done
  245.0 3.7 %add_convert_fusion = bf16[384,2432]{1,0:T(8,128)(2,1)} fusion(bf16[384,2432]{1,0:T(8,128)(2,1)} %collective-permute-done, bf16[384,2432]{1,0:T(8,128)(2,1)} %get-tuple-element.75), kind=kLoop, calls=%fused_computation | loop fusion | flops 3735552 | bytes 5603328 | tf_op jit(solution)/shard_map/convert_element_type | solution.py:1072
  248.8 4.0 %all-to-all-start.3 = ((bf16[4,96,2432]{2,1,0:T(8,128)(2,1)}), bf16[4,96,2432]{2,1,0:T(8,128)(2,1)S(1)}, u32[]{:S(2)}, u32[]{:S(2)}) async-start(bf16[4,96,2432]{2,1,0:T(8,128)(2,1)} %bitcast.32), calls=%async_computation.4 | async-start | bytes 3735552 | tf_op jit(solution)/shard_map/all_to_all | solution.py:1075
  253.6 22.1 %all-to-all-done.3 = bf16[4,96,2432]{2,1,0:T(8,128)(2,1)S(1)} async-done(((bf16[4,96,2432]{2,1,0:T(8,128)(2,1)}), bf16[4,96,2432]{2,1,0:T(8,128)(2,1)S(1)}, u32[]{:S(2)}, u32[]{:S(2)}) %all-to-all-start.3) | async-done | bytes 1867808 | tf_op jit(solution)/shard_map/all_to_all | solution.py:1075
  276.0 4.6 %all-to-all-start.4 = ((bf16[8,2,176,768]{3,2,1,0:T(8,128)(2,1)}), bf16[8,2,176,768]{3,2,1,0:T(8,128)(2,1)}, u32[]{:S(2)}, u32[]{:S(2)}) async-start(bf16[8,2,176,768]{3,2,1,0:T(8,128)(2,1)} %get-tuple-element.81), calls=%async_computation.5 | async-start | bytes 8650752 | tf_op jit(solution)/shard_map/all_to_all | solution.py:1088
  282.3 2.5 collective-permute-start.2
  285.1 7.9 %collective-permute-done.1 = bf16[24,2432]{1,0:T(8,128)(2,1)S(1)} collective-permute-done((bf16[24,2432]{1,0:T(8,128)(2,1)S(1)}, bf16[24,2432]{1,0:T(8,128)(2,1)S(1)}, u32[]{:S(2)}, u32[]{:S(2)}) %collective-permute-start.1) | collective-permute-done | bytes 116768 | tf_op jit(solution)/shard_map/ppermute | solution.py:1080
  292.9 4.1 %collective-permute-done.3 = bf16[24,2432]{1,0:T(8,128)(2,1)S(1)} collective-permute-done((bf16[24,2432]{1,0:T(8,128)(2,1)S(1)}, bf16[24,2432]{1,0:T(8,128)(2,1)S(1)}, u32[]{:S(2)}, u32[]{:S(2)}) %collective-permute-start.3) | collective-permute-done | bytes 116768 | tf_op jit(solution)/shard_map/ppermute | solution.py:1080
  297.2 2.4 collective-permute-start.4
  299.6 2.4 collective-permute-start.6
  302.0 5.4 %collective-permute-done.4.refs_1_ = bf16[24,2432]{1,0:T(8,128)(2,1)S(1)} collective-permute-done((bf16[24,2432]{1,0:T(8,128)(2,1)S(1)}, bf16[24,2432]{1,0:T(8,128)(2,1)S(1)}, u32[]{:S(2)}, u32[]{:S(2)}) %collective-permute-start.4) | collective-permute-done | bytes 116768 | tf_op jit(solution)/shard_map/ppermute | solution.py:1080
  307.4 10.4 %collective-permute-done.5.refs_2_ = bf16[24,2432]{1,0:T(8,128)(2,1)S(1)} collective-permute-done((bf16[24,2432]{1,0:T(8,128)(2,1)S(1)}, bf16[24,2432]{1,0:T(8,128)(2,1)S(1)}, u32[]{:S(2)}, u32[]{:S(2)}) %collective-permute-start.5) | collective-permute-done | bytes 116768 | tf_op jit(solution)/shard_map/ppermute | solution.py:1080
  320.6 14.4 %all-reduce.6.cloned.1.call-done = (bf16[768,768]{1,0:T(8,128)(2,1)}, bf16[112,768]{1,0:T(8,128)(2,1)}) async-done(((bf16[768,768]{1,0:T(8,128)(2,1)}, bf16[112,768]{1,0:T(8,128)(2,1)}), (bf16[768,768]{1,0:T(8,128)(2,1)}, bf16[112,768]{1,0:T(8,128)(2,1)})) %all-reduce.6.cloned.1.call-update) | async-done | bytes 1351696 | tf_op jit(solution)/shard_map/psum | solution.py:1074
  334.9 2.8 shard_map.208
  337.8 2.5 slice_bitcast_fusion
  (54 shorter events, 18.6 us)
Async XLA Ops:
  10.5 30.9 %all-to-all-start = ((bf16[8,164,768]{2,1,0:T(8,128)(2,1)}), bf16[8,164,768]{2,1,0:T(8,128)(2,1)S(1)}, u32[]{:S(2)}, u32[]{:S(2)}) async-start(bf16[8,164,768]{2,1,0:T(8,128)(2,1)} %bitcast.29), calls=%async_computation | async-start | bytes 4128768 | tf_op jit(solution)/shard_map/all_to_all | solution.py:1023
  17.6 1.6 copy-start.5
  17.6 1.6 copy-start.6
  17.6 1.6 copy-start.8
  17.6 1.6 copy-start.9
  17.6 2.3 copy-start.10
  17.6 4.1 %copy-start.7 = (bf16[3072]{0:T(1024)(128)(2,1)S(1)}, bf16[3072]{0:T(1024)(128)(2,1)}, u32[]{:S(2)}) copy-start(bf16[3072]{0:T(1024)(128)(2,1)} %param.20) | copy-start | bytes 18436
  41.4 1.3 copy-start
  42.7 49.4 %all-to-all-start.1 = ((bf16[8,176,768]{2,1,0:T(8,128)(2,1)}), bf16[8,176,768]{2,1,0:T(8,128)(2,1)}, u32[]{:S(2)}, u32[]{:S(2)}) async-start(bf16[8,176,768]{2,1,0:T(8,128)(2,1)} %pad.17), calls=%async_computation.1 | async-start | bytes 4325376 | tf_op jit(solution)/shard_map/all_to_all | solution.py:1023
  47.1 201.7 %reduce-scatter.2.cloned.1.call-start = ((), (), s32[]{:S(2)}) async-start(), calls=%async_computation.6 | async-start | bytes 10616832 | tf_op jit(solution)/shard_map/reduce_scatter | solution.py:1059
  155.0 85.8 %all-to-all-start.2 = ((bf16[8,112,768]{2,1,0:T(8,128)(2,1)}), bf16[8,112,768]{2,1,0:T(8,128)(2,1)S(1)}, u32[]{:S(2)}, u32[]{:S(2)}) async-start(bf16[8,112,768]{2,1,0:T(8,128)(2,1)} %get-tuple-element.74), calls=%async_computation.2 | async-start | bytes 2752512 | tf_op jit(solution)/shard_map/all_to_all | solution.py:1060
  240.8 4.3 %collective-permute-start = (bf16[384,2432]{1,0:T(8,128)(2,1)}, bf16[384,2432]{1,0:T(8,128)(2,1)}, u32[]{:S(2)}, u32[]{:S(2)}) collective-permute-start(bf16[384,2432]{1,0:T(8,128)(2,1)} %get-tuple-element.76), channel_id=1, source_target_pairs={{0,4},{4,0},{1,5},{5,1},{2,6},{6,2},{3,7},{7,3},{8,12},{12,8},{9,1... | collective-permute-start | bytes 5603336 | tf_op jit(solution)/shard_map/ppermute | solution.py:1070
  248.8 26.9 %all-to-all-start.3 = ((bf16[4,96,2432]{2,1,0:T(8,128)(2,1)}), bf16[4,96,2432]{2,1,0:T(8,128)(2,1)S(1)}, u32[]{:S(2)}, u32[]{:S(2)}) async-start(bf16[4,96,2432]{2,1,0:T(8,128)(2,1)} %bitcast.32), calls=%async_computation.4 | async-start | bytes 3735552 | tf_op jit(solution)/shard_map/all_to_all | solution.py:1075
  252.8 82.1 %all-reduce.6.cloned.1.call-start = ((), (), s32[]{:S(2)}) async-start(), calls=%async_computation.7 | async-start | bytes 2703360 | tf_op jit(solution)/shard_map/psum | solution.py:1074
  276.0 61.8 %all-to-all-start.4 = ((bf16[8,2,176,768]{3,2,1,0:T(8,128)(2,1)}), bf16[8,2,176,768]{3,2,1,0:T(8,128)(2,1)}, u32[]{:S(2)}, u32[]{:S(2)}) async-start(bf16[8,2,176,768]{3,2,1,0:T(8,128)(2,1)} %get-tuple-element.81), calls=%async_computation.5 | async-start | bytes 8650752 | tf_op jit(solution)/shard_map/all_to_all | solution.py:1088
  280.6 12.3 %collective-permute-start.1 = (bf16[24,2432]{1,0:T(8,128)(2,1)S(1)}, bf16[24,2432]{1,0:T(8,128)(2,1)S(1)}, u32[]{:S(2)}, u32[]{:S(2)}) collective-permute-start(bf16[24,2432]{1,0:T(8,128)(2,1)S(1)} %get-tuple-element.134), channel_id=1, source_target_pairs={{0,8},{8,0},{16,24},{24,16},{1,9},{9,1},{17,25},{25,17},{2,10},{10... | collective-permute-start | bytes 350216 | tf_op jit(solution)/shard_map/ppermute | solution.py:1080
  282.3 10.6 %collective-permute-start.2 = (bf16[24,2432]{1,0:T(8,128)(2,1)S(1)}, bf16[24,2432]{1,0:T(8,128)(2,1)S(1)}, u32[]{:S(2)}, u32[]{:S(2)}) collective-permute-start(bf16[24,2432]{1,0:T(8,128)(2,1)S(1)} %get-tuple-element.136), channel_id=1, source_target_pairs={{0,16},{8,24},{16,0},{24,8},{1,17},{9,25},{17,1},{25,9},{2,18},{10... | collective-permute-start | bytes 350216 | tf_op jit(solution)/shard_map/ppermute | solution.py:1080
  284.8 12.2 %collective-permute-start.3 = (bf16[24,2432]{1,0:T(8,128)(2,1)S(1)}, bf16[24,2432]{1,0:T(8,128)(2,1)S(1)}, u32[]{:S(2)}, u32[]{:S(2)}) collective-permute-start(bf16[24,2432]{1,0:T(8,128)(2,1)S(1)} %get-tuple-element.135), channel_id=1, source_target_pairs={{0,24},{8,16},{16,8},{24,0},{1,25},{9,17},{17,9},{25,1},{2,26},{10... | collective-permute-start | bytes 350216 | tf_op jit(solution)/shard_map/ppermute | solution.py:1080
  297.2 20.6 %copy-start.1 = (bf16[24,2432]{1,0:T(8,128)(2,1)}, bf16[24,2432]{1,0:T(8,128)(2,1)S(1)}, u32[]{:S(2)}) copy-start(bf16[24,2432]{1,0:T(8,128)(2,1)S(1)} %fusion.2.refs_0_) | copy-start | bytes 350212
  297.2 10.2 %collective-permute-start.4 = (bf16[24,2432]{1,0:T(8,128)(2,1)S(1)}, bf16[24,2432]{1,0:T(8,128)(2,1)S(1)}, u32[]{:S(2)}, u32[]{:S(2)}) collective-permute-start(bf16[24,2432]{1,0:T(8,128)(2,1)S(1)} %fusion.2.refs_0_), channel_id=1, source_target_pairs={{0,8},{8,0},{16,24},{24,16},{1,9},{9,1},{17,25},{25,17},{2,10},{10... | collective-permute-start | bytes 350216 | tf_op jit(solution)/shard_map/ppermute | solution.py:1080
  299.6 18.2 %collective-permute-start.5 = (bf16[24,2432]{1,0:T(8,128)(2,1)S(1)}, bf16[24,2432]{1,0:T(8,128)(2,1)S(1)}, u32[]{:S(2)}, u32[]{:S(2)}) collective-permute-start(bf16[24,2432]{1,0:T(8,128)(2,1)S(1)} %fusion.2.refs_0_), channel_id=1, source_target_pairs={{0,16},{8,24},{16,0},{24,8},{1,17},{9,25},{17,1},{25,9},{2,18},{10... | collective-permute-start | bytes 350216 | tf_op jit(solution)/shard_map/ppermute | solution.py:1080
  299.6 18.2 %collective-permute-start.6 = (bf16[24,2432]{1,0:T(8,128)(2,1)S(1)}, bf16[24,2432]{1,0:T(8,128)(2,1)S(1)}, u32[]{:S(2)}, u32[]{:S(2)}) collective-permute-start(bf16[24,2432]{1,0:T(8,128)(2,1)S(1)} %fusion.2.refs_0_), channel_id=1, source_target_pairs={{0,24},{8,16},{16,8},{24,0},{1,25},{9,17},{17,9},{25,1},{2,26},{10... | collective-permute-start | bytes 350216 | tf_op jit(solution)/shard_map/ppermute | solution.py:1080
  307.4 10.4 %copy-start.2 = (bf16[24,2432]{1,0:T(8,128)(2,1)}, bf16[24,2432]{1,0:T(8,128)(2,1)S(1)}, u32[]{:S(2)}) copy-start(bf16[24,2432]{1,0:T(8,128)(2,1)S(1)} %collective-permute-done.4.refs_1_) | copy-start | bytes 350212
  317.8 0.7 copy-start.4
  (1 other events, 0.6 us)
Sparse Core Ops, SparseCore 0:
  155.1 78.0 reduce-scatter.1
  256.7 78.2 all-reduce.5

commit v6 on v5

--- a/solution.py
+++ b/solution.py
@@ -971,7 +971,7 @@
         rows = slice(own + part * share, own + (part + 1) * share)
         up_ref[:, part * width : (part + 1) * width] = rows_ref[rows, :].astype(F32)
     outp_ref[...] = sums_ref[0:share, :].astype(F32)
-    bias_ref[...] = sums_ref[share : share + 16, 0:own].astype(F32)[0]
+    bias_ref[...] = sums_ref[share : share + 8, 0:own].astype(F32)[0]
 
 
 def collect_mlp(rows, sums, share):
@@ -1068,7 +1068,7 @@
     )
     kept, sent, moved = lax.optimization_barrier((kept, sent, moved))
     got = lax.ppermute(sent, "freq", [(0, 1), (1, 0)])
-    outp_rows = jnp.sum(moved.astype(F32), axis=0).astype(BF16)
+    outp_rows = jnp.sum(moved[:, : share + 8].astype(F32), axis=0).astype(BF16)
     joint_half = (kept.astype(F32) + got.astype(F32)).astype(BF16).reshape(time_size, share, kept.shape[1])
     joint_half, mlp_rows, outp_rows = lax.optimization_barrier((joint_half, mlp_rows, outp_rows))
     mlp_sum, outp_sum = lax.psum((mlp_rows, outp_rows), "dp")

time: 352 us -> 351 us (level)
  no operation moved by 1% of the time
where the time goes in v6:
time: 351 us; the launch traced here: 349 us
  Pallas kernels  194 us (55%)
  waiting for transfers between devices  85.8 us (24%)
  starting transfers between devices  31.8 us (9%)
  local copies, waits for them, and re-layouts  17 us (5%)
  between operations  14.5 us (4%)
  other arithmetic  5.21 us (1%)
    pallas_call x1, Pallas kernels, attention_backward(): pl.pallas_call(attention_backward_kernel, grid=(pairs,), in_specs=[block]...  81.8 us
    pallas_call x1, Pallas kernels, feed_forward(): pl.pallas_call(feed_forward_kernel, grid=(steps,), in_specs=[anywhere, an...  62.8 us
    pallas_call x1, Pallas kernels, attention_forward(): pl.pallas_call(attention_forward_kernel, grid=(pairs,), in_specs=[block,...  32.9 us
    ppermute x6, waiting for transfers between devices, to_group(): return lax.ppermute(array, 'dp', [(i, i ^ distance) for i in range(groups)])  27.3 us
    all_to_all x1, waiting for transfers between devices, per_device(): arrived = lax.all_to_all(joint_half, 'tm', 0, 0, tiled=True)  22.1 us
    all_to_all x2, waiting for transfers between devices, to_clip(): return lax.all_to_all(array, group, 0, 0, tiled=True)  19 us
    psum x1, waiting for transfers between devices, per_device(): mlp_sum, outp_sum = lax.psum((mlp_rows, outp_rows), 'dp')  13.8 us
    pallas_call x1, Pallas kernels, project(): pl.pallas_call(project_kernel, grid=(steps,), in_specs=[pl.BlockSpec((mem...  12 us
  transfers between devices with their start and end apart: 14, of which 8 were waited for; matrix products, arithmetic and copies ran while one was open for 3% of the time, Pallas kernels for 38%

profile of v6, /device:TPU:0, one launch (start us, length us, event | category | flops | bytes accessed | tf_op | source)
XLA Modules:
  0.0 348.8 jit_solution(14600559752472181529)
XLA Ops:
  7.2 3.3 copy.39
  10.5 5.2 %all-to-all-start = ((bf16[8,164,768]{2,1,0:T(8,128)(2,1)}), bf16[8,164,768]{2,1,0:T(8,128)(2,1)S(1)}, u32[]{:S(2)}, u32[]{:S(2)}) async-start(bf16[8,164,768]{2,1,0:T(8,128)(2,1)} %bitcast.29), calls=%async_computation | async-start | bytes 4128768 | tf_op jit(solution)/shard_map/all_to_all | solution.py:1023
  22.4 19.0 %all-to-all-done.x_ref = bf16[8,164,768]{2,1,0:T(8,128)(2,1)S(1)} async-done(((bf16[8,164,768]{2,1,0:T(8,128)(2,1)}), bf16[8,164,768]{2,1,0:T(8,128)(2,1)S(1)}, u32[]{:S(2)}, u32[]{:S(2)}) %all-to-all-start) | async-done | bytes 2015264 | tf_op jit(solution)/shard_map/all_to_all | solution.py:1023
  42.7 4.4 %all-to-all-start.1 = ((bf16[8,176,768]{2,1,0:T(8,128)(2,1)}), bf16[8,176,768]{2,1,0:T(8,128)(2,1)}, u32[]{:S(2)}, u32[]{:S(2)}) async-start(bf16[8,176,768]{2,1,0:T(8,128)(2,1)} %pad.17), calls=%async_computation.1 | async-start | bytes 4325376 | tf_op jit(solution)/shard_map/all_to_all | solution.py:1023
  47.2 12.0 %shard_map.203 = (bf16[1408,768]{1,0:T(8,128)(2,1)}, bf16[1408,768]{1,0:T(8,128)(2,1)}, bf16[1408,768]{1,0:T(8,128)(2,1)}, bf16[1408,768]{1,0:T(8,128)(2,1)}, bf16[1408,768]{1,0:T(8,128)(2,1)}) custom-call(bf16[8,164,768]{2,1,0:T(8,128)(2,1)} %copy-done, f32[1408,128]{1,0:T(8,128)} %broadcast_in_dim.20.live_ref.keep_ref, bf16[768,2304]{1,0:T(8,128)(2,1)} %w_ref.3, ...), custom_call_target="tpu_custom_call" | custom-call | flops 4982833152 | bytes 10813440 | tf_op jit(solution)/shard_map/pallas_call | solution.py:412
  59.2 32.9 %shard_map.204 = (bf16[1408,768]{1,0:T(8,128)(2,1)}, f32[1408,768]{1,0:T(8,128)}, bf16[6,1408,2816]{2,1,0:T(8,128)(2,1)}) custom-call(bf16[1408,768]{1,0:T(8,128)(2,1)} %get-tuple-element.56.q_ref, bf16[1408,768]{1,0:T(8,128)(2,1)} %get-tuple-element.57.k_ref, bf16[1408,768]{1,0:T(8,128)(2,1)} %get-tuple-element.58.v_ref, f32[8,1408]{1,0:T(8,128)} %broadcast_in_dim.21.live_ref), custom_call_target="tpu_custom_call" | custom-call | flops 12180258816 | bytes 47579136 | tf_op jit(solution)/shard_map/pallas_call | solution.py:514
  92.1 62.8 %shard_map.205 = (bf16[8,2,176,768]{3,2,1,0:T(8,128)(2,1)}, bf16[8,112,768]{2,1,0:T(8,128)(2,1)}, bf16[1408,768]{1,0:T(8,128)(2,1)}, bf16[1408,768]{1,0:T(8,128)...) custom-call(bf16[1408,768]{1,0:T(8,128)(2,1)} %get-tuple-element.61.x_hbm.x_ref, ...), custom_call_target="tpu_custom_call" | custom-call | flops 44845498368 | bytes 31850496 | tf_op jit(solution)/shard_map/pallas_call | solution.py:871
  155.0 4.0 %all-to-all-start.2 = ((bf16[8,112,768]{2,1,0:T(8,128)(2,1)}), bf16[8,112,768]{2,1,0:T(8,128)(2,1)S(1)}, u32[]{:S(2)}, u32[]{:S(2)}) async-start(bf16[8,112,768]{2,1,0:T(8,128)(2,1)} %get-tuple-element.74), calls=%async_computation.2 | async-start | bytes 2752512 | tf_op jit(solution)/shard_map/all_to_all | solution.py:1060
  159.0 81.8 %shard_map.206 = (bf16[384,2432]{1,0:T(8,128)(2,1)}, bf16[384,2432]{1,0:T(8,128)(2,1)}, bf16[8,2,176,768]{3,2,1,0:T(8,128)(2,1)}) custom-call(bf16[1408,768]{1,0:T(8,128)(2,1)} %get-tuple-element.56.q_ref, bf16[1408,768]{1,0:T(8,128)(2,1)} %get-tuple-element.57.k_ref, bf16[1408,768]{1,0:T(8,128)(2,1)} %get-tuple-element.58.v_ref, ...), custom_call_target="tpu_custom_call", output_to_operand_aliasing={{2}: (16, {})} | custom-call | flops 24360517632 | bytes 47579136 | tf_op jit(solution)/shard_map/pallas_call | solution.py:657
  242.1 2.8 collective-permute-done
  244.9 3.2 add_convert_fusion
  248.1 4.0 %all-to-all-start.3 = ((bf16[4,96,2432]{2,1,0:T(8,128)(2,1)}), bf16[4,96,2432]{2,1,0:T(8,128)(2,1)S(1)}, u32[]{:S(2)}, u32[]{:S(2)}) async-start(bf16[4,96,2432]{2,1,0:T(8,128)(2,1)} %bitcast.32), calls=%async_computation.4 | async-start | bytes 3735552 | tf_op jit(solution)/shard_map/all_to_all | solution.py:1075
  252.9 22.1 %all-to-all-done.3 = bf16[4,96,2432]{2,1,0:T(8,128)(2,1)S(1)} async-done(((bf16[4,96,2432]{2,1,0:T(8,128)(2,1)}), bf16[4,96,2432]{2,1,0:T(8,128)(2,1)S(1)}, u32[]{:S(2)}, u32[]{:S(2)}) %all-to-all-start.3) | async-done | bytes 1867808 | tf_op jit(solution)/shard_map/all_to_all | solution.py:1075
  275.3 4.6 %all-to-all-start.4 = ((bf16[8,2,176,768]{3,2,1,0:T(8,128)(2,1)}), bf16[8,2,176,768]{3,2,1,0:T(8,128)(2,1)}, u32[]{:S(2)}, u32[]{:S(2)}) async-start(bf16[8,2,176,768]{3,2,1,0:T(8,128)(2,1)} %get-tuple-element.81), calls=%async_computation.5 | async-start | bytes 8650752 | tf_op jit(solution)/shard_map/all_to_all | solution.py:1088
  281.7 2.5 collective-permute-start.2
  284.4 7.3 %collective-permute-done.1 = bf16[24,2432]{1,0:T(8,128)(2,1)S(1)} collective-permute-done((bf16[24,2432]{1,0:T(8,128)(2,1)S(1)}, bf16[24,2432]{1,0:T(8,128)(2,1)S(1)}, u32[]{:S(2)}, u32[]{:S(2)}) %collective-permute-start.1) | collective-permute-done | bytes 116768 | tf_op jit(solution)/shard_map/ppermute | solution.py:1080
  291.8 4.3 %collective-permute-done.3 = bf16[24,2432]{1,0:T(8,128)(2,1)S(1)} collective-permute-done((bf16[24,2432]{1,0:T(8,128)(2,1)S(1)}, bf16[24,2432]{1,0:T(8,128)(2,1)S(1)}, u32[]{:S(2)}, u32[]{:S(2)}) %collective-permute-start.3) | collective-permute-done | bytes 116768 | tf_op jit(solution)/shard_map/ppermute | solution.py:1080
  296.2 2.2 collective-permute-start.4
  298.4 2.4 collective-permute-start.6
  300.9 6.4 %collective-permute-done.4.refs_1_ = bf16[24,2432]{1,0:T(8,128)(2,1)S(1)} collective-permute-done((bf16[24,2432]{1,0:T(8,128)(2,1)S(1)}, bf16[24,2432]{1,0:T(8,128)(2,1)S(1)}, u32[]{:S(2)}, u32[]{:S(2)}) %collective-permute-start.4) | collective-permute-done | bytes 116768 | tf_op jit(solution)/shard_map/ppermute | solution.py:1080
  307.3 9.2 %collective-permute-done.5.refs_2_ = bf16[24,2432]{1,0:T(8,128)(2,1)S(1)} collective-permute-done((bf16[24,2432]{1,0:T(8,128)(2,1)S(1)}, bf16[24,2432]{1,0:T(8,128)(2,1)S(1)}, u32[]{:S(2)}, u32[]{:S(2)}) %collective-permute-start.5) | collective-permute-done | bytes 116768 | tf_op jit(solution)/shard_map/ppermute | solution.py:1080
  319.3 13.8 %all-reduce.6.cloned.1.call-done = (bf16[768,768]{1,0:T(8,128)(2,1)}, bf16[104,768]{1,0:T(8,128)(2,1)}) async-done(((bf16[768,768]{1,0:T(8,128)(2,1)}, bf16[104,768]{1,0:T(8,128)(2,1)}), (bf16[768,768]{1,0:T(8,128)(2,1)}, bf16[104,768]{1,0:T(8,128)(2,1)})) %all-reduce.6.cloned.1.call-update) | async-done | bytes 1339408 | tf_op jit(solution)/shard_map/psum | solution.py:1074
  333.1 2.8 shard_map.208
  335.9 2.5 slice_bitcast_fusion
  (54 shorter events, 18.6 us)
Async XLA Ops:
  10.5 30.9 %all-to-all-start = ((bf16[8,164,768]{2,1,0:T(8,128)(2,1)}), bf16[8,164,768]{2,1,0:T(8,128)(2,1)S(1)}, u32[]{:S(2)}, u32[]{:S(2)}) async-start(bf16[8,164,768]{2,1,0:T(8,128)(2,1)} %bitcast.29), calls=%async_computation | async-start | bytes 4128768 | tf_op jit(solution)/shard_map/all_to_all | solution.py:1023
  17.6 1.6 copy-start.5
  17.6 1.6 copy-start.6
  17.6 1.6 copy-start.8
  17.6 1.6 copy-start.9
  17.6 2.3 copy-start.10
  17.6 4.1 %copy-start.7 = (bf16[3072]{0:T(1024)(128)(2,1)S(1)}, bf16[3072]{0:T(1024)(128)(2,1)}, u32[]{:S(2)}) copy-start(bf16[3072]{0:T(1024)(128)(2,1)} %param.20) | copy-start | bytes 18436
  41.4 1.3 copy-start
  42.7 49.4 %all-to-all-start.1 = ((bf16[8,176,768]{2,1,0:T(8,128)(2,1)}), bf16[8,176,768]{2,1,0:T(8,128)(2,1)}, u32[]{:S(2)}, u32[]{:S(2)}) async-start(bf16[8,176,768]{2,1,0:T(8,128)(2,1)} %pad.17), calls=%async_computation.1 | async-start | bytes 4325376 | tf_op jit(solution)/shard_map/all_to_all | solution.py:1023
  47.1 201.0 %reduce-scatter.2.cloned.1.call-start = ((), (), s32[]{:S(2)}) async-start(), calls=%async_computation.6 | async-start | bytes 10616832 | tf_op jit(solution)/shard_map/reduce_scatter | solution.py:1059
  155.0 85.8 %all-to-all-start.2 = ((bf16[8,112,768]{2,1,0:T(8,128)(2,1)}), bf16[8,112,768]{2,1,0:T(8,128)(2,1)S(1)}, u32[]{:S(2)}, u32[]{:S(2)}) async-start(bf16[8,112,768]{2,1,0:T(8,128)(2,1)} %get-tuple-element.74), calls=%async_computation.2 | async-start | bytes 2752512 | tf_op jit(solution)/shard_map/all_to_all | solution.py:1060
  240.8 4.1 %collective-permute-start = (bf16[384,2432]{1,0:T(8,128)(2,1)}, bf16[384,2432]{1,0:T(8,128)(2,1)S(1)}, u32[]{:S(2)}, u32[]{:S(2)}) collective-permute-start(bf16[384,2432]{1,0:T(8,128)(2,1)} %get-tuple-element.76), channel_id=1, source_target_pairs={{0,4},{4,0},{1,5},{5,1},{2,6},{6,2},{3,7},{7,3},{8,12},{12,8},{9,1... | collective-permute-start | bytes 5603336 | tf_op jit(solution)/shard_map/ppermute | solution.py:1070
  248.1 26.9 %all-to-all-start.3 = ((bf16[4,96,2432]{2,1,0:T(8,128)(2,1)}), bf16[4,96,2432]{2,1,0:T(8,128)(2,1)S(1)}, u32[]{:S(2)}, u32[]{:S(2)}) async-start(bf16[4,96,2432]{2,1,0:T(8,128)(2,1)} %bitcast.32), calls=%async_computation.4 | async-start | bytes 3735552 | tf_op jit(solution)/shard_map/all_to_all | solution.py:1075
  252.2 80.9 %all-reduce.6.cloned.1.call-start = ((), (), s32[]{:S(2)}) async-start(), calls=%async_computation.7 | async-start | bytes 2678784 | tf_op jit(solution)/shard_map/psum | solution.py:1074
  275.3 60.6 %all-to-all-start.4 = ((bf16[8,2,176,768]{3,2,1,0:T(8,128)(2,1)}), bf16[8,2,176,768]{3,2,1,0:T(8,128)(2,1)}, u32[]{:S(2)}, u32[]{:S(2)}) async-start(bf16[8,2,176,768]{3,2,1,0:T(8,128)(2,1)} %get-tuple-element.81), calls=%async_computation.5 | async-start | bytes 8650752 | tf_op jit(solution)/shard_map/all_to_all | solution.py:1088
  280.0 11.8 %collective-permute-start.1 = (bf16[24,2432]{1,0:T(8,128)(2,1)S(1)}, bf16[24,2432]{1,0:T(8,128)(2,1)S(1)}, u32[]{:S(2)}, u32[]{:S(2)}) collective-permute-start(bf16[24,2432]{1,0:T(8,128)(2,1)S(1)} %get-tuple-element.134), channel_id=1, source_target_pairs={{0,8},{8,0},{16,24},{24,16},{1,9},{9,1},{17,25},{25,17},{2,10},{10... | collective-permute-start | bytes 350216 | tf_op jit(solution)/shard_map/ppermute | solution.py:1080
  281.7 10.1 %collective-permute-start.2 = (bf16[24,2432]{1,0:T(8,128)(2,1)S(1)}, bf16[24,2432]{1,0:T(8,128)(2,1)S(1)}, u32[]{:S(2)}, u32[]{:S(2)}) collective-permute-start(bf16[24,2432]{1,0:T(8,128)(2,1)S(1)} %get-tuple-element.136), channel_id=1, source_target_pairs={{0,16},{8,24},{16,0},{24,8},{1,17},{9,25},{17,1},{25,9},{2,18},{10... | collective-permute-start | bytes 350216 | tf_op jit(solution)/shard_map/ppermute | solution.py:1080
  284.2 11.9 %collective-permute-start.3 = (bf16[24,2432]{1,0:T(8,128)(2,1)S(1)}, bf16[24,2432]{1,0:T(8,128)(2,1)S(1)}, u32[]{:S(2)}, u32[]{:S(2)}) collective-permute-start(bf16[24,2432]{1,0:T(8,128)(2,1)S(1)} %get-tuple-element.135), channel_id=1, source_target_pairs={{0,24},{8,16},{16,8},{24,0},{1,25},{9,17},{17,9},{25,1},{2,26},{10... | collective-permute-start | bytes 350216 | tf_op jit(solution)/shard_map/ppermute | solution.py:1080
  296.2 20.3 %copy-start.1 = (bf16[24,2432]{1,0:T(8,128)(2,1)}, bf16[24,2432]{1,0:T(8,128)(2,1)S(1)}, u32[]{:S(2)}) copy-start(bf16[24,2432]{1,0:T(8,128)(2,1)S(1)} %fusion.2.refs_0_) | copy-start | bytes 350212
  296.2 11.0 %collective-permute-start.4 = (bf16[24,2432]{1,0:T(8,128)(2,1)S(1)}, bf16[24,2432]{1,0:T(8,128)(2,1)S(1)}, u32[]{:S(2)}, u32[]{:S(2)}) collective-permute-start(bf16[24,2432]{1,0:T(8,128)(2,1)S(1)} %fusion.2.refs_0_), channel_id=1, source_target_pairs={{0,8},{8,0},{16,24},{24,16},{1,9},{9,1},{17,25},{25,17},{2,10},{10... | collective-permute-start | bytes 350216 | tf_op jit(solution)/shard_map/ppermute | solution.py:1080
  298.4 18.1 %collective-permute-start.5 = (bf16[24,2432]{1,0:T(8,128)(2,1)S(1)}, bf16[24,2432]{1,0:T(8,128)(2,1)S(1)}, u32[]{:S(2)}, u32[]{:S(2)}) collective-permute-start(bf16[24,2432]{1,0:T(8,128)(2,1)S(1)} %fusion.2.refs_0_), channel_id=1, source_target_pairs={{0,16},{8,24},{16,0},{24,8},{1,17},{9,25},{17,1},{25,9},{2,18},{10... | collective-permute-start | bytes 350216 | tf_op jit(solution)/shard_map/ppermute | solution.py:1080
  298.4 18.1 %collective-permute-start.6 = (bf16[24,2432]{1,0:T(8,128)(2,1)S(1)}, bf16[24,2432]{1,0:T(8,128)(2,1)S(1)}, u32[]{:S(2)}, u32[]{:S(2)}) collective-permute-start(bf16[24,2432]{1,0:T(8,128)(2,1)S(1)} %fusion.2.refs_0_), channel_id=1, source_target_pairs={{0,24},{8,16},{16,8},{24,0},{1,25},{9,17},{17,9},{25,1},{2,26},{10... | collective-permute-start | bytes 350216 | tf_op jit(solution)/shard_map/ppermute | solution.py:1080
  307.3 9.2 %copy-start.2 = (bf16[24,2432]{1,0:T(8,128)(2,1)}, bf16[24,2432]{1,0:T(8,128)(2,1)S(1)}, u32[]{:S(2)}) copy-start(bf16[24,2432]{1,0:T(8,128)(2,1)S(1)} %collective-permute-done.4.refs_1_) | copy-start | bytes 350212
  316.5 0.7 copy-start.4
  (1 other events, 0.6 us)
Sparse Core Ops, SparseCore 0:
  155.1 78.0 reduce-scatter.1
  256.0 77.0 all-reduce.5
